TPU v7x, 32 devices: a whole 2x2x4 slice. The times are simulated.
32 devices in a mesh: dp: 8 (over z, y), sp: 4 (over x, core).
Axes of the slice: x: 2, y: 2, z: 4, core: 2. Of those that a mesh axis runs over, the one named last changes fastest.
Arguments:
- tokens: bfloat16 [16, 1024, 512], P('dp', 'sp'), may hold values from -6 to 6
- lengths: int32 [16], P('dp'), may hold values from 64 to 1024, as said below
- post_query: bfloat16 [512, 512], replicated, may hold values from -0.25 to 0.25
- post_key: bfloat16 [512, 512], replicated, may hold values from -0.25 to 0.25
- post_value: bfloat16 [512, 512], replicated, may hold values from -0.25 to 0.25
- post_out: bfloat16 [512, 512], replicated, may hold values from -1 to 1
- post_gate: bfloat16 [512, 1376], replicated, may hold values from -0.25 to 0.25
- post_up: bfloat16 [512, 1376], replicated, may hold values from -0.25 to 0.25
- post_down: bfloat16 [1376, 512], replicated, may hold values from -0.15625 to 0.15625
- post_attn_gain: float32 [512], replicated, may hold values from 0.5 to 1.5
- post_ffn_gain: float32 [512], replicated, may hold values from 0.5 to 1.5
- pre_query: bfloat16 [512, 512], replicated, may hold values from -0.25 to 0.25
- pre_key: bfloat16 [512, 512], replicated, may hold values from -0.25 to 0.25
- pre_value: bfloat16 [512, 512], replicated, may hold values from -0.25 to 0.25
- pre_out: bfloat16 [512, 512], replicated, may hold values from -1 to 1
- pre_gate: bfloat16 [512, 1376], replicated, may hold values from -0.25 to 0.25
- pre_up: bfloat16 [512, 1376], replicated, may hold values from -0.25 to 0.25
- pre_down: bfloat16 [1376, 512], replicated, may hold values from -0.15625 to 0.15625
- pre_attn_gain: float32 [512], replicated, may hold values from 0.5 to 1.5
- pre_ffn_gain: float32 [512], replicated, may hold values from 0.5 to 1.5
- out_grad: bfloat16 [16, 1024, 512], P('dp', 'sp'), may hold values from -6 to 6
Outputs:
- output: bfloat16 [16, 1024, 512], P('dp', 'sp')
- tokens_grad: bfloat16 [16, 1024, 512], P('dp', 'sp')
- grad_post_query: float32 [512, 512], replicated
- grad_post_key: float32 [512, 512], replicated
- grad_post_value: float32 [512, 512], replicated
- grad_post_out: float32 [512, 512], replicated
- grad_post_gate: float32 [512, 1376], replicated
- grad_post_up: float32 [512, 1376], replicated
- grad_post_down: float32 [1376, 512], replicated
- grad_post_attn_gain: float32 [512], replicated
- grad_post_ffn_gain: float32 [512], replicated
- grad_pre_query: float32 [512, 512], replicated
- grad_pre_key: float32 [512, 512], replicated
- grad_pre_value: float32 [512, 512], replicated
- grad_pre_out: float32 [512, 512], replicated
- grad_pre_gate: float32 [512, 1376], replicated
- grad_pre_up: float32 [512, 1376], replicated
- grad_pre_down: float32 [1376, 512], replicated
- grad_pre_attn_gain: float32 [512], replicated
- grad_pre_ffn_gain: float32 [512], replicated
Inputs may be any that keep to these rules, and one draw needn't show every extreme that they name: `lengths`: some slot has length exactly 1024 and some exactly 64.
All inputs are finite; a program needn't handle non-finite values.
Results may differ from a plain program's by a relative error of at most 0.024.
Values may be sent and summed in bfloat16 or wider, within the bound.
No kernel may reach another device: no remote copies, remote signals or barrier semaphores. Data moves between devices by JAX's collectives and lax.ppermute only.
A program may use at most 192 MiB of HBM per device.

v0:
```python
import jax
import jax.numpy as jnp
from jax import lax
from jax.sharding import PartitionSpec as P

HEADS = 8
HD = 64
SEQ = 1024


eps = 1e-06


def norm_rows(values, gain_vec):
    return values * lax.rsqrt(jnp.mean(values * values, axis=-1, keepdims=True) + eps) * gain_vec


def rotary_tables(start, row_count):
    half_dim = HD // 2
    inverse = 10000.0 ** (-jnp.arange(half_dim, dtype=jnp.float32) * 2.0 / HD)
    positions = (start + jnp.arange(row_count, dtype=jnp.int32)).astype(jnp.float32)
    angles = positions[:, None] * inverse[None, :]
    cosine = jnp.concatenate([jnp.cos(angles), jnp.cos(angles)], axis=-1)
    sine_table = jnp.concatenate([jnp.sin(angles), jnp.sin(angles)], axis=-1)
    return (cosine, sine_table)


def rotate(values, cosine, sine_table):
    half_dim = values.shape[-1] // 2
    turned = jnp.concatenate([-values[..., half_dim:], values[..., :half_dim]], axis=-1)
    return values * cosine[:, None, :] + turned * sine_table[:, None, :]


def rotate_back(grads, cosine, sine_table):
    half_dim = grads.shape[-1] // 2
    turned = grads * sine_table[:, None, :]
    backward = jnp.concatenate([turned[..., half_dim:], -turned[..., :half_dim]], axis=-1)
    return grads * cosine[:, None, :] + backward


def gated(gate_act, up_act):
    return jax.nn.silu(gate_act) * up_act


def slot_scores(queries, key_heads, length):
    scores = jnp.einsum(
        "qhd,khd->hqk", queries, key_heads, preferred_element_type=jnp.float32
    ) * HD ** (-0.5)
    row_index = jnp.arange(SEQ, dtype=jnp.int32)[:, None]
    col_index = jnp.arange(SEQ, dtype=jnp.int32)[None, :]
    allowed = (col_index <= row_index) & (col_index < length)
    return jnp.where(allowed[None], scores, -1000000000.0)


def attend_slot(pieces):
    queries, key_heads, value_heads, length = pieces
    scores = slot_scores(queries, key_heads, length)
    maxima = jnp.max(scores, axis=-1, keepdims=True)
    log_total = maxima + jnp.log(jnp.sum(jnp.exp(scores - maxima), axis=-1, keepdims=True))
    softmax_p = jnp.exp(scores - log_total)
    mixed_heads = jnp.einsum(
        "hqk,khd->qhd",
        softmax_p.astype(jnp.bfloat16),
        value_heads,
        preferred_element_type=jnp.float32,
    )
    return (mixed_heads.astype(jnp.bfloat16), log_total)


def attend_back(pieces):
    queries, key_heads, value_heads, log_total, grad_mixed, length = pieces
    softmax_p = jnp.exp(slot_scores(queries, key_heads, length) - log_total)
    grad_values = jnp.einsum(
        "hqk,qhd->khd",
        softmax_p.astype(jnp.bfloat16),
        grad_mixed,
        preferred_element_type=jnp.float32,
    )
    grad_probs = jnp.einsum(
        "qhd,khd->hqk", grad_mixed, value_heads, preferred_element_type=jnp.float32
    )
    row_delta = jnp.sum(softmax_p * grad_probs, axis=-1, keepdims=True)
    grad_scores = (softmax_p * (grad_probs - row_delta)).astype(jnp.bfloat16)
    grad_queries = jnp.einsum(
        "hqk,khd->qhd", grad_scores, key_heads, preferred_element_type=jnp.float32
    ) * HD ** (-0.5)
    grad_keys = jnp.einsum(
        "hqk,qhd->khd", grad_scores, queries, preferred_element_type=jnp.float32
    ) * HD ** (-0.5)
    return (
        grad_queries.astype(jnp.bfloat16),
        grad_keys.astype(jnp.bfloat16),
        grad_values.astype(jnp.bfloat16),
    )


def layer_forward(inputs, weights, lengths, post_norm, cosine, sine_table):
    w_query, w_key, w_value, w_out, w_gate, w_up, w_down, gain_att, gain_ffn = weights
    group = lax.axis_size("sp")
    slot_count, row_count, width = inputs.shape
    local_heads = HEADS // group
    full_rows = row_count * group
    if post_norm:
        entry_rows = inputs.astype(jnp.bfloat16)
    else:
        entry_rows = norm_rows(inputs, gain_att).astype(jnp.bfloat16)

    def rotated(weight):
        product = jnp.einsum("nsd,de->nse", entry_rows, weight, preferred_element_type=jnp.float32)
        turned = rotate(product.reshape(slot_count, row_count, HEADS, HD), cosine, sine_table)
        return turned.astype(jnp.bfloat16).reshape(slot_count, row_count, group, local_heads * HD)

    query_rows = rotated(w_query)
    key_rows = rotated(w_key)
    value_rows = jnp.einsum("nsd,de->nse", entry_rows, w_value, preferred_element_type=jnp.float32)
    value_rows = value_rows.astype(jnp.bfloat16).reshape(
        slot_count, row_count, group, local_heads * HD
    )
    query_heads, key_heads, value_heads = (
        lax.all_to_all(query_rows, "sp", split_axis=2, concat_axis=1, tiled=True),
        lax.all_to_all(key_rows, "sp", split_axis=2, concat_axis=1, tiled=True),
        lax.all_to_all(value_rows, "sp", split_axis=2, concat_axis=1, tiled=True),
    )

    def head_view(values):
        return values.reshape(slot_count, full_rows, local_heads, HD)

    query_heads = head_view(query_heads)
    key_heads = head_view(key_heads)
    value_heads = head_view(value_heads)
    mixed_heads, log_total = lax.map(attend_slot, (query_heads, key_heads, value_heads, lengths))
    mixed_rows = lax.all_to_all(
        mixed_heads.reshape(slot_count, full_rows, 1, local_heads * HD),
        "sp",
        split_axis=1,
        concat_axis=2,
        tiled=True,
    )
    mixed_rows = mixed_rows.reshape(slot_count, row_count, width)
    middle = inputs + jnp.einsum(
        "nsd,de->nse", mixed_rows, w_out, preferred_element_type=jnp.float32
    )
    if post_norm:
        state_rows = norm_rows(middle, gain_att)
        ffn_in = state_rows.astype(jnp.bfloat16)
    else:
        state_rows = middle
        ffn_in = norm_rows(middle, gain_ffn).astype(jnp.bfloat16)
    gate_act = jnp.einsum("nsd,df->nsf", ffn_in, w_gate, preferred_element_type=jnp.float32)
    up_act = jnp.einsum("nsd,df->nsf", ffn_in, w_up, preferred_element_type=jnp.float32)
    hidden = gated(gate_act, up_act).astype(jnp.bfloat16)
    result = state_rows + jnp.einsum(
        "nsf,fd->nsd", hidden, w_down, preferred_element_type=jnp.float32
    )
    saved = (
        inputs,
        entry_rows,
        query_heads,
        key_heads,
        value_heads,
        log_total,
        mixed_rows,
        middle,
        ffn_in,
        gate_act,
        up_act,
        hidden,
        result,
    )
    if post_norm:
        return (norm_rows(result, gain_ffn), saved)
    return (result, saved)


def layer_backward(grad_output, saved, weights, lengths, post_norm, cosine, sine_table):
    w_query, w_key, w_value, w_out, w_gate, w_up, w_down, gain_att, gain_ffn = weights
    (
        inputs,
        entry_rows,
        query_heads,
        key_heads,
        value_heads,
        log_total,
        mixed_rows,
        middle,
        ffn_in,
        gate_act,
        up_act,
        hidden,
        result,
    ) = saved
    group = lax.axis_size("sp")
    slot_count, row_count, width = inputs.shape
    local_heads = HEADS // group
    full_rows = row_count * group
    if post_norm:
        discard, pull_result = jax.vjp(norm_rows, result, gain_ffn)
        grad_result, grad_gain_ffn = pull_result(grad_output)
    else:
        grad_result = grad_output
    grad_down_in = grad_result.astype(jnp.bfloat16)
    grad_w_down = jnp.einsum(
        "nsf,nsd->fd", hidden, grad_down_in, preferred_element_type=jnp.float32
    )
    grad_hidden = jnp.einsum(
        "nsd,fd->nsf", grad_down_in, w_down, preferred_element_type=jnp.float32
    )
    discard, pull_glu = jax.vjp(gated, gate_act, up_act)
    grad_gate, grad_up = pull_glu(grad_hidden)
    grad_gate = grad_gate.astype(jnp.bfloat16)
    grad_up = grad_up.astype(jnp.bfloat16)
    grad_w_gate = jnp.einsum("nsd,nsf->df", ffn_in, grad_gate, preferred_element_type=jnp.float32)
    grad_w_up = jnp.einsum("nsd,nsf->df", ffn_in, grad_up, preferred_element_type=jnp.float32)
    grad_ffn_in = jnp.einsum("nsf,df->nsd", grad_gate, w_gate, preferred_element_type=jnp.float32)
    grad_ffn_in = grad_ffn_in + jnp.einsum(
        "nsf,df->nsd", grad_up, w_up, preferred_element_type=jnp.float32
    )
    if post_norm:
        discard, pull_middle = jax.vjp(norm_rows, middle, gain_att)
        grad_middle, grad_gain_att = pull_middle(grad_result + grad_ffn_in)
    else:
        discard, pull_middle = jax.vjp(norm_rows, middle, gain_ffn)
        grad_normed, grad_gain_ffn = pull_middle(grad_ffn_in)
        grad_middle = grad_result + grad_normed
    grad_attn = grad_middle.astype(jnp.bfloat16)
    grad_w_out = jnp.einsum(
        "nsd,nse->de", mixed_rows, grad_attn, preferred_element_type=jnp.float32
    )
    grad_mixed = jnp.einsum(
        "nse,de->nsd", grad_attn, w_out, preferred_element_type=jnp.float32
    ).astype(jnp.bfloat16)
    grad_mixed = lax.all_to_all(
        grad_mixed.reshape(slot_count, row_count, group, local_heads * HD),
        "sp",
        split_axis=2,
        concat_axis=1,
        tiled=True,
    )
    grad_mixed = grad_mixed.reshape(slot_count, full_rows, local_heads, HD)
    grad_queries, grad_keys, grad_values = lax.map(
        attend_back, (query_heads, key_heads, value_heads, log_total, grad_mixed, lengths)
    )

    def head_pack(values):
        return values.reshape(slot_count, full_rows, 1, local_heads * HD)

    grad_query_rows, grad_key_rows, grad_value_rows = (
        lax.all_to_all(head_pack(grad_queries), "sp", split_axis=1, concat_axis=2, tiled=True),
        lax.all_to_all(head_pack(grad_keys), "sp", split_axis=1, concat_axis=2, tiled=True),
        lax.all_to_all(head_pack(grad_values), "sp", split_axis=1, concat_axis=2, tiled=True),
    )

    def unrotate(values):
        grads = values.astype(jnp.float32).reshape(slot_count, row_count, HEADS, HD)
        return (
            rotate_back(grads, cosine, sine_table)
            .astype(jnp.bfloat16)
            .reshape(slot_count, row_count, width)
        )

    grad_query_pre = unrotate(grad_query_rows)
    grad_key_pre = unrotate(grad_key_rows)
    grad_value_pre = grad_value_rows.reshape(slot_count, row_count, width)
    grad_w_query = jnp.einsum(
        "nsd,nse->de", entry_rows, grad_query_pre, preferred_element_type=jnp.float32
    )
    grad_w_key = jnp.einsum(
        "nsd,nse->de", entry_rows, grad_key_pre, preferred_element_type=jnp.float32
    )
    grad_w_value = jnp.einsum(
        "nsd,nse->de", entry_rows, grad_value_pre, preferred_element_type=jnp.float32
    )
    grad_entry = jnp.einsum(
        "nse,de->nsd", grad_query_pre, w_query, preferred_element_type=jnp.float32
    )
    grad_entry = grad_entry + jnp.einsum(
        "nse,de->nsd", grad_key_pre, w_key, preferred_element_type=jnp.float32
    )
    grad_entry = grad_entry + jnp.einsum(
        "nse,de->nsd", grad_value_pre, w_value, preferred_element_type=jnp.float32
    )
    if post_norm:
        grad_inputs = grad_middle + grad_entry
    else:
        discard, pull_inputs = jax.vjp(norm_rows, inputs, gain_att)
        grad_normed_in, grad_gain_att = pull_inputs(grad_entry)
        grad_inputs = grad_middle + grad_normed_in
    return (
        grad_inputs,
        (
            grad_w_query,
            grad_w_key,
            grad_w_value,
            grad_w_out,
            grad_w_gate,
            grad_w_up,
            grad_w_down,
            grad_gain_att,
            grad_gain_ffn,
        ),
    )


def body(
    tokens,
    lengths,
    post_query,
    post_key,
    post_value,
    post_out,
    post_gate,
    post_up,
    post_down,
    post_attn_gain,
    post_ffn_gain,
    pre_query,
    pre_key,
    pre_value,
    pre_out,
    pre_gate,
    pre_up,
    pre_down,
    pre_attn_gain,
    pre_ffn_gain,
    out_grad,
):
    slot_count, row_count, width = tokens.shape
    start = lax.axis_index("sp") * row_count
    cosine, sine_table = rotary_tables(start, row_count)
    layer_one = (
        post_query,
        post_key,
        post_value,
        post_out,
        post_gate,
        post_up,
        post_down,
        post_attn_gain,
        post_ffn_gain,
    )
    layer_two = (
        pre_query,
        pre_key,
        pre_value,
        pre_out,
        pre_gate,
        pre_up,
        pre_down,
        pre_attn_gain,
        pre_ffn_gain,
    )
    inputs_one = tokens.astype(jnp.float32)
    middle_state, saved_one = layer_forward(
        inputs_one, layer_one, lengths, True, cosine, sine_table
    )
    final_state, saved_two = layer_forward(
        middle_state, layer_two, lengths, False, cosine, sine_table
    )
    output = final_state.astype(jnp.bfloat16)
    positions = start + jnp.arange(row_count, dtype=jnp.int32)
    valid_rows = (positions[None, :] < lengths[:, None]).astype(jnp.float32)
    grad_final = out_grad.astype(jnp.float32) * valid_rows[:, :, None]
    grad_middle_state, grads_two = layer_backward(
        grad_final, saved_two, layer_two, lengths, False, cosine, sine_table
    )
    first_again, saved_one = layer_forward(inputs_one, layer_one, lengths, True, cosine, sine_table)
    grad_tokens, grads_one = layer_backward(
        grad_middle_state, saved_one, layer_one, lengths, True, cosine, sine_table
    )
    summed = lax.psum(
        (
            grads_one[0],
            grads_one[1],
            grads_one[2],
            grads_one[3],
            grads_one[4],
            grads_one[5],
            grads_one[6],
            grads_one[7],
            grads_one[8],
            grads_two[0],
            grads_two[1],
            grads_two[2],
            grads_two[3],
            grads_two[4],
            grads_two[5],
            grads_two[6],
            grads_two[7],
            grads_two[8],
        ),
        ("dp", "sp"),
    )
    grads_one = summed[:9]
    grads_two = summed[9:]
    tokens_grad = grad_tokens.astype(jnp.bfloat16)
    return (
        output,
        tokens_grad,
        grads_one[0],
        grads_one[1],
        grads_one[2],
        grads_one[3],
        grads_one[4],
        grads_one[5],
        grads_one[6],
        grads_one[7],
        grads_one[8],
        grads_two[0],
        grads_two[1],
        grads_two[2],
        grads_two[3],
        grads_two[4],
        grads_two[5],
        grads_two[6],
        grads_two[7],
        grads_two[8],
    )


def solution(mesh):
    in_specs = (
        P("dp", "sp", None),
        P("dp"),
        P(),
        P(),
        P(),
        P(),
        P(),
        P(),
        P(),
        P(),
        P(),
        P(),
        P(),
        P(),
        P(),
        P(),
        P(),
        P(),
        P(),
        P(),
        P("dp", "sp", None),
    )
    out_specs = (
        P("dp", "sp", None),
        P("dp", "sp", None),
        P(),
        P(),
        P(),
        P(),
        P(),
        P(),
        P(),
        P(),
        P(),
        P(),
        P(),
        P(),
        P(),
        P(),
        P(),
        P(),
        P(),
        P(),
    )
    return jax.shard_map(body, mesh=mesh, in_specs=in_specs, out_specs=out_specs, check_vma=False)
```

profile of v0, /device:TPU:0, one launch (start us, length us, event | category | flops | bytes accessed | tf_op | source)
XLA Modules:
  0.0 1287.1 jit_solution(16333060521162305157)
XLA Ops:
  9.9 4.2 all-to-all-start
  19.0 4.6 all-to-all-done
  23.6 3.5 all-to-all-start.1
  28.9 6.9 all-to-all-done.1
  35.9 3.5 all-to-all-start.2
  39.4 4.1 fusion.149
  53.9 17.7 %while.62 = (s32[]{:T(128)}, bf16[2,1024,2,64]{1,3,2,0:T(8,128)(2,1)}, bf16[2,1024,2,64]{1,3,2,0:T(8,128)(2,1)}, s32[2]{0:T(128)S(1)}, bf16[2,1024,2,64]{1,3,2,0...) while((s32[]{:T(128)}, bf16[2,1024,2,64]{1,3,2,0:T(8,128)(2,1)}, ...), condition=%wide.region_3.4_spmd, body=%wide.region_0.3_spmd.sunk | while | flops 562166784 | bytes 36761784 | solution.py:131
  59.5 2.5 fusion.372
  68.3 2.5 fusion.372
  73.6 4.6 all-to-all-start.3
  79.1 17.7 %while.65 = (s32[]{:T(128)}, bf16[2,1024,2,64]{1,3,2,0:T(8,128)(2,1)}, f32[2,2,1024,1]{2,1,3,0:T(2,128)S(1)}, bf16[2,1024,2,64]{1,3,2,0:T(8,128)(2,1)}, s32[2]{0...) while((s32[]{:T(128)}, ...), condition=%wide.region_20.21_spmd, body=%wide.region_17.20_spmd.sunk | while | flops 562166784 | bytes 36769988 | solution.py:131
  84.6 2.5 fusion.393
  93.5 2.5 fusion.393
  99.0 4.1 all-to-all-start.12
  110.4 2.6 fusion.176
  113.0 5.5 multiply_reduce_fusion.14
  125.3 4.3 all-to-all-start.4
  138.6 4.1 all-to-all-start.5
  145.2 6.4 all-to-all-done.5
  151.6 4.1 all-to-all-start.6
  157.2 4.0 fusion.174
  170.1 17.7 %while.63 = (s32[]{:T(128)}, bf16[2,1024,2,64]{1,3,2,0:T(8,128)(2,1)}, f32[2,2,1024,1]{2,1,3,0:T(2,128)S(1)}, bf16[2,1024,2,64]{1,3,2,0:T(8,128)(2,1)}, s32[2]{0...) while((s32[]{:T(128)}, ...), condition=%wide.region_10.11_spmd, body=%wide.region_7.10_spmd.sunk | while | flops 562166784 | bytes 36769988 | solution.py:131
  189.8 4.4 all-to-all-start.7
  194.2 5.3 multiply_convert_fusion.3
  211.6 3.0 fusion.143
  219.8 4.5 all-to-all-start.8
  224.4 3.9 convolution_bitcast_fusion.1
  228.3 5.0 all-to-all-done.8
  240.1 28.9 %while.64 = (s32[]{:T(128)}, bf16[2,1024,2,64]{1,3,2,0:T(8,128)(2,1)}, bf16[2,1024,2,64]{1,3,2,0:T(8,128)(2,1)}, bf16[2,1024,2,64]{1,3,2,0:T(8,128)(2,1)}, bf16[...) while((s32[]{:T(128)}, ...), condition=%wide.region_15.16_spmd, body=%wide.region_13.15_spmd.sunk | while | flops 1376386048 | bytes 86572392 | solution.py:240
  243.1 3.0 multiply_reduce_fusion.18
  246.1 2.7 multiply_convert_fusion.11
  251.3 2.5 fusion.389
  257.5 3.0 multiply_reduce_fusion.18
  260.5 2.7 multiply_convert_fusion.11
  265.7 2.5 fusion.389
  271.0 3.6 all-to-all-start.10
  274.7 4.1 convolution_bitcast_fusion
  278.8 2.5 convolution_bitcast_fusion.4
  283.5 4.1 all-to-all-start.9
  292.2 2.5 copy.361
  296.5 3.5 all-to-all-start.11
  302.2 2.5 copy.356
  333.2 4.4 all-to-all-start.13
  339.0 3.8 convolution_bitcast_fusion.2
  342.8 3.7 all-to-all-done.13
  353.3 28.9 %while.66 = (s32[]{:T(128)}, bf16[2,1024,2,64]{1,3,2,0:T(8,128)(2,1)}, bf16[2,1024,2,64]{1,3,2,0:T(8,128)(2,1)}, bf16[2,1024,2,64]{1,3,2,0:T(8,128)(2,1)}, bf16[...) while((s32[]{:T(128)}, ...), condition=%wide.region_27.28_spmd, body=%wide.region_25.27_spmd.sunk | while | flops 1376386048 | bytes 86572392 | solution.py:240
  356.3 3.0 multiply_reduce_fusion.19
  359.3 2.7 multiply_convert_fusion.12
  364.5 2.5 fusion.406
  370.7 3.0 multiply_reduce_fusion.19
  373.7 2.7 multiply_convert_fusion.12
  378.9 2.5 fusion.406
  384.2 3.7 all-to-all-start.15
  388.0 2.5 convolution_bitcast_fusion.9
  390.5 4.2 convolution_bitcast_fusion.5
  397.5 3.5 all-to-all-start.14
  410.6 3.5 all-to-all-start.16
  416.3 2.5 copy.374
  432.9 3.6 fusion.198
  436.5 43.2 %all-reduce = (f32[512]{0:T(512)}, f32[512]{0:T(512)}, f32[512]{0:T(512)}, f32[512]{0:T(512)}) all-reduce(f32[512]{0:T(512)S(1)} %get-tuple-element.373, f32[512]{0:T(512)S(1)} %get-tuple-element.371, f32[512]{0:T(512)S(1)} %get-tuple-element.367, f32[512]{0:T(512)S(1)} %copy-done.112), channel_id=1, replica_groups=mesh['dp'=8,'sp'=4] {'dp','sp'}, use_global_device_ids=true, to_apply=%region_36.37 | all-reduce | flops 2048 | bytes 16384 | tf_op jit(solution)/shard_map/psum | solution.py:370
  485.3 765.8 %all-reduce.4.cloned.1.call-done = (f32[512,512]{0,1:T(8,128)}, f32[512,512]{0,1:T(8,128)}, f32[512,512]{0,1:T(8,128)}, f32[512,512]{1,0:T(8,128)}, f32[512,1376...) async-done(((f32[512,512]{0,1:T(8,128)}, ...) | async-done | bytes 25296912 | tf_op jit(solution)/shard_map/psum | solution.py:370
  1251.1 2.5 copy.393
  1253.6 2.7 copy.394
  1256.3 2.5 copy.395
  (528 shorter events, 260.0 us)
Async XLA Ops:
  7.2 203.2 %copy-start = (bf16[512,1376]{0,1:T(8,128)(2,1)S(1)}, bf16[512,1376]{0,1:T(8,128)(2,1)}, u32[]{:S(2)}) copy-start(bf16[512,1376]{0,1:T(8,128)(2,1)} %param.46) | copy-start | bytes 4227076
  7.2 6.9 copy-start.2
  7.2 8.7 copy-start.86
  9.9 13.7 %all-to-all-start = ((bf16[2,256,4,128]{3,1,0,2:T(8,128)(2,1)}), bf16[2,256,4,128]{3,1,0,2:T(8,128)(2,1)}, u32[]{:S(2)}, u32[]{:S(2)}) async-start(bf16[2,256,4,128]{3,1,0,2:T(8,128)(2,1)} %bitcast.523), calls=%async_computation | async-start | bytes 1048576 | tf_op jit(solution)/shard_map/all_to_all | solution.py:122
  16.9 114.2 %copy-start.12 = (f32[256,8,64]{0,2,1:T(8,128)}, f32[256,8,64]{0,2,1:T(8,128)S(1)}, u32[]{:S(2)}) copy-start(f32[256,8,64]{0,2,1:T(8,128)S(1)} %mul.533) | copy-start | bytes 1572868
  18.1 21.2 %copy-start.113 = (s32[2]{0:T(128)S(1)}, s32[2]{0:T(128)}, u32[]{:S(2)}) copy-start(s32[2]{0:T(128)} %param.32) | copy-start | bytes 28
  23.6 12.3 all-to-all-start.1
  35.9 14.6 %all-to-all-start.2 = ((bf16[2,256,4,128]{1,3,0,2:T(8,128)(2,1)}), bf16[2,256,4,128]{1,3,0,2:T(8,128)(2,1)S(1)}, u32[]{:S(2)}, u32[]{:S(2)}) async-start(bf16[2,256,4,128]{1,3,0,2:T(8,128)(2,1)} %copy.334), calls=%async_computation.2 | async-start | bytes 1048576 | tf_op jit(solution)/shard_map/all_to_all | solution.py:121
  39.4 6.2 copy-start.103
  73.6 25.5 %all-to-all-start.3 = ((bf16[2,1024,1,128]{3,0,2,1:T(2,128)(2,1)}), bf16[2,1024,1,128]{3,0,2,1:T(2,128)(2,1)}, u32[]{:S(2)}, u32[]{:S(2)}) async-start(bf16[2,1024,1,128]{3,0,2,1:T(2,128)(2,1)} %copy.336), calls=%async_computation.3 | async-start | bytes 1048576 | tf_op jit(solution)/shard_map/all_to_all | solution.py:132
  96.8 12.6 copy-start.6
  96.8 12.6 copy-start.8
  96.8 12.6 copy-start.97
  99.0 26.3 %all-to-all-start.12 = ((bf16[2,1024,1,128]{3,0,2,1:T(2,128)(2,1)}), bf16[2,1024,1,128]{3,0,2,1:T(2,128)(2,1)}, u32[]{:S(2)}, u32[]{:S(2)}) async-start(bf16[2,1024,1,128]{3,0,2,1:T(2,128)(2,1)} %copy.367), calls=%async_computation.12 | async-start | bytes 1048576 | tf_op jit(solution)/shard_map/all_to_all | solution.py:132
  103.2 7.2 copy-start.100
  113.0 5.5 copy-start.99
  113.0 5.8 copy-start.105
  118.8 3.4 copy-start.107
  119.0 3.6 copy-start.4
  125.3 13.2 %all-to-all-start.4 = ((bf16[2,256,4,128]{3,1,0,2:T(8,128)(2,1)}), bf16[2,256,4,128]{3,1,0,2:T(8,128)(2,1)}, u32[]{:S(2)}, u32[]{:S(2)}) async-start(bf16[2,256,4,128]{3,1,0,2:T(8,128)(2,1)} %bitcast.646), calls=%async_computation.4 | async-start | bytes 1048576 | tf_op jit(solution)/shard_map/all_to_all | solution.py:122
  138.6 18.6 %copy-start.36 = (bf16[2,256,512]{2,1,0:T(8,128)(2,1)}, bf16[2,256,512]{2,1,0:T(8,128)(2,1)S(1)}, u32[]{:S(2)}) copy-start(bf16[2,256,512]{2,1,0:T(8,128)(2,1)S(1)} %reshape.627) | copy-start | bytes 1572868
  138.6 13.1 %all-to-all-start.5 = ((bf16[2,256,4,128]{1,3,0,2:T(8,128)(2,1)}), bf16[2,256,4,128]{1,3,0,2:T(8,128)(2,1)}, u32[]{:S(2)}, u32[]{:S(2)}) async-start(bf16[2,256,4,128]{1,3,0,2:T(8,128)(2,1)} %copy.343), calls=%async_computation.5 | async-start | bytes 1048576 | tf_op jit(solution)/shard_map/all_to_all | solution.py:120
  145.2 16.0 %copy-start.109 = (f32[2,256]{1,0:T(2,128)}, f32[2,256]{1,0:T(2,128)S(1)}, u32[]{:S(2)}) copy-start(f32[2,256]{1,0:T(2,128)S(1)} %get-tuple-element.529) | copy-start | bytes 6148
  151.6 13.9 %all-to-all-start.6 = ((bf16[2,256,4,128]{1,3,0,2:T(8,128)(2,1)}), bf16[2,256,4,128]{1,3,0,2:T(8,128)(2,1)}, u32[]{:S(2)}, u32[]{:S(2)}) async-start(bf16[2,256,4,128]{1,3,0,2:T(8,128)(2,1)} %copy.347), calls=%async_computation.6 | async-start | bytes 1048576 | tf_op jit(solution)/shard_map/all_to_all | solution.py:121
  157.2 5.4 copy-start.57
  189.8 13.3 %all-to-all-start.7 = ((bf16[2,1024,1,128]{3,0,2,1:T(2,128)(2,1)}), bf16[2,1024,1,128]{3,0,2,1:T(2,128)(2,1)}, u32[]{:S(2)}, u32[]{:S(2)}) async-start(bf16[2,1024,1,128]{3,0,2,1:T(2,128)(2,1)} %copy.349), calls=%async_computation.7 | async-start | bytes 1048576 | tf_op jit(solution)/shard_map/all_to_all | solution.py:132
  194.1 6.4 copy-start.10
  194.1 6.4 copy-start.114
  204.1 5.1 copy-start.111
  209.2 8.2 copy-start.16
  209.4 5.1 copy-start.59
  219.8 13.4 %all-to-all-start.8 = ((bf16[2,256,4,128]{3,1,0,2:T(8,128)(2,1)}), bf16[2,256,4,128]{3,1,0,2:T(8,128)(2,1)}, u32[]{:S(2)}, u32[]{:S(2)}) async-start(bf16[2,256,4,128]{3,1,0,2:T(8,128)(2,1)} %bitcast.657), calls=%async_computation.8 | async-start | bytes 1048576 | tf_op jit(solution)/shard_map/all_to_all | solution.py:232
  249.7 4.1 copy-start.69
  264.1 4.1 copy-start.69
  271.0 12.4 all-to-all-start.10
  274.7 4.1 copy-start.82
  274.7 4.1 copy-start.118
  278.8 8.9 copy-start.38
  283.5 13.1 %all-to-all-start.9 = ((bf16[2,1024,1,128]{3,0,2,1:T(2,128)(2,1)}), bf16[2,1024,1,128]{3,0,2,1:T(2,128)(2,1)}, u32[]{:S(2)}, u32[]{:S(2)}) async-start(bf16[2,1024,1,128]{3,0,2,1:T(2,128)(2,1)} %copy.354), calls=%async_computation.9 | async-start | bytes 1048576 | tf_op jit(solution)/shard_map/all_to_all | solution.py:248
  294.7 10.0 copy-start.91
  296.5 15.1 %all-to-all-start.11 = ((bf16[2,1024,1,128]{3,0,2,1:T(2,128)(2,1)}), bf16[2,1024,1,128]{3,0,2,1:T(2,128)(2,1)S(1)}, u32[]{:S(2)}, u32[]{:S(2)}) async-start(bf16[2,1024,1,128]{3,0,2,1:T(2,128)(2,1)} %copy.364), calls=%async_computation.11 | async-start | bytes 1048576 | tf_op jit(solution)/shard_map/all_to_all | solution.py:250
  311.7 4.6 copy-start.102
  311.7 4.6 copy-start.106
  318.6 5.8 copy-start.46
  323.4 3.5 copy-start.89
  329.9 7.7 copy-start.5
  333.2 13.3 %all-to-all-start.13 = ((bf16[2,256,4,128]{3,1,0,2:T(8,128)(2,1)}), bf16[2,256,4,128]{3,1,0,2:T(8,128)(2,1)}, u32[]{:S(2)}, u32[]{:S(2)}) async-start(bf16[2,256,4,128]{3,1,0,2:T(8,128)(2,1)} %bitcast.649), calls=%async_computation.13 | async-start | bytes 1048576 | tf_op jit(solution)/shard_map/all_to_all | solution.py:232
  342.8 10.5 copy-start.7
  342.8 10.5 copy-start.9
  342.8 10.5 copy-start.98
  362.9 4.1 copy-start.63
  377.3 4.1 copy-start.63
  384.2 12.5 all-to-all-start.15
  390.5 10.6 copy-start.40
  397.5 12.3 all-to-all-start.14
  408.2 10.6 copy-start.22
  408.2 10.6 copy-start.92
  410.6 12.3 all-to-all-start.16
  414.1 837.0 %all-reduce.4.cloned.1.call-start = ((), (), s32[]{:S(2)}) async-start(), calls=%async_computation.17 | async-start | bytes 50593792 | tf_op jit(solution)/shard_map/psum | solution.py:370
  426.7 3.5 copy-start.44
  432.9 3.6 copy-start.112
  432.9 48.5 %copy-start.43 = (bf16[2,256,512]{1,2,0:T(8,128)(2,1)S(1)}, bf16[2,256,512]{1,2,0:T(8,128)(2,1)}, u32[]{:S(2)}) copy-start(bf16[2,256,512]{1,2,0:T(8,128)(2,1)} %copy-done.42) | copy-start | bytes 1572868
  1253.6 7.5 copy-start.55
  1275.4 4.4 copy-start.1
  (99 other events, 190.2 us)
Sparse Core Ops, SparseCore 0:
  431.8 819.2 all-reduce.3
where the time goes:
time: 1300 us; the launch traced here: 1290 us
  waiting for transfers between devices  797 us (61%)
  matrix products  157 us (12%)
  local copies, waits for them, and re-layouts  147 us (11%)
  starting transfers between devices  67.7 us (5%)
  other arithmetic  57.9 us (4%)
  blocking collectives  43.2 us (3%)
  between operations  15.9 us (1%)
    psum x1, waiting for transfers between devices, body(): lax.psum((grads_one[0], grads_one[1], grads_one[2], grads_one[3], grads_o...  766 us
    unnamed x204, local copies, waits for them, and re-layouts  44.3 us
    psum x1, blocking collectives, body(): lax.psum((grads_one[0], grads_one[1], grads_one[2], grads_one[3], grads_o...  43.2 us
  transfers between devices with their start and end apart: 18, of which 12 were waited for; matrix products, arithmetic and copies ran while one was open for 12% of the time, Pallas kernels for 0%

commit v1 on v0

--- a/solution.py
+++ b/solution.py
@@ -299,6 +299,13 @@
             grad_gain_ffn,
         ),
     )
+
+
+def reduce_grads(grads):
+    weights = tuple(grad.astype(jnp.bfloat16) for grad in grads[:7])
+    summed = lax.psum(weights, ("dp", "sp"))
+    gains = lax.psum(grads[7:], ("dp", "sp"))
+    return tuple(grad.astype(jnp.float32) for grad in summed) + tuple(gains)
 
 
 def body(
@@ -363,35 +370,11 @@
     grad_middle_state, grads_two = layer_backward(
         grad_final, saved_two, layer_two, lengths, False, cosine, sine_table
     )
-    first_again, saved_one = layer_forward(inputs_one, layer_one, lengths, True, cosine, sine_table)
     grad_tokens, grads_one = layer_backward(
         grad_middle_state, saved_one, layer_one, lengths, True, cosine, sine_table
     )
-    summed = lax.psum(
-        (
-            grads_one[0],
-            grads_one[1],
-            grads_one[2],
-            grads_one[3],
-            grads_one[4],
-            grads_one[5],
-            grads_one[6],
-            grads_one[7],
-            grads_one[8],
-            grads_two[0],
-            grads_two[1],
-            grads_two[2],
-            grads_two[3],
-            grads_two[4],
-            grads_two[5],
-            grads_two[6],
-            grads_two[7],
-            grads_two[8],
-        ),
-        ("dp", "sp"),
-    )
-    grads_one = summed[:9]
-    grads_two = summed[9:]
+    grads_one = reduce_grads(grads_one)
+    grads_two = reduce_grads(grads_two)
     tokens_grad = grad_tokens.astype(jnp.bfloat16)
     return (
         output,

time: 1300 us -> 982 us (0.76)
  waiting for transfers between devices: 797 us -> 536 us
  local copies, waits for them, and re-layouts: 147 us -> 113 us
  matrix products: 157 us -> 129 us
    psum x1, waiting for transfers between devices: 766 us -> 487 us  [reduce_grads(): summed = lax.psum(weights, ('dp', 'sp'))]
    unnamed x204 -> x201, local copies, waits for them, and re-layouts: 44.3 us -> 20.7 us
    convert_element_type x0 -> x11, other arithmetic: none -> 17.2 us  [reduce_grads(): return tuple((grad.astype(jnp.float32) for grad in summed)) + tuple(gains)]
  transfers between devices with their start and end apart: 18 -> 16, of which waited for: 12 -> 14; matrix products, arithmetic and copies ran while one was open for 12% -> 9% of each run, Pallas kernels for 0% -> 0%
where the time goes in v1:
time: 982 us; the launch traced here: 970 us
  waiting for transfers between devices  536 us (55%)
  matrix products  129 us (13%)
  local copies, waits for them, and re-layouts  113 us (12%)
  other arithmetic  61.6 us (6%)
  starting transfers between devices  58.6 us (6%)
  blocking collectives  55.3 us (6%)
  between operations  15.6 us (2%)
    psum x1, waiting for transfers between devices, reduce_grads(): summed = lax.psum(weights, ('dp', 'sp'))  487 us
    psum x1, blocking collectives, reduce_grads(): gains = lax.psum(grads[7:], ('dp', 'sp'))  42.8 us
    unnamed x201, local copies, waits for them, and re-layouts  20.7 us
  transfers between devices with their start and end apart: 16, of which 14 were waited for; matrix products, arithmetic and copies ran while one was open for 9% of the time, Pallas kernels for 0%

profile of v1, /device:TPU:0, one launch (start us, length us, event | category | flops | bytes accessed | tf_op | source)
XLA Modules:
  0.0 970.1 jit_solution(17261309546535177547)
XLA Ops:
  9.9 4.2 all-to-all-start
  19.5 4.1 all-to-all-done
  23.6 3.5 all-to-all-start.1
  27.9 8.0 all-to-all-done.1
  35.9 3.5 all-to-all-start.2
  41.4 2.2 reshape.529
  51.6 17.7 %while.52 = (s32[]{:T(128)}, bf16[2,1024,2,64]{1,3,2,0:T(8,128)(2,1)}, f32[2,2,1024,1]{2,1,3,0:T(2,128)S(1)}, bf16[2,1024,2,64]{1,3,2,0:T(8,128)(2,1)}, s32[2]{0...) while((s32[]{:T(128)}, ...), condition=%wide.region_3.4_spmd, body=%wide.region_0.3_spmd.sunk | while | flops 562166784 | bytes 36769988 | solution.py:131
  57.2 2.5 fusion.338
  66.1 2.5 fusion.338
  69.3 2.3 copy.321
  71.6 12.5 %all_to_all.216 = bf16[2,1024,1,128]{3,0,2,1:T(2,128)(2,1)S(1)} all-to-all(bf16[2,1024,1,128]{3,0,2,1:T(2,128)(2,1)} %copy.321), channel_id=1, replica_groups=mesh['dp'=8,'sp'=4] {'sp'}, dimensions={1} | all-to-all | bytes 1048576 | tf_op jit(solution)/shard_map/all_to_all | solution.py:132
  91.4 2.8 multiply_convert_fusion.5
  97.9 4.1 all-to-all-start.4
  107.6 3.3 all-to-all-done.4
  110.9 3.5 all-to-all-start.5
  115.3 8.0 all-to-all-done.5
  123.2 3.7 all-to-all-start.6
  129.1 2.2 reshape.539
  139.2 17.7 %while.53 = (s32[]{:T(128)}, bf16[2,1024,2,64]{1,3,2,0:T(8,128)(2,1)}, f32[2,2,1024,1]{2,1,3,0:T(2,128)S(1)}, bf16[2,1024,2,64]{1,3,2,0:T(8,128)(2,1)}, s32[2]{0...) while((s32[]{:T(128)}, ...), condition=%wide.region_10.11_spmd, body=%wide.region_7.10_spmd.sunk | while | flops 562166784 | bytes 36769988 | solution.py:131
  144.8 2.5 fusion.342
  153.7 2.5 fusion.342
  158.9 4.6 all-to-all-start.7
  163.6 4.1 fusion.136
  167.7 4.7 all-to-all-done.7
  181.0 3.0 fusion.130
  189.2 4.3 all-to-all-start.8
  193.5 3.4 fusion.126
  197.0 5.4 all-to-all-done.8
  209.3 28.9 %while.54 = (s32[]{:T(128)}, bf16[2,1024,2,64]{1,3,2,0:T(8,128)(2,1)}, bf16[2,1024,2,64]{1,3,2,0:T(8,128)(2,1)}, bf16[2,1024,2,64]{1,3,2,0:T(8,128)(2,1)}, bf16[...) while((s32[]{:T(128)}, ...), condition=%wide.region_15.16_spmd, body=%wide.region_13.15_spmd.sunk | while | flops 1376386048 | bytes 86572392 | solution.py:240
  212.2 3.0 multiply_reduce_fusion.16
  215.2 2.7 multiply_convert_fusion.11
  220.4 2.5 fusion.355
  226.7 3.0 multiply_reduce_fusion.16
  229.7 2.7 multiply_convert_fusion.11
  234.9 2.5 fusion.355
  240.2 3.7 all-to-all-start.10
  243.9 3.6 fusion.127
  247.5 3.2 fusion.123
  252.7 4.1 all-to-all-start.9
  262.8 2.9 all-to-all-done.9
  265.7 4.1 all-to-all-start.11
  272.0 2.5 copy.341
  302.5 4.6 all-to-all-start.12
  308.4 3.3 fusion.125
  311.7 4.3 all-to-all-done.12
  322.8 29.0 %while.55 = (s32[]{:T(128)}, bf16[2,1024,2,64]{1,3,2,0:T(8,128)(2,1)}, bf16[2,1024,2,64]{1,3,2,0:T(8,128)(2,1)}, bf16[2,1024,2,64]{1,3,2,0:T(8,128)(2,1)}, bf16[...) while((s32[]{:T(128)}, ...), condition=%wide.region_21.22_spmd, body=%wide.region_19.21_spmd.sunk | while | flops 1376386048 | bytes 86572392 | solution.py:240
  325.8 3.0 multiply_reduce_fusion.17
  328.8 2.7 multiply_convert_fusion.12
  334.0 2.5 fusion.368
  340.3 3.0 multiply_reduce_fusion.17
  343.3 2.7 multiply_convert_fusion.12
  348.5 2.5 fusion.368
  353.8 3.6 all-to-all-start.14
  357.5 2.4 fusion.182
  359.8 3.6 fusion.122
  366.2 3.5 all-to-all-start.13
  369.7 2.3 fusion.183
  379.3 3.5 all-to-all-start.15
  385.0 2.5 copy.356
  401.9 3.6 fusion.185
  405.5 42.8 %all-reduce = (f32[512]{0:T(512)}, f32[512]{0:T(512)}, f32[512]{0:T(512)}, f32[512]{0:T(512)}) all-reduce(f32[512]{0:T(512)S(1)} %get-tuple-element.339, f32[512]{0:T(512)S(1)} %get-tuple-element.334, f32[512]{0:T(512)S(1)} %get-tuple-element.336, f32[512]{0:T(512)S(1)} %copy-done.113), channel_id=1, replica_groups=mesh['dp'=8,'sp'=4] {'dp','sp'}, use_global_device_ids=true, to_apply=%region_30.31 | all-reduce | flops 2048 | bytes 16384 | tf_op jit(solution)/shard_map/psum | solution.py:307
  452.7 487.3 %all-reduce.4.cloned.1.call-done = (bf16[512,512]{0,1:T(8,128)(2,1)}, bf16[512,512]{0,1:T(8,128)(2,1)}, bf16[512,512]{0,1:T(8,128)(2,1)}, bf16[512,512]{1,0:T(8,...) async-done(((bf16[512,512]{0,1:T(8,128)(2,1)}, ...) | async-done | bytes 12648464 | tf_op jit(solution)/shard_map/psum | solution.py:306
  940.0 2.4 copy.375
  942.4 2.2 copy.376
  (496 shorter events, 217.5 us)
Async XLA Ops:
  7.2 172.6 %copy-start = (bf16[512,1376]{0,1:T(8,128)(2,1)S(1)}, bf16[512,1376]{0,1:T(8,128)(2,1)}, u32[]{:S(2)}) copy-start(bf16[512,1376]{0,1:T(8,128)(2,1)} %param.44) | copy-start | bytes 4227076
  7.2 6.9 copy-start.6
  7.2 8.7 copy-start.74
  9.9 13.7 %all-to-all-start = ((bf16[2,256,4,128]{3,1,0,2:T(8,128)(2,1)}), bf16[2,256,4,128]{3,1,0,2:T(8,128)(2,1)}, u32[]{:S(2)}, u32[]{:S(2)}) async-start(bf16[2,256,4,128]{3,1,0,2:T(8,128)(2,1)} %bitcast.512), calls=%async_computation | async-start | bytes 1048576 | tf_op jit(solution)/shard_map/all_to_all | solution.py:122
  16.9 88.5 %copy-start.12 = (f32[256,8,64]{0,2,1:T(8,128)}, f32[256,8,64]{0,2,1:T(8,128)S(1)}, u32[]{:S(2)}) copy-start(f32[256,8,64]{0,2,1:T(8,128)S(1)} %mul.485) | copy-start | bytes 1572868
  23.6 12.3 %all-to-all-start.1 = ((bf16[2,256,4,128]{1,3,0,2:T(8,128)(2,1)}), bf16[2,256,4,128]{1,3,0,2:T(8,128)(2,1)S(1)}, u32[]{:S(2)}, u32[]{:S(2)}) async-start(bf16[2,256,4,128]{1,3,0,2:T(8,128)(2,1)} %copy.315), calls=%async_computation.1 | async-start | bytes 1048576 | tf_op jit(solution)/shard_map/all_to_all | solution.py:120
  35.9 12.3 %all-to-all-start.2 = ((bf16[2,256,4,128]{1,3,0,2:T(8,128)(2,1)}), bf16[2,256,4,128]{1,3,0,2:T(8,128)(2,1)S(1)}, u32[]{:S(2)}, u32[]{:S(2)}) async-start(bf16[2,256,4,128]{1,3,0,2:T(8,128)(2,1)} %copy.319), calls=%async_computation.2 | async-start | bytes 1048576 | tf_op jit(solution)/shard_map/all_to_all | solution.py:121
  41.4 10.2 %copy-start.114 = (s32[2]{0:T(128)S(1)}, s32[2]{0:T(128)}, u32[]{:S(2)}) copy-start(s32[2]{0:T(128)} %param.30) | copy-start | bytes 28
  69.3 19.9 %copy-start.2 = (bf16[2,1024,2,64]{1,3,2,0:T(8,128)(2,1)}, bf16[2,1024,2,64]{1,3,2,0:T(8,128)(2,1)S(1)}, u32[]{:S(2)}) copy-start(bf16[2,1024,2,64]{1,3,2,0:T(8,128)(2,1)S(1)} %get-tuple-element.864) | copy-start | bytes 1572868
  69.3 19.9 %copy-start.8 = (bf16[2,1024,2,64]{1,3,2,0:T(8,128)(2,1)}, bf16[2,1024,2,64]{1,3,2,0:T(8,128)(2,1)S(1)}, u32[]{:S(2)}) copy-start(bf16[2,1024,2,64]{1,3,2,0:T(8,128)(2,1)S(1)} %get-tuple-element.866) | copy-start | bytes 1572868
  69.3 19.9 %copy-start.95 = (f32[2,2,1024,1]{2,1,3,0:T(2,128)}, f32[2,2,1024,1]{2,1,3,0:T(2,128)S(1)}, u32[]{:S(2)}) copy-start(f32[2,2,1024,1]{2,1,3,0:T(2,128)S(1)} %get-tuple-element.810) | copy-start | bytes 49156
  84.1 5.8 copy-start.104
  89.3 4.9 copy-start.10
  89.9 4.3 copy-start.98
  90.0 4.1 copy-start.45
  96.3 7.3 copy-start.106
  96.3 7.3 copy-start.102
  96.5 7.0 copy-start.4
  97.9 13.1 %all-to-all-start.4 = ((bf16[2,256,4,128]{3,1,0,2:T(8,128)(2,1)}), bf16[2,256,4,128]{3,1,0,2:T(8,128)(2,1)}, u32[]{:S(2)}, u32[]{:S(2)}) async-start(bf16[2,256,4,128]{3,1,0,2:T(8,128)(2,1)} %bitcast.625), calls=%async_computation.4 | async-start | bytes 1048576 | tf_op jit(solution)/shard_map/all_to_all | solution.py:122
  110.9 12.3 %all-to-all-start.5 = ((bf16[2,256,4,128]{1,3,0,2:T(8,128)(2,1)}), bf16[2,256,4,128]{1,3,0,2:T(8,128)(2,1)S(1)}, u32[]{:S(2)}, u32[]{:S(2)}) async-start(bf16[2,256,4,128]{1,3,0,2:T(8,128)(2,1)} %copy.328), calls=%async_computation.5 | async-start | bytes 1048576 | tf_op jit(solution)/shard_map/all_to_all | solution.py:120
  123.2 12.5 %all-to-all-start.6 = ((bf16[2,256,4,128]{1,3,0,2:T(8,128)(2,1)}), bf16[2,256,4,128]{1,3,0,2:T(8,128)(2,1)S(1)}, u32[]{:S(2)}, u32[]{:S(2)}) async-start(bf16[2,256,4,128]{1,3,0,2:T(8,128)(2,1)} %copy.332), calls=%async_computation.6 | async-start | bytes 1048576 | tf_op jit(solution)/shard_map/all_to_all | solution.py:121
  158.9 13.5 %all-to-all-start.7 = ((bf16[2,1024,1,128]{3,0,2,1:T(2,128)(2,1)}), bf16[2,1024,1,128]{3,0,2,1:T(2,128)(2,1)}, u32[]{:S(2)}, u32[]{:S(2)}) async-start(bf16[2,1024,1,128]{3,0,2,1:T(2,128)(2,1)} %copy.334), calls=%async_computation.7 | async-start | bytes 1048576 | tf_op jit(solution)/shard_map/all_to_all | solution.py:132
  173.5 5.1 copy-start.110
  178.6 8.2 copy-start.14
  178.9 5.1 copy-start.47
  189.2 13.2 %all-to-all-start.8 = ((bf16[2,256,4,128]{3,1,0,2:T(8,128)(2,1)}), bf16[2,256,4,128]{3,1,0,2:T(8,128)(2,1)}, u32[]{:S(2)}, u32[]{:S(2)}) async-start(bf16[2,256,4,128]{3,1,0,2:T(8,128)(2,1)} %bitcast.638), calls=%async_computation.8 | async-start | bytes 1048576 | tf_op jit(solution)/shard_map/all_to_all | solution.py:232
  218.8 4.1 copy-start.59
  233.3 4.1 copy-start.59
  240.2 12.5 %all-to-all-start.10 = ((bf16[2,1024,1,128]{3,0,2,1:T(2,128)(2,1)}), bf16[2,1024,1,128]{3,0,2,1:T(2,128)(2,1)S(1)}, u32[]{:S(2)}, u32[]{:S(2)}) async-start(bf16[2,1024,1,128]{3,0,2,1:T(2,128)(2,1)} %copy.344), calls=%async_computation.10 | async-start | bytes 1048576 | tf_op jit(solution)/shard_map/all_to_all | solution.py:249
  243.9 3.6 copy-start.119
  247.5 9.4 copy-start.34
  252.7 13.1 %all-to-all-start.9 = ((bf16[2,1024,1,128]{3,0,2,1:T(2,128)(2,1)}), bf16[2,1024,1,128]{3,0,2,1:T(2,128)(2,1)}, u32[]{:S(2)}, u32[]{:S(2)}) async-start(bf16[2,1024,1,128]{3,0,2,1:T(2,128)(2,1)} %copy.339), calls=%async_computation.9 | async-start | bytes 1048576 | tf_op jit(solution)/shard_map/all_to_all | solution.py:248
  262.8 11.8 %copy-start.18 = (f32[2,256,4,1,128]{1,4,2,0,3:T(8,128)}, f32[2,256,4,1,128]{1,4,2,0,3:T(8,128)S(1)}, u32[]{:S(2)}) copy-start(f32[2,256,4,1,128]{1,4,2,0,3:T(8,128)S(1)} %copy.346) | copy-start | bytes 3145732
  262.8 11.8 %copy-start.87 = (f32[256,64]{0,1:T(8,128)S(1)}, f32[256,64]{0,1:T(8,128)}, u32[]{:S(2)}) copy-start(f32[256,64]{0,1:T(8,128)} %copy-done.86) | copy-start | bytes 196612
  265.7 14.7 %all-to-all-start.11 = ((bf16[2,1024,1,128]{3,0,2,1:T(2,128)(2,1)}), bf16[2,1024,1,128]{3,0,2,1:T(2,128)(2,1)}, u32[]{:S(2)}, u32[]{:S(2)}) async-start(bf16[2,1024,1,128]{3,0,2,1:T(2,128)(2,1)} %copy.349), calls=%async_computation.11 | async-start | bytes 1048576 | tf_op jit(solution)/shard_map/all_to_all | solution.py:250
  278.2 8.6 copy-start.35
  281.5 5.2 copy-start.101
  288.9 5.5 copy-start.40
  293.3 3.5 copy-start.85
  299.6 7.4 copy-start.5
  299.6 7.4 copy-start.37
  302.5 13.4 %all-to-all-start.12 = ((bf16[2,256,4,128]{3,1,0,2:T(8,128)(2,1)}), bf16[2,256,4,128]{3,1,0,2:T(8,128)(2,1)}, u32[]{:S(2)}, u32[]{:S(2)}) async-start(bf16[2,256,4,128]{3,1,0,2:T(8,128)(2,1)} %bitcast.630), calls=%async_computation.12 | async-start | bytes 1048576 | tf_op jit(solution)/shard_map/all_to_all | solution.py:232
  311.7 11.1 %copy-start.3 = (bf16[2,1024,2,64]{1,3,2,0:T(8,128)(2,1)S(1)}, bf16[2,1024,2,64]{1,3,2,0:T(8,128)(2,1)}, u32[]{:S(2)}) copy-start(bf16[2,1024,2,64]{1,3,2,0:T(8,128)(2,1)} %copy-done.2) | copy-start | bytes 1572868
  311.7 11.1 %copy-start.9 = (bf16[2,1024,2,64]{1,3,2,0:T(8,128)(2,1)S(1)}, bf16[2,1024,2,64]{1,3,2,0:T(8,128)(2,1)}, u32[]{:S(2)}) copy-start(bf16[2,1024,2,64]{1,3,2,0:T(8,128)(2,1)} %copy-done.8) | copy-start | bytes 1572868
  311.7 11.1 %copy-start.96 = (f32[2,2,1024,1]{2,1,3,0:T(2,128)S(1)}, f32[2,2,1024,1]{2,1,3,0:T(2,128)}, u32[]{:S(2)}) copy-start(f32[2,2,1024,1]{2,1,3,0:T(2,128)} %copy-done.95) | copy-start | bytes 49156
  332.4 4.1 copy-start.52
  346.9 4.1 copy-start.52
  353.8 12.4 %all-to-all-start.14 = ((bf16[2,1024,1,128]{3,0,2,1:T(2,128)(2,1)}), bf16[2,1024,1,128]{3,0,2,1:T(2,128)(2,1)S(1)}, u32[]{:S(2)}, u32[]{:S(2)}) async-start(bf16[2,1024,1,128]{3,0,2,1:T(2,128)(2,1)} %copy.359), calls=%async_computation.14 | async-start | bytes 1048576 | tf_op jit(solution)/shard_map/all_to_all | solution.py:249
  357.4 6.0 copy-start.53
  366.2 12.3 %all-to-all-start.13 = ((bf16[2,1024,1,128]{3,0,2,1:T(2,128)(2,1)}), bf16[2,1024,1,128]{3,0,2,1:T(2,128)(2,1)S(1)}, u32[]{:S(2)}, u32[]{:S(2)}) async-start(bf16[2,1024,1,128]{3,0,2,1:T(2,128)(2,1)} %copy.354), calls=%async_computation.13 | async-start | bytes 1048576 | tf_op jit(solution)/shard_map/all_to_all | solution.py:248
  376.7 10.8 %copy-start.88 = (f32[256,64]{0,1:T(8,128)S(1)}, f32[256,64]{0,1:T(8,128)}, u32[]{:S(2)}) copy-start(f32[256,64]{0,1:T(8,128)} %copy-done.86) | copy-start | bytes 196612
  379.3 12.3 %all-to-all-start.15 = ((bf16[2,1024,1,128]{3,0,2,1:T(2,128)(2,1)}), bf16[2,1024,1,128]{3,0,2,1:T(2,128)(2,1)S(1)}, u32[]{:S(2)}, u32[]{:S(2)}) async-start(bf16[2,1024,1,128]{3,0,2,1:T(2,128)(2,1)} %copy.364), calls=%async_computation.15 | async-start | bytes 1048576 | tf_op jit(solution)/shard_map/all_to_all | solution.py:250
  382.8 557.2 %all-reduce.4.cloned.1.call-start = ((), (), s32[]{:S(2)}) async-start(), calls=%async_computation.16 | async-start | bytes 25296896 | tf_op jit(solution)/shard_map/psum | solution.py:306
  401.9 3.6 copy-start.113
  401.9 46.4 %copy-start.39 = (bf16[2,256,512]{1,2,0:T(8,128)(2,1)S(1)}, bf16[2,256,512]{1,2,0:T(8,128)(2,1)}, u32[]{:S(2)}) copy-start(bf16[2,256,512]{1,2,0:T(8,128)(2,1)} %copy-done.38) | copy-start | bytes 1572868
  405.5 45.9 %copy-start.44 = (bf16[512,512]{1,0:T(8,128)(2,1)S(1)}, bf16[512,512]{1,0:T(8,128)(2,1)}, u32[]{:S(2)}) copy-start(bf16[512,512]{1,0:T(8,128)(2,1)} %param.33) | copy-start | bytes 1572868
  405.5 45.9 %copy-start.49 = (bf16[2,256,512]{2,1,0:T(8,128)(2,1)S(1)}, bf16[2,256,512]{2,1,0:T(8,128)(2,1)}, u32[]{:S(2)}) copy-start(bf16[2,256,512]{2,1,0:T(8,128)(2,1)} %reshape.559) | copy-start | bytes 1572868
  940.0 4.6 copy-start.94
  940.0 5.8 copy-start.93
  940.0 6.9 copy-start.81
  950.8 4.2 copy-start.90
  952.8 3.3 copy-start.89
  952.8 4.4 copy-start.78
  959.2 3.9 copy-start.1
  (95 other events, 175.4 us)
Sparse Core Ops, SparseCore 0:
  400.8 539.1 all-reduce.3

commit v2 on v1

v2 whole, which is shorter than its diff:
```python
import jax
import jax.numpy as jnp
from jax import lax
from jax.experimental import pallas as pl
from jax.experimental.pallas import tpu as pltpu
from jax.sharding import PartitionSpec as P

D = 512
HEADS = 8
HD = 64
FF = 1376
SEQ = 1024
EPS = 1e-06
NEG = -1000000000.0
AXES = ("dp", "sp")
BF = jnp.bfloat16
F32 = jnp.float32
LANES = 128
PANELS = D // LANES
BLK = SEQ // 4
ROWS = 2 * BLK
SCALE = HD ** (-0.5)
FFN_ROWS = 3 * PANELS * FF
ATTN_ROWS = 4 * PANELS * D
GAIN_ROWS = 16


def dot(left, right):
    return lax.dot_general(left, right, (((1,), (0,)), ((), ())), preferred_element_type=F32)


def dot_nt(left, right):
    return lax.dot_general(left, right, (((1,), (1,)), ((), ())), preferred_element_type=F32)


def dot_tn(left, right):
    return lax.dot_general(left, right, (((0,), (0,)), ((), ())), preferred_element_type=F32)


def inv_rms(values):
    return lax.rsqrt(jnp.mean(values * values, axis=-1, keepdims=True) + EPS)


def rms_back(values, gain, upstream):
    scale = inv_rms(values)
    weighted = upstream * gain
    grad = scale * weighted - values * (
        scale * scale * scale * jnp.mean(weighted * values, axis=-1, keepdims=True)
    )
    grad_gain = jnp.sum(upstream * (values * scale), axis=0, keepdims=True)
    return grad, grad_gain


class Refs:
    def __init__(self, inputs, outputs, vmem, sems):
        self.vmem, self.outputs, self.sems = vmem, outputs, sems
        self.waiting, self.sent = {}, []
        for k, name in enumerate(inputs):
            copy = pltpu.make_async_copy(inputs[name], vmem[name], sems.at[k])
            copy.start()
            self.waiting[name] = copy
        self.first_out = len(inputs)

    def __getattr__(self, name):
        if name in self.waiting:
            self.waiting.pop(name).wait()
        return self.vmem[name]

    def send(self, *refs):
        for ref in refs:
            for k, name in enumerate(self.outputs):
                if name in self.vmem and self.vmem[name] is ref:
                    sem = self.sems.at[self.first_out + k]
                    copy = pltpu.make_async_copy(ref, self.outputs[name], sem)
                    copy.start()
                    self.sent.append(copy)

    def finish(self):
        for name in list(self.waiting):
            self.waiting.pop(name).wait()
        for copy in self.sent:
            copy.wait()


def run_kernel(body, scalars, ins, outs, scratch, pieces=None, flops=0):
    outs, scratch = dict(outs), dict(scratch)
    twins = list(ins) + list(outs) + list(scratch)
    shapes = [pltpu.VMEM(ins[n].shape, ins[n].dtype) for n in ins]
    shapes += [pltpu.VMEM(*outs[n]) for n in outs] + [pltpu.VMEM(*scratch[n]) for n in scratch]
    n_in, n_out, n_copies = len(ins), len(outs), 1
    out_shapes = [jax.ShapeDtypeStruct(*outs[n]) for n in outs]
    if pieces is not None:
        orders, n_copies, rows = pieces
        twins.append("grads")
        shapes.append(pltpu.VMEM((n_copies * rows, LANES), BF))
        out_shapes += [jax.ShapeDtypeStruct((n_copies // 2 * rows, LANES), BF)] * 2

    def kernel(scalars_ref, *args):
        inputs = dict(zip(ins, args[:n_in]))
        outputs = dict(zip(outs, args[n_in : n_in + n_out]))
        rest = args[n_in + len(out_shapes) :]
        vmem = dict(zip(twins, rest))
        sems, piece_sems = rest[len(twins) :]
        refs = Refs(inputs, outputs, vmem, sems)
        body(refs, scalars_ref)
        if pieces is not None:
            keep, send = args[n_in + n_out : n_in + n_out + 2]
            piece_copies(refs.grads, keep, send, scalars_ref[0], piece_sems, pieces, True)
        refs.finish()

    moved = sum(a.size * a.dtype.itemsize for a in ins.values())
    return pl.pallas_call(
        kernel,
        name=body.__name__,
        out_shape=out_shapes,
        grid_spec=pltpu.PrefetchScalarGridSpec(
            num_scalar_prefetch=1,
            grid=(),
            in_specs=[pl.BlockSpec(memory_space=pl.ANY)] * n_in,
            out_specs=[pl.BlockSpec(memory_space=pl.ANY)] * len(out_shapes),
            scratch_shapes=shapes
            + [pltpu.SemaphoreType.DMA((n_in + n_out,)), pltpu.SemaphoreType.DMA((n_copies,))],
        ),
        compiler_params=pltpu.CompilerParams(vmem_limit_bytes=56 << 20),
        cost_estimate=pl.CostEstimate(flops=flops, transcendentals=0, bytes_accessed=moved),
    )(scalars, *ins.values())


def piece_position(j, me, order):
    where = 0
    for bit in order:
        where = where * 2 + (((me >> bit) & 1) ^ ((j >> bit) & 1))
    return where


def piece_copies(buffer, first, second, me, sems, pieces, out):
    orders, count, rows = pieces

    def copies(mine):
        made = []
        for j in range(count):
            spot = pl.multiple_of(piece_position(j, me, orders[j & 1]) * rows, 16)
            half = first if (j & 1) == mine else second
            here = buffer.at[pl.ds(j * rows, rows), :]
            there = half.at[pl.ds(spot, rows), :]
            ends = (here, there) if out else (there, here)
            made.append(pltpu.make_async_copy(*ends, sems.at[j]))
        for copy in made:
            copy.start()
        for copy in made:
            copy.wait()

    @pl.when(me & 1 == 0)
    def even():
        copies(0)

    @pl.when(me & 1 == 1)
    def odd():
        copies(1)


def head_lanes(rows, which):
    lane = lax.broadcasted_iota(jnp.int32, (rows, LANES), 1)
    return (lane < HD) if which == 0 else (lane >= HD)


def only_head(panel, which):
    return jnp.where(head_lanes(panel.shape[0], which), panel, jnp.zeros_like(panel))


def turned(panel):
    lane = lax.broadcasted_iota(jnp.int32, panel.shape, 1)
    return jnp.where(
        lane % HD < HD // 2,
        pltpu.roll(panel, LANES - HD // 2, 1),
        pltpu.roll(panel, HD // 2, 1),
    )


def block_rows(index):
    return pl.ds(pl.multiple_of(index * BLK, BLK), BLK)


def panel_cols(panel):
    return slice(panel * LANES, (panel + 1) * LANES)


def blocks_of(sp):
    return sp, 3 - sp


def project_heads(refs, sp, entry, own):
    for half, block in enumerate(blocks_of(sp)):
        here = slice(half * BLK, (half + 1) * BLK)
        there = block_rows(block)
        rows = entry[here, :]
        keys = dot(rows, refs.w_key[...])
        refs.v[there, :] = dot(rows, refs.w_value[...]).astype(BF)
        if own:
            queries = dot(rows, refs.w_query[...])
        cosine = refs.cosine[there, :]
        sine = refs.sine[there, :]
        for panel in range(PANELS):
            cols = panel_cols(panel)
            part = keys[:, cols]
            refs.k[there, cols] = (part * cosine + turned(part) * sine).astype(BF)
            if own:
                part = queries[:, cols]
                refs.q[here, cols] = (part * cosine + turned(part) * sine).astype(BF) * SCALE


def query_blocks(sp, low):
    chip = sp >> 1
    return (block_rows(chip), low + 1), (block_rows(1 - chip), 4 - low)


def both_ways(sp, step):
    low = (sp & 1) ^ (sp >> 1)

    @pl.when(low == 0)
    def outer():
        step(0)

    @pl.when(low == 1)
    def inner():
        step(1)


def attend(refs, scalars, low):
    sp, length = scalars[1], scalars[2]
    lane = lax.broadcasted_iota(jnp.int32, (BLK, LANES), 1)

    def panel_step(panel, carry):
        cols = pl.ds(pl.multiple_of(panel * LANES, LANES), LANES)
        for rows, blocks in query_blocks(sp, low):
            seen = blocks * BLK
            queries = refs.q[rows, cols]
            outs, logs = [], []
            for which in range(2):
                scores = dot_nt(only_head(queries, which), refs.k[0:seen, cols])
                key_at = lax.broadcasted_iota(jnp.int32, (BLK, seen), 1)
                row_at = lax.broadcasted_iota(jnp.int32, (BLK, seen), 0) + (blocks - 1) * BLK
                scores = jnp.where((key_at <= row_at) & (key_at < length), scores, NEG)
                top = jnp.max(scores, axis=-1, keepdims=True)
                weights = jnp.exp(scores - top)
                total = jnp.sum(weights, axis=-1, keepdims=True)
                outs.append(dot(weights.astype(BF), refs.v[0:seen, cols]) / total)
                logs.append(top + jnp.log(total))
            refs.mixed[rows, cols] = jnp.where(head_lanes(BLK, 0), outs[0], outs[1]).astype(BF)
            kept = jnp.where(lane == 2 * panel, logs[0], refs.lse[rows, :])
            refs.lse[rows, :] = jnp.where(lane == 2 * panel + 1, logs[1], kept)
        return carry

    lax.fori_loop(0, PANELS, panel_step, 0)


def attention_forward(refs, scalars):
    sp = scalars[1]
    project_heads(refs, sp, refs.own, True)
    project_heads(refs, sp ^ 1, refs.sib, False)
    refs.lse[...] = jnp.zeros((ROWS, LANES), F32)
    both_ways(sp, lambda low: attend(refs, scalars, low))
    refs.send(refs.q, refs.k, refs.v, refs.lse, refs.mixed)


def ffn_forward(refs, ffn_in):
    for half in range(2):
        rows = slice(half * BLK, (half + 1) * BLK)
        gate = dot_nt(ffn_in[rows, :], refs.w_gate[...])
        up = dot_nt(ffn_in[rows, :], refs.w_up[...])
        refs.gate[rows, :] = gate
        refs.up[rows, :] = up
        refs.hidden[rows, :] = (gate * jax.nn.sigmoid(gate) * up).astype(BF)


def store_panels(refs, at, grad):
    height = grad.shape[0]
    for panel in range(PANELS):
        put = slice(at + panel * height, at + (panel + 1) * height)
        refs.grads[put, :] = grad[:, panel_cols(panel)].astype(BF)


def ffn_weight_grads(refs, at, ffn_in, grad_result):
    grad_down = grad_result.astype(BF)
    store_panels(refs, at, dot_tn(refs.hidden[...], grad_down))
    for half in range(2):
        rows = slice(half * BLK, (half + 1) * BLK)
        grad_hidden = dot_nt(grad_down[rows, :], refs.w_down[...])
        gate = refs.gate[rows, :]
        sigma = jax.nn.sigmoid(gate)
        grad_gate = grad_hidden * refs.up[rows, :] * (sigma * (1.0 + gate * (1.0 - sigma)))
        refs.dgate[rows, :] = grad_gate.astype(BF)
        refs.dup[rows, :] = (grad_hidden * (gate * sigma)).astype(BF)
    store_panels(refs, at + PANELS * FF, dot_tn(refs.dgate[...], ffn_in))
    store_panels(refs, at + 2 * PANELS * FF, dot_tn(refs.dup[...], ffn_in))


def ffn_input_grad(refs):
    return dot(refs.dgate[...], refs.w_gate[...]) + dot(refs.dup[...], refs.w_up[...])


def clear_tail(refs, start):
    end = refs.grads.shape[0]
    refs.grads[start:end, :] = jnp.zeros((end - start, LANES), BF)


def store_gains(refs, at, gains):
    row = lax.broadcasted_iota(jnp.int32, (GAIN_ROWS, LANES), 0)
    block = jnp.zeros((GAIN_ROWS, LANES), F32)
    for slot, gain in enumerate(gains):
        for panel in range(PANELS):
            block = jnp.where(row == PANELS * slot + panel, gain[:, panel_cols(panel)], block)
    refs.grads[at : at + GAIN_ROWS, :] = block.astype(BF)


def post_forward(refs, scalars):
    attention_forward(refs, scalars)
    middle = refs.own[...].astype(F32) + dot(refs.mixed[...], refs.w_out[...])
    refs.middle[...] = middle
    refs.send(refs.middle)
    state = middle * inv_rms(middle) * refs.attn_gain[...]
    ffn_forward(refs, state.astype(BF))
    result = state + dot(refs.hidden[...], refs.w_down[...])
    refs.result[...] = result
    output = result * inv_rms(result) * refs.ffn_gain[...]
    entry = output * inv_rms(output) * refs.next_gain[...]
    refs.entry[...] = entry.astype(BF)
    refs.send(refs.result, refs.entry)


def pre_forward(refs, scalars):
    attention_forward(refs, scalars)
    clear_tail(refs, FFN_ROWS)
    result = refs.result[...]
    inputs = result * inv_rms(result) * refs.last_gain[...]
    middle = inputs + dot(refs.mixed[...], refs.w_out[...])
    refs.middle[...] = middle
    refs.send(refs.middle)
    ffn_in = (middle * inv_rms(middle) * refs.ffn_gain[...]).astype(BF)
    ffn_forward(refs, ffn_in)
    output = middle + dot(refs.hidden[...], refs.w_down[...])
    refs.output[...] = output.astype(BF)
    refs.send(refs.output)
    sp, length = scalars[1], scalars[2]
    row = lax.broadcasted_iota(jnp.int32, (ROWS, D), 0)
    position = row + jnp.where(row < BLK, sp * BLK, (2 - sp) * BLK)
    cotangent = jnp.where(position < length, refs.cotangent[...].astype(F32), 0.0)
    refs.upstream[...] = cotangent
    refs.send(refs.upstream)
    ffn_weight_grads(refs, 0, ffn_in, cotangent)
    refs.send(refs.dgate, refs.dup)


def attend_back(refs, scalars, low):
    sp, length = scalars[1], scalars[2]
    if low == 1:
        refs.dk[3 * BLK :, :] = jnp.zeros((BLK, D), F32)
        refs.dv[3 * BLK :, :] = jnp.zeros((BLK, D), F32)

    def panel_step(panel, carry):
        cols = pl.ds(pl.multiple_of(panel * LANES, LANES), LANES)
        for rows, blocks in reversed(query_blocks(sp, low)):
            seen = blocks * BLK
            queries = refs.q[rows, cols]
            grads = refs.gmix[rows, cols]
            keys = refs.k[0:seen, cols]
            values = refs.v[0:seen, cols]
            key_at = lax.broadcasted_iota(jnp.int32, (seen, BLK), 0)
            row_at = lax.broadcasted_iota(jnp.int32, (seen, BLK), 1) + (blocks - 1) * BLK
            allowed = (key_at <= row_at) & (key_at < length)
            grad_q = jnp.zeros((BLK, LANES), F32)
            grad_k = jnp.zeros((seen, LANES), F32)
            grad_v = jnp.zeros((seen, LANES), F32)
            for which in range(2):
                q_head = only_head(queries, which)
                g_head = only_head(grads, which)
                at = pl.ds(2 * panel + which, 1)
                scores = jnp.where(allowed, dot_nt(keys, q_head), NEG)
                probs = jnp.exp(scores - refs.lse_t[at, rows])
                grad_p = dot_nt(values, g_head)
                grad_s = (probs * (grad_p - refs.delta_t[at, rows])).astype(BF)
                grad_v = grad_v + dot(probs.astype(BF), g_head)
                grad_k = grad_k + dot(grad_s, q_head)
                grad_q = grad_q + dot_tn(grad_s, only_head(keys, which))
            refs.dq[rows, cols] = grad_q * SCALE
            if blocks == 4 - low:
                refs.dk[0:seen, cols] = grad_k
                refs.dv[0:seen, cols] = grad_v
            else:
                refs.dk[0:seen, cols] += grad_k
                refs.dv[0:seen, cols] += grad_v
        return carry

    lax.fori_loop(0, PANELS, panel_step, 0)


def attention_backward(refs, scalars, grad_middle):
    sp = scalars[1]
    grad_attn = grad_middle.astype(BF)
    mixed = refs.mixed[...]
    grad_mixed = dot_nt(grad_attn, refs.w_out[...]).astype(BF)
    refs.gmix[...] = grad_mixed
    product = grad_mixed.astype(F32) * mixed.astype(F32)
    high = product.astype(BF)
    rest = (product - high.astype(F32)).astype(BF)
    head_of = lax.broadcasted_iota(jnp.int32, (HEADS, D), 1) // HD
    pick = (head_of == lax.broadcasted_iota(jnp.int32, (HEADS, D), 0)).astype(F32).astype(BF)
    refs.delta_t[...] = dot_nt(pick, high) + dot_nt(pick, rest)
    refs.lse_t[...] = jnp.transpose(refs.lse[...])[0:HEADS, :]
    refs.q, refs.k, refs.v
    both_ways(sp, lambda low: attend_back(refs, scalars, low))

    def unrotated(ref, here, there, cols):
        part = ref[here, cols]
        return (part * refs.cosine[there, :] - turned(part) * refs.sine[there, :]).astype(BF)

    for spot, block in enumerate(blocks_of(sp) + blocks_of(sp ^ 1)):
        put, there = slice(spot * BLK, (spot + 1) * BLK), block_rows(block)
        refs.dvp[put, :] = refs.dv[there, :].astype(BF)
        for panel in range(PANELS):
            cols = panel_cols(panel)
            refs.dkp[put, cols] = unrotated(refs.dk, there, there, cols)
            if spot < 2:
                refs.dqp[put, cols] = unrotated(refs.dq, put, there, cols)
    refs.send(refs.dqp, refs.dkp, refs.dvp)
    w_key, w_value = refs.w_key[...], refs.w_value[...]
    theirs = slice(ROWS, 2 * ROWS)
    ge_sib = dot_nt(refs.dkp[theirs, :], w_key) + dot_nt(refs.dvp[theirs, :], w_value)
    refs.ge_sib[...] = ge_sib.astype(BF)
    refs.send(refs.ge_sib)
    mine = slice(0, ROWS)
    return (
        dot_nt(refs.dqp[...], refs.w_query[...])
        + dot_nt(refs.dkp[mine, :], w_key)
        + dot_nt(refs.dvp[mine, :], w_value)
    )


def pre_attention_backward(refs, scalars):
    grad_normed, grad_gain = rms_back(refs.middle[...], refs.ffn_gain[...], ffn_input_grad(refs))
    grad_middle = refs.upstream[...] + grad_normed
    refs.grad_middle[...] = grad_middle
    refs.grad_gain[...] = grad_gain
    refs.send(refs.grad_middle, refs.grad_gain)
    refs.ge_own[...] = attention_backward(refs, scalars, grad_middle)
    refs.send(refs.ge_own)


def post_attention_backward(refs, scalars):
    grad_middle = refs.grad_middle[...]
    refs.ge_own[...] = grad_middle + attention_backward(refs, scalars, grad_middle)
    refs.send(refs.ge_own)


def attention_weight_grads(refs, at):
    step = PANELS * D
    store_panels(refs, at, dot_tn(refs.mixed[...], refs.grad_middle[...].astype(BF)))
    own, sib = refs.own[...], refs.sib[...]
    store_panels(refs, at + step, dot_tn(own, refs.dqp[...]))
    for k, ref in enumerate((refs.dkp, refs.dvp)):
        total = dot_tn(own, ref[0:ROWS, :]) + dot_tn(sib, ref[ROWS : 2 * ROWS, :])
        store_panels(refs, at + (k + 2) * step, total)


def last_weight_grads(refs, scalars):
    attention_weight_grads(refs, 0)
    if refs.grads.shape[0] > ATTN_ROWS:
        clear_tail(refs, ATTN_ROWS)


def post_ffn_backward(refs, scalars):
    attention_weight_grads(refs, FFN_ROWS)
    clear_tail(refs, FFN_ROWS + ATTN_ROWS)
    middle = refs.middle[...]
    gain = refs.attn_gain[...]
    ffn_in = (middle * inv_rms(middle) * gain).astype(BF)
    ffn_forward(refs, ffn_in)
    result = refs.result[...]
    out_gain = refs.ffn_gain[...]
    inputs = result * inv_rms(result) * out_gain
    grad_entry = refs.ge_own[...] + refs.ge_recv[...].astype(F32)
    grad_normed, grad_next = rms_back(inputs, refs.next_gain[...], grad_entry)
    grad_result, grad_ffn_gain = rms_back(result, out_gain, refs.grad_middle[...] + grad_normed)
    ffn_weight_grads(refs, 0, ffn_in, grad_result)
    grad_middle, grad_attn_gain = rms_back(middle, gain, grad_result + ffn_input_grad(refs))
    refs.new_middle[...] = grad_middle
    refs.send(refs.new_middle)
    gains = (refs.grad_gain[...], grad_next, grad_ffn_gain, grad_attn_gain)
    store_gains(refs, FFN_ROWS + ATTN_ROWS, gains)


def unpack(first, second, scalars, pieces, heights, gains):
    orders, count, rows = pieces
    shapes = [(height, D) for height in heights] + [(PANELS, LANES)] * gains

    def unpack(scalars_ref, first_ref, second_ref, *rest):
        outs, buffer, sems = rest[: len(shapes)], rest[-2], rest[-1]
        piece_copies(buffer, first_ref, second_ref, scalars_ref[0], sems, pieces, False)
        at = 0
        for height, out in zip(heights, outs):
            for panel in range(PANELS):
                out[:, panel_cols(panel)] = buffer[at : at + height, :].astype(F32)
                at += height
        if gains:
            block = buffer[at : at + GAIN_ROWS, :].astype(F32)
            for slot in range(gains):
                outs[len(heights) + slot][...] = block[PANELS * slot : PANELS * (slot + 1), :]

    return pl.pallas_call(
        unpack,
        name=unpack.__name__,
        out_shape=[jax.ShapeDtypeStruct(shape, F32) for shape in shapes],
        grid_spec=pltpu.PrefetchScalarGridSpec(
            num_scalar_prefetch=1,
            grid=(),
            in_specs=[pl.BlockSpec(memory_space=pl.ANY)] * 2,
            out_specs=[pl.BlockSpec(memory_space=pltpu.VMEM)] * len(shapes),
            scratch_shapes=[
                pltpu.VMEM((count * rows, LANES), BF),
                pltpu.SemaphoreType.DMA((count,)),
            ],
        ),
        compiler_params=pltpu.CompilerParams(vmem_limit_bytes=40 << 20),
        cost_estimate=pl.CostEstimate(
            flops=0, transcendentals=0, bytes_accessed=6 * count * rows * LANES
        ),
    )(scalars, first, second)


def solution(mesh):
    n_dp, n_sp = mesh.shape["dp"], mesh.shape["sp"]
    count = n_dp * n_sp
    if n_sp != 4 or n_dp & (n_dp - 1) or n_dp < 2:
        raise ValueError
    bits = count.bit_length() - 1

    def swap(array, move):
        return lax.ppermute(array, AXES, [(k, move(k)) for k in range(count)])

    def sibling(array):
        return swap(array, lambda k: k ^ 1)

    tail = list(range(3, bits))
    orders = ([1, 2] + tail, [2, 1] + tail)

    def pieces_for(used):
        return orders, count, pl.cdiv(pl.cdiv(used, count), 16) * 16

    class Sum:
        def __init__(self, keep, send):
            self.keep, self.wire, self.stage = keep, sibling(send), 0

        def move(self, stage):
            return lambda k: k ^ (1 << orders[k & 1][stage])

        def step(self):
            last = bits - 1
            if self.stage < last:
                half = self.keep.shape[0] // 2
                total = self.keep.astype(F32) + self.wire.astype(F32)
                self.wire = swap(total[half:].astype(BF), self.move(self.stage))
                self.keep = total[:half].astype(BF)
            else:
                if self.stage == last:
                    self.keep = (self.keep.astype(F32) + self.wire.astype(F32)).astype(BF)
                else:
                    self.keep = jnp.concatenate([self.keep, self.wire], axis=0)
                back = 2 * last - 1 - self.stage
                self.wire = sibling(self.keep) if back < 0 else swap(self.keep, self.move(back))
            self.stage += 1

        def before(self, array):
            array, self.wire = lax.optimization_barrier((array, self.wire))
            self.step()
            return array

        def finish(self):
            while self.stage < 2 * bits - 1:
                self.step()
            return self.keep, self.wire

    def body(tokens, lengths, *rest):
        out_grad = rest[-1]
        post_query, post_key, post_value, post_out, post_gate, post_up, post_down = rest[0:7]
        pre_query, pre_key, pre_value, pre_out, pre_gate, pre_up, pre_down = rest[9:16]
        gains = [rest[k].reshape(1, D) for k in (7, 8, 16, 17)]
        post_attn_gain, post_ffn_gain, pre_attn_gain, pre_ffn_gain = gains
        sp = lax.axis_index("sp")
        me = lax.axis_index("dp") * n_sp + sp
        chip = sp >> 1
        scalars = jnp.stack([me, sp, lengths[chip]]).astype(jnp.int32)

        def to_slot(array):
            mine = lax.dynamic_index_in_dim(array, chip, 0, keepdims=False)
            other = lax.dynamic_index_in_dim(array, 1 - chip, 0, keepdims=False)
            return jnp.concatenate([mine, swap(other, lambda k: k ^ 3)], axis=0)

        def from_slot(array):
            mine, other = array[:BLK], swap(array[BLK:], lambda k: k ^ 3)
            return jnp.where(chip == 0, jnp.stack([mine, other]), jnp.stack([other, mine]))

        inverse = 10000.0 ** (-jnp.arange(HD // 2, dtype=F32) * 2.0 / HD)
        angles = jnp.arange(SEQ, dtype=F32)[:, None] * inverse[None, :]
        cosine = jnp.tile(jnp.cos(angles), (1, 4))
        sine = jnp.tile(jnp.concatenate([-jnp.sin(angles), jnp.sin(angles)], axis=-1), (1, 2))
        tables = dict(cosine=cosine, sine=sine)

        own_one = to_slot(tokens)
        sib_one = sibling(own_one)
        cotangent = to_slot(out_grad)

        rows_bf, rows_f32, full_bf = ((ROWS, D), BF), ((ROWS, D), F32), ((SEQ, D), BF)
        wide_bf, wide_f32 = ((ROWS, FF), BF), ((ROWS, FF), F32)
        saved = dict(q=rows_bf, k=full_bf, v=full_bf, lse=((ROWS, LANES), F32), mixed=rows_bf)
        wide = dict(gate=wide_f32, up=wide_f32, hidden=wide_bf)
        wide_back = dict(dgate=wide_bf, dup=wide_bf)
        ffn_pieces = pieces_for(FFN_ROWS)
        both_pieces = pieces_for(FFN_ROWS + ATTN_ROWS + GAIN_ROWS)
        attn_pieces = pieces_for(ATTN_ROWS)
        post_ffn = dict(w_gate=post_gate.T, w_up=post_up.T, w_down=post_down)
        pre_ffn = dict(w_gate=pre_gate.T, w_up=pre_up.T, w_down=pre_down)

        q1, k1, v1, lse1, mixed1, middle1, result1, entry2 = run_kernel(
            post_forward,
            scalars,
            dict(own=own_one, w_key=post_key, w_value=post_value, w_query=post_query, **tables)
            | dict(sib=sib_one, w_out=post_out, attn_gain=post_attn_gain, **post_ffn)
            | dict(ffn_gain=post_ffn_gain, next_gain=pre_attn_gain),
            saved | dict(middle=rows_f32, result=rows_f32, entry=rows_bf),
            wide,
            flops=8 * 10**9,
        )
        sib_two = sibling(entry2)
        pre_out_shapes = dict(middle=rows_f32, output=rows_bf, upstream=rows_f32)
        q2, k2, v2, lse2, mixed2, middle2, out_rows, upstream2, dgate2, dup2, keep, send = run_kernel(
            pre_forward,
            scalars,
            dict(own=entry2, w_key=pre_key, w_value=pre_value, w_query=pre_query, **tables)
            | dict(sib=sib_two, result=result1, last_gain=post_ffn_gain, w_out=pre_out)
            | dict(ffn_gain=pre_ffn_gain, cotangent=cotangent, **pre_ffn),
            saved | pre_out_shapes | wide_back,
            wide,
            pieces=ffn_pieces,
            flops=14 * 10**9,
        )
        sum_ffn2 = Sum(keep, send)

        back_outs = dict(dqp=rows_bf, dkp=full_bf, dvp=full_bf, ge_sib=rows_bf)
        head_f32 = ((HEADS, ROWS), F32)
        full_f32 = ((SEQ, D), F32)
        back_scratch = dict(gmix=rows_bf, lse_t=head_f32, delta_t=head_f32, dq=rows_f32)
        back_scratch |= dict(dk=full_f32, dv=full_f32)

        dqp, dkp, dvp, ge_sib, grad_middle2, grad_gain, ge_own = run_kernel(
            pre_attention_backward,
            scalars,
            dict(dgate=dgate2, w_gate=pre_ffn["w_gate"], dup=dup2, w_up=pre_ffn["w_up"])
            | dict(middle=middle2, ffn_gain=pre_ffn_gain, upstream=upstream2)
            | dict(mixed=mixed2, w_out=pre_out, lse=lse2, q=q2, k=k2, v=v2, **tables)
            | dict(w_key=pre_key, w_value=pre_value, w_query=pre_query),
            back_outs | dict(grad_middle=rows_f32, grad_gain=((1, D), F32), ge_own=rows_f32),
            back_scratch,
            flops=12 * 10**9,
        )
        ge_recv = sibling(ge_sib)
        ge_recv = sum_ffn2.before(ge_recv)
        grad_middle1, keep, send = run_kernel(
            post_ffn_backward,
            scalars,
            dict(mixed=mixed2, grad_middle=grad_middle2, own=entry2, sib=sib_two)
            | dict(dqp=dqp, dkp=dkp, dvp=dvp, middle=middle1, attn_gain=post_attn_gain, **post_ffn)
            | dict(result=result1, ffn_gain=post_ffn_gain, ge_own=ge_own, ge_recv=ge_recv)
            | dict(next_gain=pre_attn_gain, grad_gain=grad_gain),
            dict(new_middle=rows_f32),
            wide | wide_back,
            pieces=both_pieces,
            flops=10 * 10**9,
        )
        sum_both = Sum(keep, send)
        grad_middle1 = sum_ffn2.before(grad_middle1)
        dqp, dkp, dvp, ge_sib, ge_own = run_kernel(
            post_attention_backward,
            scalars,
            dict(grad_middle=grad_middle1, mixed=mixed1, w_out=post_out)
            | dict(lse=lse1, q=q1, k=k1, v=v1, **tables)
            | dict(w_key=post_key, w_value=post_value, w_query=post_query),
            back_outs | dict(ge_own=rows_f32),
            back_scratch,
            flops=12 * 10**9,
        )
        dqp = sum_ffn2.before(dqp)
        dqp = sum_both.before(dqp)
        keep, send = run_kernel(
            last_weight_grads,
            scalars,
            dict(mixed=mixed1, grad_middle=grad_middle1, own=own_one, sib=sib_one)
            | dict(dqp=dqp, dkp=dkp, dvp=dvp),
            {},
            {},
            pieces=attn_pieces,
            flops=3 * 10**9,
        )
        sum_attn1 = Sum(keep, send)
        ge_recv = sibling(ge_sib)
        output = from_slot(out_rows)
        tokens_grad = from_slot((ge_own + ge_recv.astype(F32)).astype(BF))

        ffn_heights, attn_heights = [FF] * 3, [D] * 4
        down2, gate2, up2 = unpack(*sum_ffn2.finish(), scalars, ffn_pieces, ffn_heights, 0)
        both = unpack(*sum_both.finish(), scalars, both_pieces, ffn_heights + attn_heights, 4)
        down1, gate1, up1, out2, query2, key2, value2 = both[:7]
        gain_pre_ffn, gain_pre_attn, gain_post_ffn, gain_post_attn = (g.reshape(D) for g in both[7:])
        out1, query1, key1, value1 = unpack(
            *sum_attn1.finish(), scalars, attn_pieces, attn_heights, 0
        )
        post_grads = (query1, key1, value1, out1, gate1.T, up1.T, down1, gain_post_attn, gain_post_ffn)
        pre_grads = (query2, key2, value2, out2, gate2.T, up2.T, down2, gain_pre_attn, gain_pre_ffn)
        return (output, tokens_grad) + post_grads + pre_grads

    spread = P("dp", "sp", None)
    in_specs = (spread, P("dp")) + (P(),) * 18 + (spread,)
    out_specs = (spread, spread) + (P(),) * 18
    return jax.shard_map(body, mesh=mesh, in_specs=in_specs, out_specs=out_specs, check_vma=False)
```

time: 982 us -> 321 us (0.33)
  waiting for transfers between devices: 536 us -> 123 us
  matrix products: 129 us -> 0 us
  Pallas kernels: 0 us -> 124 us
  local copies, waits for them, and re-layouts: 113 us -> 14.6 us
  blocking collectives: 55.3 us -> 0 us
  other arithmetic: 61.6 us -> 13.6 us
  starting transfers between devices: 58.6 us -> 39.3 us
  between operations: 15.6 us -> 1.72 us
    psum x1 -> x0, waiting for transfers between devices: 487 us -> none  [reduce_grads(): summed = lax.psum(weights, ('dp', 'sp'))]
    dot_general x66 -> x0, matrix products: 124 us -> none  [the longest x8 12.8 us: slot_scores(): jnp.einsum('qhd,khd->hqk', queries, key_heads, preferred_element_type=jnp...]
    pallas_call x0 -> x9, Pallas kernels: none -> 124 us  [the longest x6 101 us: run_kernel(): pl.pallas_call(kernel, name=body.__name__, out_shape=out_shapes, grid_spe...]
    ppermute x0 -> x38, waiting for transfers between devices: none -> 123 us  [swap(): return lax.ppermute(array, AXES, [(k, move(k)) for k in range(count)])]
    all_to_all x15 -> x0, starting transfers between devices: 58.5 us -> none  [the longest x2 8.86 us: layer_backward(): lax.all_to_all(grad_mixed.reshape(slot_count, row_count, group, local_hea...]
    all_to_all x15 -> x0, waiting for transfers between devices: 48.6 us -> none  [the longest x2 16 us: layer_forward(): lax.all_to_all(query_rows, 'sp', split_axis=2, concat_axis=1, tiled=True)]
    psum x1 -> x0, blocking collectives: 42.8 us -> none  [reduce_grads(): gains = lax.psum(grads[7:], ('dp', 'sp'))]
    reshape x24 -> x0, local copies, waits for them, and re-layouts: 40.4 us -> none  [the longest x6 11.1 us: head_pack(): return values.reshape(slot_count, full_rows, 1, local_heads * HD)]
  transfers between devices with their start and end apart: 16 -> 38, of which waited for: 14 -> 17; matrix products, arithmetic and copies ran while one was open for 9% -> 7% of each run, Pallas kernels for 0% -> 23%
where the time goes in v2:
time: 321 us; the launch traced here: 316 us
  Pallas kernels  124 us (39%)
  waiting for transfers between devices  123 us (38%)
  starting transfers between devices  39.3 us (12%)
  local copies, waits for them, and re-layouts  14.6 us (5%)
  other arithmetic  13.6 us (4%)
    ppermute x38, waiting for transfers between devices, swap(): return lax.ppermute(array, AXES, [(k, move(k)) for k in range(count)])  123 us
    pallas_call x6, Pallas kernels, run_kernel(): pl.pallas_call(kernel, name=body.__name__, out_shape=out_shapes, grid_spe...  101 us
    ppermute x38, starting transfers between devices, swap(): return lax.ppermute(array, AXES, [(k, move(k)) for k in range(count)])  39.3 us
    pallas_call x3, Pallas kernels, unpack(): pl.pallas_call(unpack, name=unpack.__name__, out_shape=[jax.ShapeDtypeStr...  22.5 us
  transfers between devices with their start and end apart: 38, of which 17 were waited for; matrix products, arithmetic and copies ran while one was open for 7% of the time, Pallas kernels for 23%

profile of v2, /device:TPU:0, one launch (start us, length us, event | category | flops | bytes accessed | tf_op | source)
XLA Modules:
  0.0 315.5 jit_solution(4591919968416013668)
XLA Ops:
  0.7 1.1 dynamic-slice_bitcast_fusion.3
  1.7 2.4 collective-permute-start
  4.2 1.2 dynamic_slice.16
  5.4 5.5 %collective-permute-done = bf16[256,512]{1,0:T(8,128)(2,1)S(1)} collective-permute-done((bf16[256,512]{1,0:T(8,128)(2,1)S(1)}, bf16[256,512]{1,0:T(8,128)(2,1)S(1)}, u32[]{:S(2)}, u32[]{:S(2)}) %collective-permute-start) | collective-permute-done | bytes 262176 | tf_op jit(solution)/shard_map/ppermute | solution.py:538
  11.7 1.0 copy.41.args_4_.args_13_.args_7_
  12.8 1.0 copy.42.args_5_.args_14_.args_8_
  13.8 1.2 pad_add_fusion.scalars_ref
  15.0 0.8 copy-done.9
  15.8 17.8 %post_forward.1 = (bf16[512,512]{1,0:T(8,128)(2,1)}, bf16[1024,512]{1,0:T(8,128)(2,1)}, bf16[1024,512]{1,0:T(8,128)(2,1)}, f32[512,128]{1,0:T(8,128)}, bf16[512,...) custom-call(s32[3]{0:T(128)} %pad_add_fusion.scalars_ref, ...), custom_call_target="tpu_custom_call" | custom-call | flops 8000000000 | bytes 8427520 | tf_op jit(solution)/shard_map/post_forward/pallas_call | solution.py:112
  33.8 2.5 collective-permute-start.3
  36.3 6.5 %collective-permute-done.3 = bf16[256,512]{1,0:T(8,128)(2,1)S(1)} collective-permute-done((bf16[256,512]{1,0:T(8,128)(2,1)S(1)}, bf16[256,512]{1,0:T(8,128)(2,1)S(1)}, u32[]{:S(2)}, u32[]{:S(2)}) %collective-permute-start.3) | collective-permute-done | bytes 262176 | tf_op jit(solution)/shard_map/ppermute | solution.py:538
  42.8 0.8 pad_maximum_fusion.5.args_11_
  43.7 0.8 copy-done.10
  44.4 22.7 %pre_forward.1 = (bf16[512,512]{1,0:T(8,128)(2,1)}, bf16[1024,512]{1,0:T(8,128)(2,1)}, bf16[1024,512]{1,0:T(8,128)(2,1)}, f32[512,128]{1,0:T(8,128)}, bf16[512,5...) custom-call(s32[3]{0:T(128)} %pad_add_fusion.scalars_ref, ...), custom_call_target="tpu_custom_call" | custom-call | flops 14000000000 | bytes 9998336 | tf_op jit(solution)/shard_map/pre_forward/pallas_call | solution.py:112
  67.2 20.6 %pre_attention_backward.1 = (bf16[512,512]{1,0:T(8,128)(2,1)}, bf16[1024,512]{1,0:T(8,128)(2,1)}, bf16[1024,512]{1,0:T(8,128)(2,1)}, bf16[512,512]{1,0:T(8,128)(...) custom-call(s32[3]{0:T(128)} %pad_add_fusion.scalars_ref, ...), custom_call_target="tpu_custom_call" | custom-call | flops 12000000000 | bytes 14288896 | tf_op jit(solution)/shard_map/pre_attention_backward/pallas_call | solution.py:112
  88.2 1.9 collective-permute-done.5.args_15_
  90.1 0.8 add_convert_fusion.1
  90.9 2.2 collective-permute-start.7
  93.1 17.1 %post_ffn_backward.1 = (f32[512,512]{1,0:T(8,128)}, bf16[12544,128]{1,0:T(8,128)(2,1)}, bf16[12544,128]{1,0:T(8,128)(2,1)}) custom-call(s32[3]{0:T(128)} %pad_add_fusion.scalars_ref, bf16[512,512]{1,0:T(8,128)(2,1)} %get-tuple-element.86.args_7_.args_0_, f32[512,512]{1,0:T(8,128)} %get-tuple-element.95.args_1_, ...), custom_call_target="tpu_custom_call" | custom-call | flops 10000000000 | bytes 13148160 | tf_op jit(solution)/shard_map/post_ffn_backward/pallas_call | solution.py:112
  110.7 1.6 collective-permute-start.10
  112.3 16.6 %post_attention_backward.1 = (bf16[512,512]{1,0:T(8,128)(2,1)}, bf16[1024,512]{1,0:T(8,128)(2,1)}, bf16[1024,512]{1,0:T(8,128)(2,1)}, bf16[512,512]{1,0:T(8,128)(2,1)}, f32[512,512]{1,0:T(8,128)}) custom-call(s32[3]{0:T(128)} %pad_add_fusion.scalars_ref, f32[512,512]{1,0:T(8,128)} %get-tuple-element.108.args_0_.args_1_, ...), custom_call_target="tpu_custom_call" | custom-call | flops 12000000000 | bytes 7602176 | tf_op jit(solution)/shard_map/post_attention_backward/pallas_call | solution.py:112
  128.9 2.3 add_convert_fusion
  131.7 20.6 %collective-permute-done.22 = bf16[6272,128]{1,0:T(8,128)(2,1)S(1)} collective-permute-done((bf16[6272,128]{1,0:T(8,128)(2,1)S(1)}, bf16[6272,128]{1,0:T(8,128)(2,1)S(1)}, u32[]{:S(2)}, u32[]{:S(2)}) %collective-permute-start.22) | collective-permute-done | bytes 1605664 | tf_op jit(solution)/shard_map/ppermute | solution.py:538
  153.4 1.7 collective-permute-start.31
  155.1 6.3 %last_weight_grads.1 = (bf16[4096,128]{1,0:T(8,128)(2,1)}, bf16[4096,128]{1,0:T(8,128)(2,1)}) custom-call(s32[3]{0:T(128)} %pad_add_fusion.scalars_ref, bf16[512,512]{1,0:T(8,128)(2,1)} %get-tuple-element.109.args_1_.args_0_, f32[512,512]{1,0:T(8,128)} %get-tuple-element.108.args_0_.args_1_, bf16[512,512]{1,0:T(8,128)(2,1)} %copy-done.7, ...), custom_call_target="tpu_custom_call" | custom-call | flops 3000000000 | bytes 5242880 | tf_op jit(solution)/shard_map/last_weight_grads/pallas_call | solution.py:112
  161.5 3.5 %collective-permute-done.23 = bf16[3136,128]{1,0:T(8,128)(2,1)S(1)} collective-permute-done((bf16[3136,128]{1,0:T(8,128)(2,1)S(1)}, bf16[3136,128]{1,0:T(8,128)(2,1)S(1)}, u32[]{:S(2)}, u32[]{:S(2)}) %collective-permute-start.23) | collective-permute-done | bytes 802848 | tf_op jit(solution)/shard_map/ppermute | solution.py:538
  165.2 1.6 collective-permute-start.24
  166.9 2.6 collective-permute-start.32
  169.6 6.6 %collective-permute-done.32 = bf16[528,128]{1,0:T(8,128)(2,1)S(1)} collective-permute-done((bf16[528,128]{1,0:T(8,128)(2,1)S(1)}, bf16[528,128]{1,0:T(8,128)(2,1)S(1)}, u32[]{:S(2)}, u32[]{:S(2)}) %collective-permute-start.32) | collective-permute-done | bytes 135200 | tf_op jit(solution)/shard_map/ppermute | solution.py:538
  176.9 3.4 %collective-permute-start.33 = (bf16[528,128]{1,0:T(8,128)(2,1)S(1)}, bf16[528,128]{1,0:T(8,128)(2,1)S(1)}, u32[]{:S(2)}, u32[]{:S(2)}) collective-permute-start(bf16[528,128]{1,0:T(8,128)(2,1)S(1)} %get-tuple-element.147), channel_id=1, source_target_pairs={{0,16},{1,17},{2,18},{3,19},{4,20},{5,21},{6,22},{7,23},{8,24},{9,... | collective-permute-start | bytes 405512 | tf_op jit(solution)/shard_map/ppermute | solution.py:538
  180.8 1.3 collective-permute-start.13
  182.1 11.3 %collective-permute-done.25 = bf16[784,128]{1,0:T(8,128)(2,1)S(1)} collective-permute-done((bf16[784,128]{1,0:T(8,128)(2,1)S(1)}, bf16[784,128]{1,0:T(8,128)(2,1)S(1)}, u32[]{:S(2)}, u32[]{:S(2)}) %collective-permute-start.25) | collective-permute-done | bytes 200736 | tf_op jit(solution)/shard_map/ppermute | solution.py:538
  193.6 2.0 collective-permute-start.34
  196.3 7.5 %collective-permute-done.26 = bf16[784,128]{1,0:T(8,128)(2,1)S(1)} collective-permute-done((bf16[784,128]{1,0:T(8,128)(2,1)S(1)}, bf16[784,128]{1,0:T(8,128)(2,1)S(1)}, u32[]{:S(2)}, u32[]{:S(2)}) %collective-permute-start.26) | collective-permute-done | bytes 200736 | tf_op jit(solution)/shard_map/ppermute | solution.py:538
  204.1 0.9 collective-permute-start.14
  204.9 10.1 %collective-permute-done.27 = bf16[1568,128]{1,0:T(8,128)(2,1)S(1)} collective-permute-done((bf16[1568,128]{1,0:T(8,128)(2,1)S(1)}, bf16[1568,128]{1,0:T(8,128)(2,1)S(1)}, u32[]{:S(2)}, u32[]{:S(2)}) %collective-permute-start.27) | collective-permute-done | bytes 401440 | tf_op jit(solution)/shard_map/ppermute | solution.py:538
  215.6 1.7 collective-permute-start.35
  217.7 0.7 constant_dynamic-update-slice_fusion.12
  218.5 4.0 %collective-permute-done.15 = bf16[512,128]{1,0:T(8,128)(2,1)S(1)} collective-permute-done((bf16[512,128]{1,0:T(8,128)(2,1)S(1)}, bf16[512,128]{1,0:T(8,128)(2,1)S(1)}, u32[]{:S(2)}, u32[]{:S(2)}) %collective-permute-start.15) | collective-permute-done | bytes 131104 | tf_op jit(solution)/shard_map/ppermute | solution.py:538
  222.5 1.2 collective-permute-start.16
  223.7 3.6 %collective-permute-done.28 = bf16[3136,128]{1,0:T(8,128)(2,1)S(1)} collective-permute-done((bf16[3136,128]{1,0:T(8,128)(2,1)S(1)}, bf16[3136,128]{1,0:T(8,128)(2,1)S(1)}, u32[]{:S(2)}, u32[]{:S(2)}) %collective-permute-start.28) | collective-permute-done | bytes 802848 | tf_op jit(solution)/shard_map/ppermute | solution.py:538
  227.4 1.6 collective-permute-start.29
  230.1 7.7 %collective-permute-done.35 = bf16[2112,128]{1,0:T(8,128)(2,1)S(1)} collective-permute-done((bf16[2112,128]{1,0:T(8,128)(2,1)S(1)}, bf16[2112,128]{1,0:T(8,128)(2,1)S(1)}, u32[]{:S(2)}, u32[]{:S(2)}) %collective-permute-start.35) | collective-permute-done | bytes 540704 | tf_op jit(solution)/shard_map/ppermute | solution.py:538
  237.9 1.8 collective-permute-start.36
  240.0 8.5 %collective-permute-done.29 = bf16[6272,128]{1,0:T(8,128)(2,1)S(1)} collective-permute-done((bf16[6272,128]{1,0:T(8,128)(2,1)S(1)}, bf16[6272,128]{1,0:T(8,128)(2,1)S(1)}, u32[]{:S(2)}, u32[]{:S(2)}) %collective-permute-start.29) | collective-permute-done | bytes 1605664 | tf_op jit(solution)/shard_map/ppermute | solution.py:538
  248.7 2.0 collective-permute-start.30
  250.7 0.8 constant_dynamic-update-slice_fusion.11
  252.1 10.8 %collective-permute-done.36 = bf16[4224,128]{1,0:T(8,128)(2,1)S(1)} collective-permute-done((bf16[4224,128]{1,0:T(8,128)(2,1)S(1)}, bf16[4224,128]{1,0:T(8,128)(2,1)S(1)}, u32[]{:S(2)}, u32[]{:S(2)}) %collective-permute-start.36) | collective-permute-done | bytes 1081376 | tf_op jit(solution)/shard_map/ppermute | solution.py:538
  262.8 1.1 constant_dynamic-update-slice_fusion.10.first_ref
  263.9 1.7 collective-permute-start.37
  265.6 1.6 collective-permute-start.20
  268.5 0.7 constant_dynamic-update-slice_fusion.1
  269.2 5.6 %collective-permute-done.20 = bf16[2048,128]{1,0:T(8,128)(2,1)S(1)} collective-permute-done((bf16[2048,128]{1,0:T(8,128)(2,1)S(1)}, bf16[2048,128]{1,0:T(8,128)(2,1)S(1)}, u32[]{:S(2)}, u32[]{:S(2)}) %collective-permute-start.20) | collective-permute-done | bytes 524320 | tf_op jit(solution)/shard_map/ppermute | solution.py:538
  274.9 0.8 constant_dynamic-update-slice_fusion.first_ref
  275.7 0.7 slice_bitcast_fusion.1
  276.4 1.6 collective-permute-start.4
  278.3 0.8 slice_bitcast_fusion
  279.2 5.9 %collective-permute-done.4 = bf16[256,512]{1,0:T(8,128)(2,1)} collective-permute-done((bf16[256,512]{1,0:T(8,128)(2,1)}, bf16[256,512]{1,0:T(8,128)(2,1)}, u32[]{:S(2)}, u32[]{:S(2)}) %collective-permute-start.4) | collective-permute-done | bytes 262176 | tf_op jit(solution)/shard_map/ppermute | solution.py:538
  285.1 1.9 maximum_select_fusion
  287.0 3.4 %collective-permute-done.9 = bf16[256,512]{1,0:T(8,128)(2,1)} collective-permute-done((bf16[256,512]{1,0:T(8,128)(2,1)}, bf16[256,512]{1,0:T(8,128)(2,1)}, u32[]{:S(2)}, u32[]{:S(2)}) %collective-permute-start.9) | collective-permute-done | bytes 262176 | tf_op jit(solution)/shard_map/ppermute | solution.py:538
  290.3 2.2 maximum_select_fusion.1
  292.5 6.9 %unpack.5 = (f32[1376,512]{1,0:T(8,128)}, f32[1376,512]{1,0:T(8,128)}, f32[1376,512]{1,0:T(8,128)}) custom-call(s32[3]{0:T(128)S(1)} %copy-done, bf16[8448,128]{1,0:T(8,128)(2,1)} %constant_dynamic-update-slice_fusion.10.first_ref, bf16[8448,128]{1,0:T(8,128)(2,1)} %collective-permute-done.37.second_ref), custom_call_target="tpu_custom_call" | custom-call | bytes 12976128 | tf_op jit(solution)/shard_map/unpack/pallas_call | solution.py:509
  299.5 4.5 %unpack.3 = (f32[512,512]{1,0:T(8,128)}, f32[512,512]{1,0:T(8,128)}, f32[512,512]{1,0:T(8,128)}, f32[512,512]{1,0:T(8,128)}) custom-call(s32[3]{0:T(128)S(1)} %copy-done, bf16[4096,128]{1,0:T(8,128)(2,1)} %constant_dynamic-update-slice_fusion.first_ref, bf16[4096,128]{1,0:T(8,128)(2,1)} %collective-permute-done.21.second_ref), custom_call_target="tpu_custom_call" | custom-call | bytes 6291456 | tf_op jit(solution)/shard_map/unpack/pallas_call | solution.py:509
  304.0 11.1 %unpack.4 = (f32[1376,512]{1,0:T(8,128)}, f32[1376,512]{1,0:T(8,128)}, f32[1376,512]{1,0:T(8,128)}, f32[512,512]{1,0:T(8,128)}, f32[512,512]{1,0:T(8,128)}, /*in...) custom-call(s32[3]{0:T(128)S(1)} %copy-done, ...), custom_call_target="tpu_custom_call" | custom-call | bytes 19267584 | tf_op jit(solution)/shard_map/unpack/pallas_call | solution.py:509
  (111 shorter events, 11.1 us)
Async XLA Ops:
  1.7 9.1 %collective-permute-start = (bf16[256,512]{1,0:T(8,128)(2,1)S(1)}, bf16[256,512]{1,0:T(8,128)(2,1)S(1)}, u32[]{:S(2)}, u32[]{:S(2)}) collective-permute-start(bf16[256,512]{1,0:T(8,128)(2,1)S(1)} %get-tuple-element.159), channel_id=1, source_target_pairs={{0,3},{1,2},{2,1},{3,0},{4,7},{5,6},{6,5},{7,4},{8,11},{9,10},{10,... | collective-permute-start | bytes 786440 | tf_op jit(solution)/shard_map/ppermute | solution.py:538
  10.9 2.9 copy-start.7
  10.9 4.1 %collective-permute-start.1 = (bf16[512,512]{1,0:T(8,128)(2,1)S(1)}, bf16[512,512]{1,0:T(8,128)(2,1)S(1)}, u32[]{:S(2)}, u32[]{:S(2)}) collective-permute-start(bf16[512,512]{1,0:T(8,128)(2,1)S(1)} %pad_maximum_fusion.4.args_0_.args_2_), channel_id=1, source_target_pairs={{0,1},{1,0},{2,3},{3,2},{4,5},{5,4},{6,7},{7,6},{8,9},{9,8},{10,11... | collective-permute-start | bytes 1572872 | tf_op jit(solution)/shard_map/ppermute | solution.py:538
  15.0 0.8 copy-start.9
  15.8 17.9 %copy-start.5 = (bf16[2,256,512]{2,1,0:T(8,128)(2,1)S(1)}, bf16[2,256,512]{2,1,0:T(8,128)(2,1)}, u32[]{:S(2)}) copy-start(bf16[2,256,512]{2,1,0:T(8,128)(2,1)} %param.41) | copy-start | bytes 1572868
  33.6 10.0 %collective-permute-start.2 = (bf16[512,512]{1,0:T(8,128)(2,1)}, bf16[512,512]{1,0:T(8,128)(2,1)S(1)}, u32[]{:S(2)}, u32[]{:S(2)}) collective-permute-start(bf16[512,512]{1,0:T(8,128)(2,1)} %get-tuple-element.83.args_0_.args_2_), channel_id=1, source_target_pairs={{0,1},{1,0},{2,3},{3,2},{4,5},{5,4},{6,7},{7,6},{8,9},{9,8},{10,11... | collective-permute-start | bytes 1572872 | tf_op jit(solution)/shard_map/ppermute | solution.py:538
  33.8 9.0 %collective-permute-start.3 = (bf16[256,512]{1,0:T(8,128)(2,1)S(1)}, bf16[256,512]{1,0:T(8,128)(2,1)S(1)}, u32[]{:S(2)}, u32[]{:S(2)}) collective-permute-start(bf16[256,512]{1,0:T(8,128)(2,1)S(1)} %get-tuple-element.157), channel_id=1, source_target_pairs={{0,3},{1,2},{2,1},{3,0},{4,7},{5,6},{6,5},{7,4},{8,11},{9,10},{10,... | collective-permute-start | bytes 786440 | tf_op jit(solution)/shard_map/ppermute | solution.py:538
  43.6 0.8 copy-start.10
  67.1 22.9 %collective-permute-start.6 = (bf16[8448,128]{1,0:T(8,128)(2,1)}, bf16[8448,128]{1,0:T(8,128)(2,1)S(1)}, u32[]{:S(2)}, u32[]{:S(2)}) collective-permute-start(bf16[8448,128]{1,0:T(8,128)(2,1)} %get-tuple-element.102), channel_id=1, source_target_pairs={{0,1},{1,0},{2,3},{3,2},{4,5},{5,4},{6,7},{7,6},{8,9},{9,8},{10,11... | collective-permute-start | bytes 6488072 | tf_op jit(solution)/shard_map/ppermute | solution.py:538
  67.2 22.8 %copy-start.2 = (bf16[8448,128]{1,0:T(8,128)(2,1)S(1)}, bf16[8448,128]{1,0:T(8,128)(2,1)}, u32[]{:S(2)}) copy-start(bf16[8448,128]{1,0:T(8,128)(2,1)} %get-tuple-element.106) | copy-start | bytes 6488068
  87.9 2.2 collective-permute-start.5
  90.0 0.8 copy-start.11
  90.9 19.4 %collective-permute-start.7 = (bf16[4224,128]{1,0:T(8,128)(2,1)S(1)}, bf16[4224,128]{1,0:T(8,128)(2,1)S(1)}, u32[]{:S(2)}, u32[]{:S(2)}) collective-permute-start(bf16[4224,128]{1,0:T(8,128)(2,1)S(1)} %slice.136), channel_id=1, source_target_pairs={{0,2},{1,5},{2,0},{3,7},{4,6},{5,1},{6,4},{7,3},{8,10},{9,13},{10,... | collective-permute-start | bytes 3244040 | tf_op jit(solution)/shard_map/ppermute | solution.py:538
  110.3 18.6 %collective-permute-start.11 = (bf16[12544,128]{1,0:T(8,128)(2,1)}, bf16[12544,128]{1,0:T(8,128)(2,1)}, u32[]{:S(2)}, u32[]{:S(2)}) collective-permute-start(bf16[12544,128]{1,0:T(8,128)(2,1)} %get-tuple-element.119), channel_id=1, source_target_pairs={{0,1},{1,0},{2,3},{3,2},{4,5},{5,4},{6,7},{7,6},{8,9},{9,8},{10,11... | collective-permute-start | bytes 9633800 | tf_op jit(solution)/shard_map/ppermute | solution.py:538
  110.7 18.2 %collective-permute-start.10 = (bf16[2112,128]{1,0:T(8,128)(2,1)S(1)}, bf16[2112,128]{1,0:T(8,128)(2,1)S(1)}, u32[]{:S(2)}, u32[]{:S(2)}) collective-permute-start(bf16[2112,128]{1,0:T(8,128)(2,1)S(1)} %slice.140), channel_id=1, source_target_pairs={{0,4},{1,3},{2,6},{3,1},{4,0},{5,7},{6,2},{7,5},{8,12},{9,11},{10,... | collective-permute-start | bytes 1622024 | tf_op jit(solution)/shard_map/ppermute | solution.py:538
  112.3 16.6 %copy-start.1 = (bf16[12544,128]{1,0:T(8,128)(2,1)S(1)}, bf16[12544,128]{1,0:T(8,128)(2,1)}, u32[]{:S(2)}) copy-start(bf16[12544,128]{1,0:T(8,128)(2,1)} %get-tuple-element.129) | copy-start | bytes 9633796
  131.4 20.8 %collective-permute-start.22 = (bf16[6272,128]{1,0:T(8,128)(2,1)S(1)}, bf16[6272,128]{1,0:T(8,128)(2,1)S(1)}, u32[]{:S(2)}, u32[]{:S(2)}) collective-permute-start(bf16[6272,128]{1,0:T(8,128)(2,1)S(1)} %slice.150), channel_id=1, source_target_pairs={{0,2},{1,5},{2,0},{3,7},{4,6},{5,1},{6,4},{7,3},{8,10},{9,13},{10,... | collective-permute-start | bytes 4816904 | tf_op jit(solution)/shard_map/ppermute | solution.py:538
  152.7 12.2 %collective-permute-start.23 = (bf16[3136,128]{1,0:T(8,128)(2,1)S(1)}, bf16[3136,128]{1,0:T(8,128)(2,1)S(1)}, u32[]{:S(2)}, u32[]{:S(2)}) collective-permute-start(bf16[3136,128]{1,0:T(8,128)(2,1)S(1)} %slice.152), channel_id=1, source_target_pairs={{0,4},{1,3},{2,6},{3,1},{4,0},{5,7},{6,2},{7,5},{8,12},{9,11},{10,... | collective-permute-start | bytes 2408456 | tf_op jit(solution)/shard_map/ppermute | solution.py:538
  153.4 13.4 %collective-permute-start.31 = (bf16[1056,128]{1,0:T(8,128)(2,1)S(1)}, bf16[1056,128]{1,0:T(8,128)(2,1)S(1)}, u32[]{:S(2)}, u32[]{:S(2)}) collective-permute-start(bf16[1056,128]{1,0:T(8,128)(2,1)S(1)} %slice.159), channel_id=1, source_target_pairs={{0,8},{1,9},{2,10},{3,11},{4,12},{5,13},{6,14},{7,15},{8,0},{9,1},... | collective-permute-start | bytes 811016 | tf_op jit(solution)/shard_map/ppermute | solution.py:538
  161.4 19.1 %collective-permute-start.12 = (bf16[4096,128]{1,0:T(8,128)(2,1)}, bf16[4096,128]{1,0:T(8,128)(2,1)S(1)}, u32[]{:S(2)}, u32[]{:S(2)}) collective-permute-start(bf16[4096,128]{1,0:T(8,128)(2,1)} %get-tuple-element.124), channel_id=1, source_target_pairs={{0,1},{1,0},{2,3},{3,2},{4,5},{5,4},{6,7},{7,6},{8,9},{9,8},{10,11... | collective-permute-start | bytes 3145736 | tf_op jit(solution)/shard_map/ppermute | solution.py:538
  165.1 15.4 %copy-start.3 = (bf16[4096,128]{1,0:T(8,128)(2,1)S(1)}, bf16[4096,128]{1,0:T(8,128)(2,1)}, u32[]{:S(2)}) copy-start(bf16[4096,128]{1,0:T(8,128)(2,1)} %get-tuple-element.123) | copy-start | bytes 3145732
  165.2 15.1 %collective-permute-start.24 = (bf16[1568,128]{1,0:T(8,128)(2,1)S(1)}, bf16[1568,128]{1,0:T(8,128)(2,1)S(1)}, u32[]{:S(2)}, u32[]{:S(2)}) collective-permute-start(bf16[1568,128]{1,0:T(8,128)(2,1)S(1)} %slice.154), channel_id=1, source_target_pairs={{0,8},{1,9},{2,10},{3,11},{4,12},{5,13},{6,14},{7,15},{8,0},{9,1},... | collective-permute-start | bytes 1204232 | tf_op jit(solution)/shard_map/ppermute | solution.py:538
  166.9 9.2 %collective-permute-start.32 = (bf16[528,128]{1,0:T(8,128)(2,1)S(1)}, bf16[528,128]{1,0:T(8,128)(2,1)S(1)}, u32[]{:S(2)}, u32[]{:S(2)}) collective-permute-start(bf16[528,128]{1,0:T(8,128)(2,1)S(1)} %slice.161), channel_id=1, source_target_pairs={{0,16},{1,17},{2,18},{3,19},{4,20},{5,21},{6,22},{7,23},{8,24},{9,... | collective-permute-start | bytes 405512 | tf_op jit(solution)/shard_map/ppermute | solution.py:538
  176.9 16.7 %collective-permute-start.33 = (bf16[528,128]{1,0:T(8,128)(2,1)S(1)}, bf16[528,128]{1,0:T(8,128)(2,1)S(1)}, u32[]{:S(2)}, u32[]{:S(2)}) collective-permute-start(bf16[528,128]{1,0:T(8,128)(2,1)S(1)} %get-tuple-element.147), channel_id=1, source_target_pairs={{0,16},{1,17},{2,18},{3,19},{4,20},{5,21},{6,22},{7,23},{8,24},{9,... | collective-permute-start | bytes 405512 | tf_op jit(solution)/shard_map/ppermute | solution.py:538
  180.4 13.0 %collective-permute-start.25 = (bf16[784,128]{1,0:T(8,128)(2,1)S(1)}, bf16[784,128]{1,0:T(8,128)(2,1)S(1)}, u32[]{:S(2)}, u32[]{:S(2)}) collective-permute-start(bf16[784,128]{1,0:T(8,128)(2,1)S(1)} %slice.156), channel_id=1, source_target_pairs={{0,16},{1,17},{2,18},{3,19},{4,20},{5,21},{6,22},{7,23},{8,24},{9,... | collective-permute-start | bytes 602120 | tf_op jit(solution)/shard_map/ppermute | solution.py:538
  180.8 23.1 %collective-permute-start.13 = (bf16[2048,128]{1,0:T(8,128)(2,1)S(1)}, bf16[2048,128]{1,0:T(8,128)(2,1)S(1)}, u32[]{:S(2)}, u32[]{:S(2)}) collective-permute-start(bf16[2048,128]{1,0:T(8,128)(2,1)S(1)} %slice.142), channel_id=1, source_target_pairs={{0,2},{1,5},{2,0},{3,7},{4,6},{5,1},{6,4},{7,3},{8,10},{9,13},{10,... | collective-permute-start | bytes 1572872 | tf_op jit(solution)/shard_map/ppermute | solution.py:538
  193.5 10.3 %collective-permute-start.26 = (bf16[784,128]{1,0:T(8,128)(2,1)S(1)}, bf16[784,128]{1,0:T(8,128)(2,1)S(1)}, u32[]{:S(2)}, u32[]{:S(2)}) collective-permute-start(bf16[784,128]{1,0:T(8,128)(2,1)S(1)} %get-tuple-element.149), channel_id=1, source_target_pairs={{0,16},{1,17},{2,18},{3,19},{4,20},{5,21},{6,22},{7,23},{8,24},{9,... | collective-permute-start | bytes 602120 | tf_op jit(solution)/shard_map/ppermute | solution.py:538
  193.6 22.0 %collective-permute-start.34 = (bf16[1056,128]{1,0:T(8,128)(2,1)S(1)}, bf16[1056,128]{1,0:T(8,128)(2,1)S(1)}, u32[]{:S(2)}, u32[]{:S(2)}) collective-permute-start(bf16[1056,128]{1,0:T(8,128)(2,1)S(1)} %pad_maximum_fusion.8), channel_id=1, source_target_pairs={{0,8},{1,9},{2,10},{3,11},{4,12},{5,13},{6,14},{7,15},{8,0},{9,1},... | collective-permute-start | bytes 811016 | tf_op jit(solution)/shard_map/ppermute | solution.py:538
  203.8 11.2 %collective-permute-start.27 = (bf16[1568,128]{1,0:T(8,128)(2,1)S(1)}, bf16[1568,128]{1,0:T(8,128)(2,1)S(1)}, u32[]{:S(2)}, u32[]{:S(2)}) collective-permute-start(bf16[1568,128]{1,0:T(8,128)(2,1)S(1)} %pad_maximum_fusion.7), channel_id=1, source_target_pairs={{0,8},{1,9},{2,10},{3,11},{4,12},{5,13},{6,14},{7,15},{8,0},{9,1},... | collective-permute-start | bytes 1204232 | tf_op jit(solution)/shard_map/ppermute | solution.py:538
  204.1 13.2 %collective-permute-start.14 = (bf16[1024,128]{1,0:T(8,128)(2,1)S(1)}, bf16[1024,128]{1,0:T(8,128)(2,1)S(1)}, u32[]{:S(2)}, u32[]{:S(2)}) collective-permute-start(bf16[1024,128]{1,0:T(8,128)(2,1)S(1)} %slice.144), channel_id=1, source_target_pairs={{0,4},{1,3},{2,6},{3,1},{4,0},{5,7},{6,2},{7,5},{8,12},{9,11},{10,... | collective-permute-start | bytes 786440 | tf_op jit(solution)/shard_map/ppermute | solution.py:538
  215.1 12.2 %collective-permute-start.28 = (bf16[3136,128]{1,0:T(8,128)(2,1)S(1)}, bf16[3136,128]{1,0:T(8,128)(2,1)S(1)}, u32[]{:S(2)}, u32[]{:S(2)}) collective-permute-start(bf16[3136,128]{1,0:T(8,128)(2,1)S(1)} %pad_maximum_fusion.2), channel_id=1, source_target_pairs={{0,4},{1,3},{2,6},{3,1},{4,0},{5,7},{6,2},{7,5},{8,12},{9,11},{10,... | collective-permute-start | bytes 2408456 | tf_op jit(solution)/shard_map/ppermute | solution.py:538
  215.6 22.2 %collective-permute-start.35 = (bf16[2112,128]{1,0:T(8,128)(2,1)S(1)}, bf16[2112,128]{1,0:T(8,128)(2,1)S(1)}, u32[]{:S(2)}, u32[]{:S(2)}) collective-permute-start(bf16[2112,128]{1,0:T(8,128)(2,1)S(1)} %pad_maximum_fusion.3), channel_id=1, source_target_pairs={{0,4},{1,3},{2,6},{3,1},{4,0},{5,7},{6,2},{7,5},{8,12},{9,11},{10,... | collective-permute-start | bytes 1622024 | tf_op jit(solution)/shard_map/ppermute | solution.py:538
  217.4 5.0 %collective-permute-start.15 = (bf16[512,128]{1,0:T(8,128)(2,1)S(1)}, bf16[512,128]{1,0:T(8,128)(2,1)S(1)}, u32[]{:S(2)}, u32[]{:S(2)}) collective-permute-start(bf16[512,128]{1,0:T(8,128)(2,1)S(1)} %slice.146), channel_id=1, source_target_pairs={{0,8},{1,9},{2,10},{3,11},{4,12},{5,13},{6,14},{7,15},{8,0},{9,1},... | collective-permute-start | bytes 393224 | tf_op jit(solution)/shard_map/ppermute | solution.py:538
  222.5 6.6 %collective-permute-start.16 = (bf16[256,128]{1,0:T(8,128)(2,1)S(1)}, bf16[256,128]{1,0:T(8,128)(2,1)S(1)}, u32[]{:S(2)}, u32[]{:S(2)}) collective-permute-start(bf16[256,128]{1,0:T(8,128)(2,1)S(1)} %slice.148), channel_id=1, source_target_pairs={{0,16},{1,17},{2,18},{3,19},{4,20},{5,21},{6,22},{7,23},{8,24},{9,... | collective-permute-start | bytes 196616 | tf_op jit(solution)/shard_map/ppermute | solution.py:538
  227.4 21.0 %collective-permute-start.29 = (bf16[6272,128]{1,0:T(8,128)(2,1)S(1)}, bf16[6272,128]{1,0:T(8,128)(2,1)S(1)}, u32[]{:S(2)}, u32[]{:S(2)}) collective-permute-start(bf16[6272,128]{1,0:T(8,128)(2,1)S(1)} %pad_maximum_fusion), channel_id=1, source_target_pairs={{0,2},{1,5},{2,0},{3,7},{4,6},{5,1},{6,4},{7,3},{8,10},{9,13},{10,... | collective-permute-start | bytes 4816904 | tf_op jit(solution)/shard_map/ppermute | solution.py:538
  229.7 10.0 %collective-permute-start.17 = (bf16[256,128]{1,0:T(8,128)(2,1)S(1)}, bf16[256,128]{1,0:T(8,128)(2,1)S(1)}, u32[]{:S(2)}, u32[]{:S(2)}) collective-permute-start(bf16[256,128]{1,0:T(8,128)(2,1)S(1)} %get-tuple-element.151), channel_id=1, source_target_pairs={{0,16},{1,17},{2,18},{3,19},{4,20},{5,21},{6,22},{7,23},{8,24},{9,... | collective-permute-start | bytes 196616 | tf_op jit(solution)/shard_map/ppermute | solution.py:538
  237.9 24.9 %collective-permute-start.36 = (bf16[4224,128]{1,0:T(8,128)(2,1)S(1)}, bf16[4224,128]{1,0:T(8,128)(2,1)S(1)}, u32[]{:S(2)}, u32[]{:S(2)}) collective-permute-start(bf16[4224,128]{1,0:T(8,128)(2,1)S(1)} %pad_maximum_fusion.1), channel_id=1, source_target_pairs={{0,2},{1,5},{2,0},{3,7},{4,6},{5,1},{6,4},{7,3},{8,10},{9,13},{10,... | collective-permute-start | bytes 3244040 | tf_op jit(solution)/shard_map/ppermute | solution.py:538
  239.7 11.9 %collective-permute-start.18 = (bf16[512,128]{1,0:T(8,128)(2,1)S(1)}, bf16[512,128]{1,0:T(8,128)(2,1)S(1)}, u32[]{:S(2)}, u32[]{:S(2)}) collective-permute-start(bf16[512,128]{1,0:T(8,128)(2,1)S(1)} %pad_maximum_fusion.11), channel_id=1, source_target_pairs={{0,8},{1,9},{2,10},{3,11},{4,12},{5,13},{6,14},{7,15},{8,0},{9,1},... | collective-permute-start | bytes 393224 | tf_op jit(solution)/shard_map/ppermute | solution.py:538
  248.7 18.6 %copy-start.8 = (bf16[512,512]{1,0:T(8,128)(2,1)S(1)}, bf16[512,512]{1,0:T(8,128)(2,1)}, u32[]{:S(2)}) copy-start(bf16[512,512]{1,0:T(8,128)(2,1)} %get-tuple-element.115) | copy-start | bytes 1572868
  248.7 55.3 %collective-permute-start.30 = (bf16[12544,128]{1,0:T(8,128)(2,1)S(1)}, bf16[12544,128]{1,0:T(8,128)(2,1)}, u32[]{:S(2)}, u32[]{:S(2)}) collective-permute-start(bf16[12544,128]{1,0:T(8,128)(2,1)S(1)} %constant_dynamic-update-slice_fusion.5.first_ref), channel_id=1, source_target_pairs={{0,1},{1,0},{2,3},{3,2},{4,5},{5,4},{6,7},{7,6},{8,9},{9,8},{10,11... | collective-permute-start | bytes 9633800 | tf_op jit(solution)/shard_map/ppermute | solution.py:538
  251.6 24.1 %copy-start.6 = (bf16[512,512]{1,0:T(8,128)(2,1)S(1)}, bf16[512,512]{1,0:T(8,128)(2,1)}, u32[]{:S(2)}) copy-start(bf16[512,512]{1,0:T(8,128)(2,1)} %get-tuple-element.85) | copy-start | bytes 1572868
  251.6 14.0 %collective-permute-start.19 = (bf16[1024,128]{1,0:T(8,128)(2,1)S(1)}, bf16[1024,128]{1,0:T(8,128)(2,1)S(1)}, u32[]{:S(2)}, u32[]{:S(2)}) collective-permute-start(bf16[1024,128]{1,0:T(8,128)(2,1)S(1)} %pad_maximum_fusion.10), channel_id=1, source_target_pairs={{0,4},{1,3},{2,6},{3,1},{4,0},{5,7},{6,2},{7,5},{8,12},{9,11},{10,... | collective-permute-start | bytes 786440 | tf_op jit(solution)/shard_map/ppermute | solution.py:538
  263.9 14.2 %copy-start.4 = (f32[512,512]{1,0:T(8,128)S(1)}, f32[512,512]{1,0:T(8,128)}, u32[]{:S(2)}) copy-start(f32[512,512]{1,0:T(8,128)} %get-tuple-element.114) | copy-start | bytes 3145732
  263.9 28.6 %collective-permute-start.37 = (bf16[8448,128]{1,0:T(8,128)(2,1)}, bf16[8448,128]{1,0:T(8,128)(2,1)}, u32[]{:S(2)}, u32[]{:S(2)}) collective-permute-start(bf16[8448,128]{1,0:T(8,128)(2,1)} %constant_dynamic-update-slice_fusion.10.first_ref), channel_id=1, source_target_pairs={{0,1},{1,0},{2,3},{3,2},{4,5},{5,4},{6,7},{7,6},{8,9},{9,8},{10,11... | collective-permute-start | bytes 6488072 | tf_op jit(solution)/shard_map/ppermute | solution.py:538
  265.6 9.2 %collective-permute-start.20 = (bf16[2048,128]{1,0:T(8,128)(2,1)S(1)}, bf16[2048,128]{1,0:T(8,128)(2,1)S(1)}, u32[]{:S(2)}, u32[]{:S(2)}) collective-permute-start(bf16[2048,128]{1,0:T(8,128)(2,1)S(1)} %pad_maximum_fusion.6), channel_id=1, source_target_pairs={{0,2},{1,5},{2,0},{3,7},{4,6},{5,1},{6,4},{7,3},{8,10},{9,13},{10,... | collective-permute-start | bytes 1572872 | tf_op jit(solution)/shard_map/ppermute | solution.py:538
  267.2 10.9 %collective-permute-start.8 = (bf16[512,512]{1,0:T(8,128)(2,1)S(1)}, bf16[512,512]{1,0:T(8,128)(2,1)S(1)}, u32[]{:S(2)}, u32[]{:S(2)}) collective-permute-start(bf16[512,512]{1,0:T(8,128)(2,1)S(1)} %copy-done.8), channel_id=1, source_target_pairs={{0,1},{1,0},{2,3},{3,2},{4,5},{5,4},{6,7},{7,6},{8,9},{9,8},{10,11... | collective-permute-start | bytes 1572872 | tf_op jit(solution)/shard_map/ppermute | solution.py:538
  275.7 23.8 %collective-permute-start.21 = (bf16[4096,128]{1,0:T(8,128)(2,1)}, bf16[4096,128]{1,0:T(8,128)(2,1)}, u32[]{:S(2)}, u32[]{:S(2)}) collective-permute-start(bf16[4096,128]{1,0:T(8,128)(2,1)} %constant_dynamic-update-slice_fusion.first_ref), channel_id=1, source_target_pairs={{0,1},{1,0},{2,3},{3,2},{4,5},{5,4},{6,7},{7,6},{8,9},{9,8},{10,11... | collective-permute-start | bytes 3145736 | tf_op jit(solution)/shard_map/ppermute | solution.py:538
  276.4 8.6 %collective-permute-start.4 = (bf16[256,512]{1,0:T(8,128)(2,1)}, bf16[256,512]{1,0:T(8,128)(2,1)}, u32[]{:S(2)}, u32[]{:S(2)}) collective-permute-start(bf16[256,512]{1,0:T(8,128)(2,1)} %get-tuple-element.155), channel_id=1, source_target_pairs={{0,3},{1,2},{2,1},{3,0},{4,7},{5,6},{6,5},{7,4},{8,11},{9,10},{10,... | collective-permute-start | bytes 786440 | tf_op jit(solution)/shard_map/ppermute | solution.py:538
  278.1 14.4 %copy-start = (s32[3]{0:T(128)S(1)}, s32[3]{0:T(128)}, u32[]{:S(2)}) copy-start(s32[3]{0:T(128)} %pad_add_fusion.scalars_ref) | copy-start | bytes 40
  279.1 11.3 %collective-permute-start.9 = (bf16[256,512]{1,0:T(8,128)(2,1)}, bf16[256,512]{1,0:T(8,128)(2,1)}, u32[]{:S(2)}, u32[]{:S(2)}) collective-permute-start(bf16[256,512]{1,0:T(8,128)(2,1)} %get-tuple-element.153), channel_id=1, source_target_pairs={{0,3},{1,2},{2,1},{3,0},{4,7},{5,6},{6,5},{7,4},{8,11},{9,10},{10,... | collective-permute-start | bytes 786440 | tf_op jit(solution)/shard_map/ppermute | solution.py:538

commit v3 on v2

v3 whole, which is shorter than its diff:
```python
import jax
import jax.numpy as jnp
import numpy as np
from jax import lax
from jax.experimental import pallas as pl
from jax.experimental.pallas import tpu as pltpu
from jax.sharding import PartitionSpec as P

D = 512
HEADS = 8
HD = 64
FF = 1376
SEQ = 1024
EPS = 1e-06
NEG = -1000000000.0
AXES = ("dp", "sp")
BF = jnp.bfloat16
F32 = jnp.float32
LANES = 128
PANELS = D // LANES
BLK = SEQ // 4
ROWS = 2 * BLK
HALF = D // 2
SCALE = HD ** (-0.5)
FFN_ROWS = 3 * PANELS * FF
ATTN_ROWS = 4 * PANELS * D
GAIN_ROWS = 16
VMEM_LIMIT = 28 << 20


def dot(left, right):
    return lax.dot_general(left, right, (((1,), (0,)), ((), ())), preferred_element_type=F32)


def dot_nt(left, right):
    return lax.dot_general(left, right, (((1,), (1,)), ((), ())), preferred_element_type=F32)


def dot_tn(left, right):
    return lax.dot_general(left, right, (((0,), (0,)), ((), ())), preferred_element_type=F32)


def inv_rms(values):
    return lax.rsqrt(jnp.mean(values * values, axis=-1, keepdims=True) + EPS)


def rms_back(values, gain, upstream):
    scale = inv_rms(values)
    weighted = upstream * gain
    grad = scale * weighted - values * (
        scale * scale * scale * jnp.mean(weighted * values, axis=-1, keepdims=True)
    )
    grad_gain = jnp.sum(upstream * (values * scale), axis=0, keepdims=True)
    return grad, grad_gain


class Refs:
    def __init__(self, vmem, fetched, stored, sems):
        self.vmem, self.stored, self.sems = vmem, stored, sems
        self.waiting, self.sent = {}, []
        for name in fetched:
            copy = pltpu.make_async_copy(fetched[name], vmem[name], self.next_sem())
            copy.start()
            self.waiting[name] = copy

    used = 0

    def next_sem(self):
        self.used += 1
        return self.sems.at[self.used - 1]

    def __getattr__(self, name):
        if name in self.waiting:
            self.waiting.pop(name).wait()
        return self.vmem[name]

    def send(self, *refs):
        for ref in refs:
            for name in self.stored:
                if self.vmem[name] is ref:
                    copy = pltpu.make_async_copy(ref, self.stored[name], self.next_sem())
                    copy.start()
                    self.sent.append(copy)

    def finish(self):
        for name in list(self.waiting):
            self.waiting.pop(name).wait()
        for copy in self.sent:
            copy.wait()


def in_hbm(array):
    return pltpu.with_memory_space_constraint(array, pltpu.HBM)


def run_kernel(body, scalars, fetched, ins, outs, stored, scratch):
    names = list(ins) + list(outs) + list(fetched) + list(stored) + list(scratch)
    n_f, n_in, n_out, n_st = len(fetched), len(ins), len(outs), len(stored)
    shapes = [pltpu.VMEM(fetched[n].shape, fetched[n].dtype) for n in fetched]
    shapes += [pltpu.VMEM(*stored[n]) for n in stored]
    shapes += [pltpu.VMEM(*scratch[n]) for n in scratch]

    def kernel(scalars_ref, *args):
        head = n_f + n_in + n_out
        hbm_in, on_chip, hbm_out = args[:n_f], args[n_f:head], args[head : head + n_st]
        vmem = dict(zip(names, on_chip + args[head + n_st : -1]))
        refs = Refs(vmem, dict(zip(fetched, hbm_in)), dict(zip(stored, hbm_out)), args[-1])
        body(refs, scalars_ref)
        refs.finish()

    on_chip, off_chip = (pl.BlockSpec(memory_space=m) for m in (pltpu.VMEM, pltpu.HBM))
    made = pl.pallas_call(
        kernel,
        name=body.__name__,
        out_shape=[jax.ShapeDtypeStruct(*t[n]) for t in (outs, stored) for n in t],
        grid_spec=pltpu.PrefetchScalarGridSpec(
            num_scalar_prefetch=1,
            grid=(),
            in_specs=[off_chip] * n_f + [on_chip] * n_in,
            out_specs=[on_chip] * n_out + [off_chip] * n_st,
            scratch_shapes=shapes + [pltpu.SemaphoreType.DMA((max(n_f + n_st, 1),))],
        ),
        compiler_params=pltpu.CompilerParams(vmem_limit_bytes=VMEM_LIMIT),
        cost_estimate=pl.CostEstimate(flops=0, transcendentals=0, bytes_accessed=1),
    )(scalars, *[in_hbm(a) for a in fetched.values()], *ins.values())
    return list(made[:n_out]) + [in_hbm(a) for a in made[n_out:]]


def piece_position(j, me, order):
    where = 0
    for bit in order:
        where = where * 2 + (((me >> bit) & 1) ^ ((j >> bit) & 1))
    return where


def segments(pieces, start, end):
    rows = pieces[2]
    while start < end:
        stop = min(end, (start // rows + 1) * rows)
        yield start // rows, start % rows, start, stop - start
        start = stop


def put_rows(refs, pieces, start, block):
    orders, count, rows = pieces
    me = refs.me
    for j, inside, at, length in segments(pieces, start, start + block.shape[0]):
        spot = piece_position(j, me, orders[j & 1]) + ((me ^ j) & 1) * (count // 2)
        put = pl.ds(pl.multiple_of(spot * rows + inside, 16), length)
        refs.grads[put, :] = block[at - start : at - start + length, :]


def head_lanes(rows, which):
    lane = lax.broadcasted_iota(jnp.int32, (rows, LANES), 1)
    return (lane < HD) if which == 0 else (lane >= HD)


def only_head(panel, which):
    return jnp.where(head_lanes(panel.shape[0], which), panel, jnp.zeros_like(panel))


def turned(panel):
    lane = lax.broadcasted_iota(jnp.int32, panel.shape, 1)
    return jnp.where(
        lane % HD < HD // 2,
        pltpu.roll(panel, LANES - HD // 2, 1),
        pltpu.roll(panel, HD // 2, 1),
    )


def block_rows(index):
    return pl.ds(pl.multiple_of(index * BLK, BLK), BLK)


def rope_tables():
    lane = np.arange(LANES)
    inverse = np.float32(10000.0) ** (-np.arange(HD // 2, dtype=np.float32) * np.float32(2.0 / HD))
    places = np.concatenate([np.arange(BLK), np.arange(8) * BLK]).astype(np.float32)
    angles = (places[:, None] * inverse[None, :])[:, lane % (HD // 2)].astype(np.float64)
    sign = np.where(lane % HD < HD // 2, -1.0, 1.0)
    return np.cos(angles).astype(np.float32), (np.sin(angles) * sign).astype(np.float32)


def rope_of(refs, block):
    cosine, sine = refs.cosine[0:BLK, :], refs.sine[0:BLK, :]
    start = pl.ds(BLK + block, 1)
    start_cos, start_sin = refs.cosine[start, :], refs.sine[start, :]
    return cosine * start_cos - sine * start_sin, sine * start_cos + cosine * start_sin


def panel_cols(panel):
    return slice(panel * LANES, (panel + 1) * LANES)


def blocks_of(sp):
    return sp, 3 - sp


def project_heads(refs, sp, entry, own):
    for half, block in enumerate(blocks_of(sp)):
        here = slice(half * BLK, (half + 1) * BLK)
        there = block_rows(block)
        rows = entry[here, :]
        keys = dot(rows, refs.w_key[...])
        refs.v[there, :] = dot(rows, refs.w_value[...]).astype(BF)
        if own:
            queries = dot(rows, refs.w_query[...])
        cosine, sine = rope_of(refs, block)
        for panel in range(PANELS):
            cols = panel_cols(panel)
            part = keys[:, cols]
            refs.k[there, cols] = (part * cosine + turned(part) * sine).astype(BF)
            if own:
                part = queries[:, cols]
                refs.q[here, cols] = (part * cosine + turned(part) * sine).astype(BF) * SCALE


def query_blocks(sp, low):
    chip = sp >> 1
    return (block_rows(chip), low + 1), (block_rows(1 - chip), 4 - low)


def both_ways(sp, step):
    low = (sp & 1) ^ (sp >> 1)

    @pl.when(low == 0)
    def outer():
        step(0)

    @pl.when(low == 1)
    def inner():
        step(1)


def attend(refs, scalars, low):
    sp, length = scalars[1], scalars[2]
    lane = lax.broadcasted_iota(jnp.int32, (BLK, LANES), 1)

    def panel_step(panel, carry):
        cols = pl.ds(pl.multiple_of(panel * LANES, LANES), LANES)
        for rows, blocks in query_blocks(sp, low):
            seen = blocks * BLK
            queries = refs.q[rows, cols]
            outs, logs = [], []
            for which in range(2):
                scores = dot_nt(only_head(queries, which), refs.k[0:seen, cols])
                key_at = lax.broadcasted_iota(jnp.int32, (BLK, seen), 1)
                row_at = lax.broadcasted_iota(jnp.int32, (BLK, seen), 0) + (blocks - 1) * BLK
                scores = jnp.where((key_at <= row_at) & (key_at < length), scores, NEG)
                top = jnp.max(scores, axis=-1, keepdims=True)
                weights = jnp.exp(scores - top)
                total = jnp.sum(weights, axis=-1, keepdims=True)
                outs.append(dot(weights.astype(BF), refs.v[0:seen, cols]) / total)
                logs.append(top + jnp.log(total))
            refs.mixed[rows, cols] = jnp.where(head_lanes(BLK, 0), outs[0], outs[1]).astype(BF)
            kept = jnp.where(lane == 2 * panel, logs[0], refs.lse[rows, :])
            refs.lse[rows, :] = jnp.where(lane == 2 * panel + 1, logs[1], kept)
        return carry

    lax.fori_loop(0, PANELS, panel_step, 0)


def attention_forward(refs, scalars):
    sp = scalars[1]
    project_heads(refs, sp, refs.own, True)
    project_heads(refs, sp ^ 1, refs.sib, False)
    refs.send(refs.q, refs.k, refs.v)
    refs.lse[...] = jnp.zeros((ROWS, LANES), F32)
    both_ways(sp, lambda low: attend(refs, scalars, low))
    refs.send(refs.lse, refs.mixed)


def ffn_forward(refs, ffn_in):
    for half in range(2):
        rows = slice(half * BLK, (half + 1) * BLK)
        gate = dot_nt(ffn_in[rows, :], refs.w_gate[...])
        up = dot_nt(ffn_in[rows, :], refs.w_up[...])
        refs.gate[rows, :] = gate
        refs.up[rows, :] = up
        refs.hidden[rows, :] = (gate * jax.nn.sigmoid(gate) * up).astype(BF)


def store_panels(refs, at, grad):
    height, width = grad.shape
    for panel in range(width // LANES):
        block = grad[:, panel_cols(panel)].astype(BF)
        put_rows(refs, refs.pieces, at + panel * height, block)


def ffn_weight_grads(refs, at, ffn_in, grad_result):
    grad_down = grad_result.astype(BF)
    store_panels(refs, at, dot_tn(refs.hidden[...], grad_down))
    for half in range(2):
        rows = slice(half * BLK, (half + 1) * BLK)
        grad_hidden = dot_nt(grad_down[rows, :], refs.w_down[...])
        gate = refs.gate[rows, :]
        sigma = jax.nn.sigmoid(gate)
        grad_gate = grad_hidden * refs.up[rows, :] * (sigma * (1.0 + gate * (1.0 - sigma)))
        refs.dgate[rows, :] = grad_gate.astype(BF)
        refs.dup[rows, :] = (grad_hidden * (gate * sigma)).astype(BF)
    store_panels(refs, at + PANELS * FF, dot_tn(refs.dgate[...], ffn_in))
    store_panels(refs, at + 2 * PANELS * FF, dot_tn(refs.dup[...], ffn_in))


def ffn_input_grad(refs):
    return dot(refs.dgate[...], refs.w_gate[...]) + dot(refs.dup[...], refs.w_up[...])


def store_tail(refs, gains):
    end = refs.grads.shape[0]
    row = lax.broadcasted_iota(jnp.int32, (end - FFN_ROWS, LANES), 0)
    block = jnp.zeros((end - FFN_ROWS, LANES), F32)
    for slot, gain in enumerate(gains):
        for panel in range(PANELS):
            block = jnp.where(row == PANELS * slot + panel, gain[:, panel_cols(panel)], block)
    put_rows(refs, refs.pieces, FFN_ROWS, block.astype(BF))


def post_forward(refs, scalars):
    attention_forward(refs, scalars)
    middle = refs.own[...].astype(F32) + dot(refs.mixed[...], refs.w_out[...])
    refs.middle[...] = middle
    refs.send(refs.middle)
    state = middle * inv_rms(middle) * refs.attn_gain[...]
    ffn_forward(refs, state.astype(BF))
    result = state + dot(refs.hidden[...], refs.w_down[...])
    refs.result[...] = result
    refs.send(refs.result)
    output = result * inv_rms(result) * refs.ffn_gain[...]
    entry = output * inv_rms(output) * refs.next_gain[...]
    refs.entry[...] = entry.astype(BF)


def masked_cotangent(refs, scalars):
    sp, length = scalars[1], scalars[2]
    row = lax.broadcasted_iota(jnp.int32, (ROWS, D), 0)
    position = row + jnp.where(row < BLK, sp * BLK, (2 - sp) * BLK)
    return jnp.where(position < length, refs.cotangent[...].astype(F32), 0.0)


def pre_ffn_forward(refs, scalars):
    store_tail(refs, ())
    result = refs.result[...]
    inputs = result * inv_rms(result) * refs.last_gain[...]
    middle = inputs + dot(refs.mixed[...], refs.w_out[...])
    refs.middle[...] = middle
    ffn_in = (middle * inv_rms(middle) * refs.ffn_gain[...]).astype(BF)
    ffn_forward(refs, ffn_in)
    output = middle + dot(refs.hidden[...], refs.w_down[...])
    refs.output[...] = output.astype(BF)
    ffn_weight_grads(refs, 0, ffn_in, masked_cotangent(refs, scalars))


def attend_back(refs, scalars, low, first_panel):
    sp, length = scalars[1], scalars[2]
    if low == 1:
        refs.dk[3 * BLK :, :] = jnp.zeros((BLK, HALF), F32)
        refs.dv[3 * BLK :, :] = jnp.zeros((BLK, HALF), F32)

    def panel_step(panel, carry):
        cols = pl.ds(pl.multiple_of((first_panel + panel) * LANES, LANES), LANES)
        put = pl.ds(pl.multiple_of(panel * LANES, LANES), LANES)
        for rows, blocks in reversed(query_blocks(sp, low)):
            seen = blocks * BLK
            queries = refs.q[rows, cols]
            grads = refs.gmix[rows, cols]
            keys = refs.k[0:seen, cols]
            values = refs.v[0:seen, cols]
            key_at = lax.broadcasted_iota(jnp.int32, (seen, BLK), 0)
            row_at = lax.broadcasted_iota(jnp.int32, (seen, BLK), 1) + (blocks - 1) * BLK
            allowed = (key_at <= row_at) & (key_at < length)
            grad_q = jnp.zeros((BLK, LANES), F32)
            grad_k = jnp.zeros((seen, LANES), F32)
            grad_v = jnp.zeros((seen, LANES), F32)
            for which in range(2):
                q_head = only_head(queries, which)
                g_head = only_head(grads, which)
                at = pl.ds(2 * (first_panel + panel) + which, 1)
                scores = jnp.where(allowed, dot_nt(keys, q_head), NEG)
                probs = jnp.exp(scores - refs.lse_t[at, rows])
                grad_p = dot_nt(values, g_head)
                grad_s = (probs * (grad_p - refs.delta_t[at, rows])).astype(BF)
                grad_v = grad_v + dot(probs.astype(BF), g_head)
                grad_k = grad_k + dot(grad_s, q_head)
                grad_q = grad_q + dot_tn(grad_s, only_head(keys, which))
            refs.dq[rows, put] = grad_q * SCALE
            if blocks == 4 - low:
                refs.dk[0:seen, put] = grad_k
                refs.dv[0:seen, put] = grad_v
            else:
                refs.dk[0:seen, put] += grad_k
                refs.dv[0:seen, put] += grad_v
        return carry

    lax.fori_loop(0, PANELS // 2, panel_step, 0)


def start_attention_backward(refs, grad_middle):
    grad_mixed = dot_nt(grad_middle.astype(BF), refs.w_out[...]).astype(BF)
    refs.gmix[...] = grad_mixed
    product = grad_mixed.astype(F32) * refs.mixed[...].astype(F32)
    high = product.astype(BF)
    rest = (product - high.astype(F32)).astype(BF)
    head_of = lax.broadcasted_iota(jnp.int32, (HEADS, D), 1) // HD
    pick = (head_of == lax.broadcasted_iota(jnp.int32, (HEADS, D), 0)).astype(F32).astype(BF)
    refs.delta_t[...] = dot_nt(pick, high) + dot_nt(pick, rest)
    refs.lse_t[...] = jnp.transpose(refs.lse[...])[0:HEADS, :]


def attention_backward(refs, scalars, first_panel):
    sp = scalars[1]
    refs.q, refs.k, refs.v
    both_ways(sp, lambda low: attend_back(refs, scalars, low, first_panel))

    for spot, block in enumerate(blocks_of(sp) + blocks_of(sp ^ 1)):
        put, there = slice(spot * BLK, (spot + 1) * BLK), block_rows(block)
        refs.dvp[put, :] = refs.dv[there, :].astype(BF)
        cosine, sine = rope_of(refs, block)
        for panel in range(PANELS // 2):
            cols = panel_cols(panel)
            part = refs.dk[there, cols]
            refs.dkp[put, cols] = (part * cosine - turned(part) * sine).astype(BF)
            if spot < 2:
                part = refs.dq[put, cols]
                refs.dqp[put, cols] = (part * cosine - turned(part) * sine).astype(BF)
    cols = slice(first_panel * LANES, first_panel * LANES + HALF)
    w_query, w_key, w_value = refs.w_query[:, cols], refs.w_key[:, cols], refs.w_value[:, cols]
    mine, theirs = slice(0, ROWS), slice(ROWS, 2 * ROWS)
    ge_sib = dot_nt(refs.dkp[theirs, :], w_key) + dot_nt(refs.dvp[theirs, :], w_value)
    ge_own = (
        dot_nt(refs.dqp[...], w_query)
        + dot_nt(refs.dkp[mine, :], w_key)
        + dot_nt(refs.dvp[mine, :], w_value)
    )
    return ge_own, ge_sib


def first_heads_backward(refs, scalars):
    refs.ge_own[...], refs.ge_sib[...] = attention_backward(refs, scalars, 0)


def last_heads_backward(refs, scalars):
    ge_own, ge_sib = attention_backward(refs, scalars, PANELS // 2)
    refs.ge_own[...] = refs.part_own[...] + ge_own
    refs.ge_sib[...] = (refs.part_sib[...] + ge_sib).astype(BF)


def pre_middle_backward(refs, scalars):
    grad_normed, grad_gain = rms_back(refs.middle[...], refs.ffn_gain[...], ffn_input_grad(refs))
    grad_middle = masked_cotangent(refs, scalars) + grad_normed
    refs.grad_middle[...] = grad_middle
    refs.grad_gain[...] = grad_gain
    start_attention_backward(refs, grad_middle)


def attention_weight_grads(refs, scalars):
    step = PANELS * D
    store_panels(refs, 0, dot_tn(refs.mixed[...], refs.grad_middle[...].astype(BF)))
    own, sib = refs.own[...], refs.sib[...]
    for half in range(2):
        put = half * step // 2
        dqp, dkp, dvp = ((refs.dqa, refs.dka, refs.dva), (refs.dqb, refs.dkb, refs.dvb))[half]
        store_panels(refs, step + put, dot_tn(own, dqp[...]))
        for k, ref in enumerate((dkp, dvp)):
            total = dot_tn(own, ref[0:ROWS, :]) + dot_tn(sib, ref[ROWS : 2 * ROWS, :])
            store_panels(refs, (k + 2) * step + put, total)


def post_ffn_again(refs, scalars):
    middle = refs.middle[...]
    ffn_in = (middle * inv_rms(middle) * refs.attn_gain[...]).astype(BF)
    refs.ffn_in[...] = ffn_in
    ffn_forward(refs, ffn_in)


def post_ffn_backward(refs, scalars):
    middle, result = refs.middle[...], refs.result[...]
    out_gain = refs.ffn_gain[...]
    inputs = result * inv_rms(result) * out_gain
    grad_entry = refs.ge_own[...] + refs.ge_recv[...].astype(F32)
    grad_normed, grad_next = rms_back(inputs, refs.next_gain[...], grad_entry)
    grad_result, grad_ffn_gain = rms_back(result, out_gain, refs.grad_middle[...] + grad_normed)
    ffn_weight_grads(refs, 0, refs.ffn_in[...], grad_result)
    upstream = grad_result + ffn_input_grad(refs)
    grad_middle, grad_attn_gain = rms_back(middle, refs.attn_gain[...], upstream)
    refs.new_middle[...] = grad_middle
    store_tail(refs, (refs.grad_gain[...], grad_next, grad_ffn_gain, grad_attn_gain))
    start_attention_backward(refs, grad_middle)


def unpack(mine, other, scalars, pieces, heights, gains):
    orders, count, rows = pieces
    shapes = [(height, D) for height in heights] + [(PANELS, LANES)] * gains
    n_out = len(shapes)

    def unpack(scalars_ref, mine_ref, other_ref, *rest):
        outs, staged, sems = rest[:n_out], rest[n_out : 2 * n_out], rest[-1]
        me = scalars_ref[0]

        def lay_out(halves):
            sent, at = [], 0
            for k in range(n_out):
                height, width = shapes[k]
                if k < len(heights):
                    for panel in range(PANELS):
                        for j, inside, row, length in segments(pieces, at, at + height):
                            spot = piece_position(j, me, orders[j & 1]) * rows + inside
                            take = pl.ds(pl.multiple_of(spot, 16), length)
                            put = slice(row - at, row - at + length)
                            staged[k][put, panel_cols(panel)] = halves[j & 1][take, :].astype(F32)
                        at += height
                else:
                    if k == len(heights):
                        ((j, inside, row, length),) = segments(pieces, at, at + GAIN_ROWS)
                        spot = piece_position(j, me, orders[j & 1]) * rows + inside
                        take = pl.ds(pl.multiple_of(spot, 16), GAIN_ROWS)
                        block = halves[j & 1][take, :].astype(F32)
                    slot = (k - len(heights)) * PANELS
                    staged[k][...] = block[slot : slot + PANELS, :]
                sent.append(pltpu.make_async_copy(staged[k], outs[k], sems.at[k]))
                sent[-1].start()
            for copy in sent:
                copy.wait()

        @pl.when(me & 1 == 0)
        def even():
            lay_out((mine_ref, other_ref))

        @pl.when(me & 1 == 1)
        def odd():
            lay_out((other_ref, mine_ref))

    on_chip, off_chip = (pl.BlockSpec(memory_space=m) for m in (pltpu.VMEM, pltpu.HBM))
    return pl.pallas_call(
        unpack,
        name=unpack.__name__,
        out_shape=[jax.ShapeDtypeStruct(shape, F32) for shape in shapes],
        grid_spec=pltpu.PrefetchScalarGridSpec(
            num_scalar_prefetch=1,
            grid=(),
            in_specs=[on_chip] * 2,
            out_specs=[off_chip] * n_out,
            scratch_shapes=[pltpu.VMEM(shape, F32) for shape in shapes]
            + [pltpu.SemaphoreType.DMA((n_out,))],
        ),
        compiler_params=pltpu.CompilerParams(vmem_limit_bytes=VMEM_LIMIT),
        cost_estimate=pl.CostEstimate(flops=0, transcendentals=0, bytes_accessed=1),
    )(scalars, mine, other)


def solution(mesh):
    n_dp, n_sp = mesh.shape["dp"], mesh.shape["sp"]
    count = n_dp * n_sp
    if n_sp != 4 or n_dp & (n_dp - 1) or n_dp < 2:
        raise ValueError
    bits = count.bit_length() - 1

    def swap(array, move):
        return lax.ppermute(array, AXES, [(k, move(k)) for k in range(count)])

    def sibling(array):
        return swap(array, lambda k: k ^ 1)

    tail = list(range(3, bits))
    orders = ([1, 2] + tail, [2, 1] + tail)

    def pieces_for(used):
        return orders, count, pl.cdiv(pl.cdiv(used, count), 16) * 16

    class Chain:
        def __init__(self):
            self.token = None

        def after(self, *arrays):
            if self.token is None:
                return arrays
            return lax.optimization_barrier(arrays + (self.token,))[:-1]

    class Sum:
        def __init__(self, chain, pieces, heights, gains):
            self.chain, self.pieces, self.heights, self.gains = chain, pieces, heights, gains
            self.stage, self.result = 0, None

        def move(self, stage):
            return lambda k: k ^ (1 << orders[k & 1][stage])

        def put(self, grads):
            half = grads.shape[0] // 2
            sent = grads[half:]
            self.keep, self.wire = grads[:half], sibling(sent)
            self.chain.token = sent

        def step(self):
            last = bits - 1
            if self.stage > 2 * last:
                return
            keep, wire = self.chain.after(self.keep, self.wire)
            if self.stage < last:
                half = keep.shape[0] // 2
                total = keep.astype(F32) + wire.astype(F32)
                sent, self.keep = total[half:].astype(BF), total[:half].astype(BF)
                self.wire = swap(sent, self.move(self.stage))
            else:
                if self.stage == last:
                    sent = (keep.astype(F32) + wire.astype(F32)).astype(BF)
                else:
                    sent = jnp.concatenate([keep, wire], axis=0)
                back = 2 * last - 1 - self.stage
                self.keep = sent
                self.wire = sibling(sent) if back < 0 else swap(sent, self.move(back))
            self.chain.token = sent
            self.stage += 1

        def unpack(self, scalars):
            if self.result is None and self.stage == 2 * bits - 1:
                ready = self.chain.after(self.keep, self.wire)
                self.result = unpack(*ready, scalars, self.pieces, self.heights, self.gains)
                self.chain.token = self.result[-1]

    def body(tokens, lengths, *rest):
        out_grad = rest[-1]
        post_query, post_key, post_value, post_out, post_gate, post_up, post_down = rest[0:7]
        pre_query, pre_key, pre_value, pre_out, pre_gate, pre_up, pre_down = rest[9:16]
        gains = [rest[k].reshape(1, D) for k in (7, 8, 16, 17)]
        post_attn_gain, post_ffn_gain, pre_attn_gain, pre_ffn_gain = gains
        sp = lax.axis_index("sp")
        me = lax.axis_index("dp") * n_sp + sp
        chip = sp >> 1
        scalars = jnp.stack([me, sp, lengths[chip]]).astype(jnp.int32)

        def to_slot(array):
            mine = lax.dynamic_index_in_dim(array, chip, 0, keepdims=False)
            other = lax.dynamic_index_in_dim(array, 1 - chip, 0, keepdims=False)
            return jnp.concatenate([mine, swap(other, lambda k: k ^ 3)], axis=0)

        cosine, sine = rope_tables()
        tables = dict(cosine=cosine, sine=sine)

        own_one = to_slot(tokens)
        sib_one = sibling(own_one)
        cotangent = to_slot(out_grad)

        rows_bf, rows_f32, full_bf = ((ROWS, D), BF), ((ROWS, D), F32), ((SEQ, D), BF)
        wide_bf, wide_f32 = ((ROWS, FF), BF), ((ROWS, FF), F32)
        gain_f32, head_f32 = ((1, D), F32), ((HEADS, ROWS), F32)
        half_bf, half_f32 = ((SEQ, HALF), BF), ((SEQ, HALF), F32)
        half_rows_bf, half_rows_f32 = ((ROWS, HALF), BF), ((ROWS, HALF), F32)
        saved = dict(q=rows_bf, k=full_bf, v=full_bf, lse=((ROWS, LANES), F32), mixed=rows_bf)
        wide = dict(gate=wide_f32, up=wide_f32, hidden=wide_bf)
        wide_back = dict(dgate=wide_bf, dup=wide_bf)
        post_ffn = dict(w_gate=post_gate.T, w_up=post_up.T, w_down=post_down)
        pre_ffn = dict(w_gate=pre_gate.T, w_up=pre_up.T, w_down=pre_down)
        post_qkv = dict(w_key=post_key, w_value=post_value, w_query=post_query)
        pre_qkv = dict(w_key=pre_key, w_value=pre_value, w_query=pre_query)
        heads_outs = dict(dqp=half_rows_bf, dkp=half_bf, dvp=half_bf, ge_own=rows_f32)
        heads_tmp = dict(dq=half_rows_f32, dk=half_f32, dv=half_f32)
        start_outs = dict(gmix=rows_bf, delta_t=head_f32, lse_t=head_f32)

        chain = Chain()
        ffn_pieces, attn_pieces = pieces_for(FFN_ROWS + GAIN_ROWS), pieces_for(ATTN_ROWS)
        ffn_grads = dict(grads=((count * ffn_pieces[2], LANES), BF))
        attn_grads = dict(grads=((count * attn_pieces[2], LANES), BF))
        ffn2 = Sum(chain, ffn_pieces, [FF] * 3, 0)
        ffn1 = Sum(chain, ffn_pieces, [FF] * 3, 4)
        attn2 = Sum(chain, attn_pieces, [D] * 4, 0)
        attn1 = Sum(chain, attn_pieces, [D] * 4, 0)

        def run(body, fetched, ins, outs, stored, scratch, token=0, pieces=None):
            def bound(refs, scalars_ref):
                refs.pieces, refs.me = pieces, scalars_ref[0]
                body(refs, scalars_ref)

            bound.__name__ = body.__name__
            made = run_kernel(bound, *chain.after(scalars), fetched, ins, outs, stored, scratch)
            chain.token = made[token]
            return made

        class Home:
            def start(self, array):
                self.mine, (other,) = array[:BLK], chain.after(array[BLK:])
                self.wire = swap(other, lambda k: k ^ 3)
                chain.token = other

            def finish(self):
                mine, other = chain.after(self.mine, self.wire)
                ways = jnp.stack([mine, other]), jnp.stack([other, mine])
                self.result = jnp.where(chip == 0, *ways)
                chain.token = self.result

        home_output, home_grad = Home(), Home()

        entry2, q1, k1, v1, lse1, mixed1, middle1, result1 = run(
            post_forward,
            dict(**post_qkv, **tables, w_out=post_out, attn_gain=post_attn_gain, **post_ffn)
            | dict(ffn_gain=post_ffn_gain, next_gain=pre_attn_gain),
            dict(own=own_one, sib=sib_one),
            dict(entry=rows_bf),
            saved | dict(middle=rows_f32, result=rows_f32),
            wide,
        )
        sib_two = sibling(entry2)
        mixed2, q2, k2, v2, lse2 = run(
            attention_forward,
            dict(**pre_qkv, **tables),
            dict(own=entry2, sib=sib_two),
            dict(mixed=saved.pop("mixed")),
            saved,
            {},
        )
        (cotangent,) = chain.after(cotangent)
        middle2, out_rows, dgate, dup, grads = run(
            pre_ffn_forward,
            dict(w_out=pre_out, result=result1, last_gain=post_ffn_gain, ffn_gain=pre_ffn_gain)
            | pre_ffn,
            dict(mixed=mixed2, cotangent=cotangent),
            dict(middle=rows_f32, output=rows_bf) | wide_back | ffn_grads,
            {},
            wide,
            1,
            ffn_pieces,
        )
        ffn2.put(grads)
        home_output.start(out_rows)

        held = {}

        def middle_back():
            held[0] = run(
                pre_middle_backward,
                dict(w_gate=pre_ffn["w_gate"], w_up=pre_ffn["w_up"])
                | dict(ffn_gain=pre_ffn_gain, w_out=pre_out, lse=lse2),
                dict(dgate=dgate, dup=dup, middle=middle2, cotangent=cotangent, mixed=mixed2),
                dict(grad_middle=rows_f32, grad_gain=gain_f32) | start_outs,
                {},
                {},
                token=1,
            )

        def heads(start, arrays, weights, first):
            fetched = dict(zip(("q", "k", "v"), arrays)) | tables | weights
            ins = dict(zip(("gmix", "delta_t", "lse_t"), start))
            if first is None:
                outs = heads_outs | dict(ge_sib=rows_f32)
                return run(first_heads_backward, fetched, ins, outs, {}, heads_tmp, token=2)
            ins |= dict(part_own=first[3], part_sib=first[4])
            outs = heads_outs | dict(ge_sib=rows_bf)
            return run(last_heads_backward, fetched, ins, outs, {}, heads_tmp, token=4)

        def pre_heads_a():
            held[1] = heads(held[0][2:], (q2, k2, v2), pre_qkv, None)

        def pre_heads_b():
            held[2] = heads(held[0][2:], (q2, k2, v2), pre_qkv, held[1])
            held[3] = sibling(held[2][4])

        def ffn_again():
            held[4] = run(
                post_ffn_again,
                dict(middle=middle1, attn_gain=post_attn_gain)
                | dict(w_gate=post_ffn["w_gate"], w_up=post_ffn["w_up"]),
                {},
                dict(ffn_in=rows_bf) | wide,
                {},
                {},
            )

        def ffn_back():
            ins = dict(zip(("ffn_in", "gate", "up", "hidden"), held[4]))
            *rest, grads = run(
                post_ffn_backward,
                dict(middle=middle1, result=result1, ffn_gain=post_ffn_gain)
                | dict(next_gain=pre_attn_gain, attn_gain=post_attn_gain)
                | dict(**post_ffn, w_out=post_out, mixed=mixed1, lse=lse1),
                ins
                | dict(grad_middle=held[0][0], grad_gain=held[0][1])
                | dict(ge_own=held[2][3], ge_recv=held[3]),
                dict(new_middle=rows_f32) | start_outs | ffn_grads,
                {},
                wide_back,
                2,
                ffn_pieces,
            )
            held[5] = rest
            ffn1.put(grads)

        def weight_grads(total, fetched, grad_middle, own, sib, first, last):
            (grads,) = run(
                attention_weight_grads,
                fetched,
                dict(grad_middle=grad_middle, own=own, sib=sib)
                | dict(zip(("dqa", "dka", "dva"), first))
                | dict(zip(("dqb", "dkb", "dvb"), last))
                | ({} if fetched else dict(mixed=mixed2)),
                attn_grads,
                {},
                {},
                0,
                attn_pieces,
            )
            total.put(grads)

        def pre_weights():
            weight_grads(attn2, {}, held[0][0], entry2, sib_two, held[1], held[2])

        def post_heads_a():
            held[6] = heads(held[5][1:], (q1, k1, v1), post_qkv, None)

        def post_heads_b():
            held[7] = heads(held[5][1:], (q1, k1, v1), post_qkv, held[6])
            held[8] = sibling(held[7][4])

        def post_weights():
            saved_mix = dict(mixed=mixed1)
            weight_grads(attn1, saved_mix, held[5][0], own_one, sib_one, held[6], held[7])

        def send_grad():
            total = held[5][0] + held[7][3] + held[8].astype(F32)
            home_grad.start(total.astype(BF))


        plan = (
            middle_back,
            ffn2,
            pre_heads_a,
            pre_heads_b,
            ffn2,
            home_output.finish,
            ffn_again,
            ffn_back,
            ffn2,
            ffn1,
            pre_weights,
            ffn2,
            attn2,
            post_heads_a,
            ffn2,
            ffn1,
            attn2,
            post_heads_b,
            ffn2,
            ffn1,
            attn2,
            post_weights,
            send_grad,
            ffn2,
            ffn1,
            attn2,
            attn1,
            home_grad.finish,
        )
        for action in plan:
            if isinstance(action, Sum):
                action.step()
            else:
                action()
        sums = (ffn2, ffn1, attn2, attn1)
        for again in range(2 * bits):
            for total in sums:
                total.step()
        for total in sums:
            total.unpack(scalars)
        down2, gate2, up2 = ffn2.result
        down1, gate1, up1, *gains = ffn1.result
        gain_pre_ffn, gain_pre_attn, gain_post_ffn, gain_post_attn = (g.reshape(D) for g in gains)
        out2, query2, key2, value2 = attn2.result
        out1, query1, key1, value1 = attn1.result
        post_grads = (query1, key1, value1, out1, gate1.T, up1.T, down1, gain_post_attn, gain_post_ffn)
        pre_grads = (query2, key2, value2, out2, gate2.T, up2.T, down2, gain_pre_attn, gain_pre_ffn)
        return (home_output.result, home_grad.result) + post_grads + pre_grads

    spread = P("dp", "sp", None)
    in_specs = (spread, P("dp")) + (P(),) * 18 + (spread,)
    out_specs = (spread, spread) + (P(),) * 18
    return jax.shard_map(body, mesh=mesh, in_specs=in_specs, out_specs=out_specs, check_vma=False)
```

time: 321 us -> 295 us (0.919)
  waiting for transfers between devices: 123 us -> 101 us
  starting transfers between devices: 39.3 us -> 50.2 us
  Pallas kernels: 124 us -> 114 us
  other arithmetic: 13.6 us -> 7.49 us
    ppermute x38 -> x48, waiting for transfers between devices: 123 us -> 101 us  [swap(): return lax.ppermute(array, AXES, [(k, move(k)) for k in range(count)])]
    ppermute x38 -> x48, starting transfers between devices: 39.3 us -> 50.2 us  [swap(): return lax.ppermute(array, AXES, [(k, move(k)) for k in range(count)])]
    pallas_call x3 -> x4, Pallas kernels: 22.5 us -> 14.2 us  [unpack(): pl.pallas_call(unpack, name=unpack.__name__, out_shape=[jax.ShapeDtypeStr...]
    slice x12 -> x22, local copies, waits for them, and re-layouts: 0.41 us -> 4.27 us  [the longest x16 2.15 us: step(): sent, self.keep = (total[half:].astype(BF), total[:half].astype(BF))]
    another operation x6 -> x0, local copies, waits for them, and re-layouts: 3.64 us -> none  [the longest x2 1.56 us: from_slot(): jnp.stack([mine, other])]
    unnamed x33 -> x52, local copies, waits for them, and re-layouts: 6.07 us -> 8.59 us
    pallas_call x6 -> x12, Pallas kernels: 101 us -> 99.9 us  [run_kernel(): pl.pallas_call(kernel, name=body.__name__, out_shape=[jax.ShapeDtypeStruc...]
  transfers between devices with their start and end apart: 38 -> 48, of which waited for: 17 -> 19; matrix products, arithmetic and copies ran while one was open for 7% -> 3% of each run, Pallas kernels for 23% -> 20%
where the time goes in v3:
time: 295 us; the launch traced here: 290 us
  Pallas kernels  114 us (39%)
  waiting for transfers between devices  101 us (34%)
  starting transfers between devices  50.2 us (17%)
  local copies, waits for them, and re-layouts  15.4 us (5%)
  other arithmetic  7.49 us (3%)
    ppermute x48, waiting for transfers between devices, swap(): return lax.ppermute(array, AXES, [(k, move(k)) for k in range(count)])  101 us
    pallas_call x12, Pallas kernels, run_kernel(): pl.pallas_call(kernel, name=body.__name__, out_shape=[jax.ShapeDtypeStruc...  99.9 us
    ppermute x48, starting transfers between devices, swap(): return lax.ppermute(array, AXES, [(k, move(k)) for k in range(count)])  50.2 us
    pallas_call x4, Pallas kernels, unpack(): pl.pallas_call(unpack, name=unpack.__name__, out_shape=[jax.ShapeDtypeStr...  14.2 us
    unnamed x52, local copies, waits for them, and re-layouts  8.59 us
  transfers between devices with their start and end apart: 48, of which 19 were waited for; matrix products, arithmetic and copies ran while one was open for 3% of the time, Pallas kernels for 20%

profile of v3, /device:TPU:0, one launch (start us, length us, event | category | flops | bytes accessed | tf_op | source)
XLA Modules:
  0.0 289.6 jit_solution(2504183907778247250)
XLA Ops:
  0.7 1.1 dynamic-slice_bitcast_fusion.3
  1.7 2.4 collective-permute-start
  4.2 6.7 %collective-permute-done = bf16[256,512]{1,0:T(8,128)(2,1)S(1)} collective-permute-done((bf16[256,512]{1,0:T(8,128)(2,1)S(1)}, bf16[256,512]{1,0:T(8,128)(2,1)S(1)}, u32[]{:S(2)}, u32[]{:S(2)}) %collective-permute-start) | collective-permute-done | bytes 262176 | tf_op jit(solution)/shard_map/ppermute | solution.py:559
  12.9 16.7 %post_forward.1 = (bf16[512,512]{1,0:T(8,128)(2,1)S(1)}, bf16[512,512]{1,0:T(8,128)(2,1)S(1)}, bf16[1024,512]{1,0:T(8,128)(2,1)S(1)}, bf16[1024,512]{1,0:T(8,128...) custom-call(s32[3]{0:T(128)S(1)} %pad_add_fusion.scalars_ref, ...), custom_call_target="tpu_custom_call" | custom-call | bytes 1 | tf_op jit(solution)/shard_map/post_forward/pallas_call | solution.py:112
  29.6 1.0 copy-done.2
  30.6 1.0 copy-done.3
  33.1 2.3 collective-permute-start.3
  35.4 6.5 %collective-permute-done.3 = bf16[256,512]{1,0:T(8,128)(2,1)S(1)} collective-permute-done((bf16[256,512]{1,0:T(8,128)(2,1)S(1)}, bf16[256,512]{1,0:T(8,128)(2,1)S(1)}, u32[]{:S(2)}, u32[]{:S(2)}) %collective-permute-start.3) | collective-permute-done | bytes 262176 | tf_op jit(solution)/shard_map/ppermute | solution.py:559
  41.9 12.1 %attention_forward.1 = (bf16[512,512]{1,0:T(8,128)(2,1)S(1)}, bf16[512,512]{1,0:T(8,128)(2,1)S(1)}, bf16[1024,512]{1,0:T(8,128)(2,1)S(1)}, bf16[1024,512]{1,0:T(8,128)(2,1)S(1)}, f32[512,128]{1,0:T(8,128)S(1)}) custom-call(s32[3]{0:T(128)S(1)} %pad_add_fusion.scalars_ref, bf16[512,512]{1,0:T(8,128)(2,1)} %args_5_.10, bf16[512,512]{1,0:T(8,128)(2,1)} %args_6_.10, ...), custom_call_target="tpu_custom_call" | custom-call | bytes 1 | tf_op jit(solution)/shard_map/attention_forward/pallas_call | solution.py:112
  54.1 1.0 copy-done.4
  55.0 1.0 copy-done.5
  56.7 10.0 %pre_ffn_forward.1 = (f32[512,512]{1,0:T(8,128)S(1)}, bf16[512,512]{1,0:T(8,128)(2,1)S(1)}, bf16[512,1376]{1,0:T(8,128)(2,1)S(1)}, bf16[512,1376]{1,0:T(8,128)(2,1)S(1)}, bf16[16896,128]{1,0:T(8,128)(2,1)S(1)}) custom-call(s32[3]{0:T(128)S(1)} %pad_add_fusion.scalars_ref, bf16[512,512]{1,0:T(8,128)(2,1)} %args_3_.10, f32[512,512]{1,0:T(8,128)} %copy-done.1, ...), custom_call_target="tpu_custom_call" | custom-call | bytes 1 | tf_op jit(solution)/shard_map/pre_ffn_forward/pallas_call | solution.py:112
  67.9 5.5 %pre_middle_backward.1 = (f32[512,512]{1,0:T(8,128)S(1)}, f32[1,512]{1,0:T(1,128)S(1)}, bf16[512,512]{1,0:T(8,128)(2,1)S(1)}, f32[8,512]{1,0:T(8,128)S(1)}, f32[8,512]{1,0:T(8,128)S(1)}) custom-call(s32[3]{0:T(128)S(1)} %pad_add_fusion.scalars_ref, bf16[1376,512]{1,0:T(8,128)(2,1)} %bitcast.37, bf16[1376,512]{1,0:T(8,128)(2,1)} %bitcast.39, ...), custom_call_target="tpu_custom_call" | custom-call | bytes 1 | tf_op jit(solution)/shard_map/pre_middle_backward/pallas_call | solution.py:112
  74.2 1.5 fusion.3
  75.7 2.4 collective-permute-start.6
  78.9 1.0 copy-done.12
  80.0 8.7 %first_heads_backward.2 = (bf16[512,256]{1,0:T(8,128)(2,1)S(1)}, bf16[1024,256]{1,0:T(8,128)(2,1)S(1)}, bf16[1024,256]{1,0:T(8,128)(2,1)S(1)}, f32[512,512]{1,0:T(8,128)S(1)}, f32[512,512]{1,0:T(8,128)S(1)}) custom-call(s32[3]{0:T(128)S(1)} %pad_add_fusion.scalars_ref, bf16[512,512]{1,0:T(8,128)(2,1)} %copy-done.10, bf16[1024,512]{1,0:T(8,128)(2,1)} %copy-done.4, ...), custom_call_target="tpu_custom_call" | custom-call | bytes 1 | tf_op jit(solution)/shard_map/first_heads_backward/pallas_call | solution.py:112
  88.7 8.4 %last_heads_backward.2 = (bf16[512,256]{1,0:T(8,128)(2,1)S(1)}, bf16[1024,256]{1,0:T(8,128)(2,1)S(1)}, bf16[1024,256]{1,0:T(8,128)(2,1)S(1)}, f32[512,512]{1,0:T(8,128)S(1)}, bf16[512,512]{1,0:T(8,128)(2,1)S(1)}) custom-call(s32[3]{0:T(128)S(1)} %pad_add_fusion.scalars_ref, bf16[512,512]{1,0:T(8,128)(2,1)} %copy-done.10, bf16[1024,512]{1,0:T(8,128)(2,1)} %copy-done.4, ...), custom_call_target="tpu_custom_call" | custom-call | bytes 1 | tf_op jit(solution)/shard_map/last_heads_backward/pallas_call | solution.py:112
  97.2 1.6 add_convert_fusion.3
  99.7 4.4 %post_ffn_again.1 = (bf16[512,512]{1,0:T(8,128)(2,1)S(1)}, f32[512,1376]{1,0:T(8,128)S(1)}, f32[512,1376]{1,0:T(8,128)S(1)}, bf16[512,1376]{1,0:T(8,128)(2,1)S(1)}) custom-call(s32[3]{0:T(128)S(1)} %pad_add_fusion.scalars_ref, f32[512,512]{1,0:T(8,128)} %copy-done, f32[1,512]{1,0:T(1,128)} %bitcast.45, bf16[1376,512]{1,0:T(8,128)(2,1)} %bitcast.31, ...), custom_call_target="tpu_custom_call" | custom-call | bytes 1 | tf_op jit(solution)/shard_map/post_ffn_again/pallas_call | solution.py:112
  104.2 11.3 %post_ffn_backward.1 = (f32[512,512]{1,0:T(8,128)S(1)}, bf16[512,512]{1,0:T(8,128)(2,1)S(1)}, f32[8,512]{1,0:T(8,128)S(1)}, f32[8,512]{1,0:T(8,128)S(1)}, bf16[16896,128]{1,0:T(8,128)(2,1)S(1)}) custom-call(s32[3]{0:T(128)S(1)} %pad_add_fusion.scalars_ref, f32[512,512]{1,0:T(8,128)} %copy-done, f32[512,512]{1,0:T(8,128)} %copy-done.1, f32[1,512]{1,0:T(1,128)} %bitcast.49, ...), custom_call_target="tpu_custom_call" | custom-call | bytes 1 | tf_op jit(solution)/shard_map/post_ffn_backward/pallas_call | solution.py:112
  117.4 8.7 %collective-permute-done.9 = bf16[2112,128]{1,0:T(8,128)(2,1)S(1)} collective-permute-done((bf16[2112,128]{1,0:T(8,128)(2,1)S(1)}, bf16[2112,128]{1,0:T(8,128)(2,1)S(1)}, u32[]{:S(2)}, u32[]{:S(2)}) %collective-permute-start.9) | collective-permute-done | bytes 540704 | tf_op jit(solution)/shard_map/ppermute | solution.py:559
  128.0 2.5 attention_weight_grads.2
  130.8 1.6 collective-permute-start.11
  133.3 6.4 %collective-permute-done.11 = bf16[1056,128]{1,0:T(8,128)(2,1)S(1)} collective-permute-done((bf16[1056,128]{1,0:T(8,128)(2,1)S(1)}, bf16[1056,128]{1,0:T(8,128)(2,1)S(1)}, u32[]{:S(2)}, u32[]{:S(2)}) %collective-permute-start.11) | collective-permute-done | bytes 270368 | tf_op jit(solution)/shard_map/ppermute | solution.py:559
  139.8 2.6 collective-permute-start.14
  143.7 8.3 %first_heads_backward.3 = (bf16[512,256]{1,0:T(8,128)(2,1)S(1)}, bf16[1024,256]{1,0:T(8,128)(2,1)S(1)}, bf16[1024,256]{1,0:T(8,128)(2,1)S(1)}, f32[512,512]{1,0:T(8,128)S(1)}, f32[512,512]{1,0:T(8,128)S(1)}) custom-call(s32[3]{0:T(128)S(1)} %pad_add_fusion.scalars_ref, bf16[512,512]{1,0:T(8,128)(2,1)} %copy-done.7, bf16[1024,512]{1,0:T(8,128)(2,1)} %copy-done.2, ...), custom_call_target="tpu_custom_call" | custom-call | bytes 1 | tf_op jit(solution)/shard_map/first_heads_backward/pallas_call | solution.py:112
  152.8 1.6 collective-permute-start.17
  155.1 8.4 %last_heads_backward.3 = (bf16[512,256]{1,0:T(8,128)(2,1)S(1)}, bf16[1024,256]{1,0:T(8,128)(2,1)S(1)}, bf16[1024,256]{1,0:T(8,128)(2,1)S(1)}, f32[512,512]{1,0:T(8,128)S(1)}, bf16[512,512]{1,0:T(8,128)(2,1)S(1)}) custom-call(s32[3]{0:T(128)S(1)} %pad_add_fusion.scalars_ref, bf16[512,512]{1,0:T(8,128)(2,1)} %copy-done.7, bf16[1024,512]{1,0:T(8,128)(2,1)} %copy-done.2, ...), custom_call_target="tpu_custom_call" | custom-call | bytes 1 | tf_op jit(solution)/shard_map/last_heads_backward/pallas_call | solution.py:112
  163.7 1.6 collective-permute-start.23
  166.2 1.6 collective-permute-start.21
  167.8 3.6 %attention_weight_grads.3 = bf16[8192,128]{1,0:T(8,128)(2,1)S(1)} custom-call(s32[3]{0:T(128)S(1)} %pad_add_fusion.scalars_ref, bf16[512,512]{1,0:T(8,128)(2,1)} %copy-done.6, f32[512,512]{1,0:T(8,128)S(1)} %get-tuple-element.232.args_1_, bf16[512,512]{1,0:T(8,128)(2,1)S(1)} %pad_maximum_fusion.args_12_.args_2_, ...), custom_call_target="tpu_custom_call" | custom-call | bytes 1 | tf_op jit(solution)/shard_map/attention_weight_grads/pallas_call | solution.py:112
  172.0 1.1 collective-permute-start.19
  173.1 1.6 collective-permute-start.27
  174.7 4.1 %collective-permute-done.22 = bf16[1056,128]{1,0:T(8,128)(2,1)S(1)} collective-permute-done((bf16[1056,128]{1,0:T(8,128)(2,1)S(1)}, bf16[1056,128]{1,0:T(8,128)(2,1)S(1)}, u32[]{:S(2)}, u32[]{:S(2)}) %collective-permute-start.22) | collective-permute-done | bytes 270368 | tf_op jit(solution)/shard_map/ppermute | solution.py:559
  179.0 2.6 collective-permute-start.26
  181.7 2.7 collective-permute-start.25
  184.7 1.0 collective-permute-start.24
  186.7 1.2 collective-permute-start.31
  187.9 1.8 collective-permute-done.26
  190.4 2.4 collective-permute-start.29
  192.8 1.1 collective-permute-done.24
  194.2 1.6 collective-permute-start.28
  195.8 12.6 %collective-permute-done.31 = bf16[4224,128]{1,0:T(8,128)(2,1)S(1)} collective-permute-done((bf16[4224,128]{1,0:T(8,128)(2,1)S(1)}, bf16[4224,128]{1,0:T(8,128)(2,1)S(1)}, u32[]{:S(2)}, u32[]{:S(2)}) %collective-permute-start.31) | collective-permute-done | bytes 1081376 | tf_op jit(solution)/shard_map/ppermute | solution.py:559
  208.7 1.2 collective-permute-start.34
  211.0 1.2 collective-permute-start.32
  212.2 5.9 %collective-permute-done.34 = bf16[1056,128]{1,0:T(8,128)(2,1)S(1)} collective-permute-done((bf16[1056,128]{1,0:T(8,128)(2,1)S(1)}, bf16[1056,128]{1,0:T(8,128)(2,1)S(1)}, u32[]{:S(2)}, u32[]{:S(2)}) %collective-permute-start.34) | collective-permute-done | bytes 270368 | tf_op jit(solution)/shard_map/ppermute | solution.py:559
  218.2 1.6 collective-permute-start.37
  219.8 1.1 collective-permute-done.32
  221.0 10.3 %collective-permute-done.37 = bf16[2112,128]{1,0:T(8,128)(2,1)S(1)} collective-permute-done((bf16[2112,128]{1,0:T(8,128)(2,1)S(1)}, bf16[2112,128]{1,0:T(8,128)(2,1)S(1)}, u32[]{:S(2)}, u32[]{:S(2)}) %collective-permute-start.37) | collective-permute-done | bytes 540704 | tf_op jit(solution)/shard_map/ppermute | solution.py:559
  233.1 1.1 collective-permute-start.35
  234.1 7.5 %collective-permute-done.36 = bf16[1024,128]{1,0:T(8,128)(2,1)S(1)} collective-permute-done((bf16[1024,128]{1,0:T(8,128)(2,1)S(1)}, bf16[1024,128]{1,0:T(8,128)(2,1)S(1)}, u32[]{:S(2)}, u32[]{:S(2)}) %collective-permute-start.36) | collective-permute-done | bytes 262176 | tf_op jit(solution)/shard_map/ppermute | solution.py:559
  241.7 1.2 collective-permute-start.39
  243.5 3.1 %collective-permute-done.40 = bf16[4224,128]{1,0:T(8,128)(2,1)S(1)} collective-permute-done((bf16[4224,128]{1,0:T(8,128)(2,1)S(1)}, bf16[4224,128]{1,0:T(8,128)(2,1)S(1)}, u32[]{:S(2)}, u32[]{:S(2)}) %collective-permute-start.40) | collective-permute-done | bytes 1081376 | tf_op jit(solution)/shard_map/ppermute | solution.py:559
  246.9 5.4 %collective-permute-done.39 = bf16[2048,128]{1,0:T(8,128)(2,1)S(1)} collective-permute-done((bf16[2048,128]{1,0:T(8,128)(2,1)S(1)}, bf16[2048,128]{1,0:T(8,128)(2,1)S(1)}, u32[]{:S(2)}, u32[]{:S(2)}) %collective-permute-start.39) | collective-permute-done | bytes 524320 | tf_op jit(solution)/shard_map/ppermute | solution.py:559
  252.8 4.6 %collective-permute-done.41 = bf16[512,128]{1,0:T(8,128)(2,1)S(1)} collective-permute-done((bf16[512,128]{1,0:T(8,128)(2,1)S(1)}, bf16[512,128]{1,0:T(8,128)(2,1)S(1)}, u32[]{:S(2)}, u32[]{:S(2)}) %collective-permute-start.41) | collective-permute-done | bytes 131104 | tf_op jit(solution)/shard_map/ppermute | solution.py:559
  257.5 1.6 collective-permute-start.42
  259.6 6.0 %collective-permute-done.42 = bf16[1024,128]{1,0:T(8,128)(2,1)S(1)} collective-permute-done((bf16[1024,128]{1,0:T(8,128)(2,1)S(1)}, bf16[1024,128]{1,0:T(8,128)(2,1)S(1)}, u32[]{:S(2)}, u32[]{:S(2)}) %collective-permute-start.42) | collective-permute-done | bytes 262176 | tf_op jit(solution)/shard_map/ppermute | solution.py:559
  265.6 1.8 collective-permute-start.43
  267.4 7.4 %collective-permute-done.43 = bf16[2048,128]{1,0:T(8,128)(2,1)S(1)} collective-permute-done((bf16[2048,128]{1,0:T(8,128)(2,1)S(1)}, bf16[2048,128]{1,0:T(8,128)(2,1)S(1)}, u32[]{:S(2)}, u32[]{:S(2)}) %collective-permute-start.43) | collective-permute-done | bytes 524320 | tf_op jit(solution)/shard_map/ppermute | solution.py:559
  275.1 4.4 %unpack.4 = (f32[1376,512]{1,0:T(8,128)}, f32[1376,512]{1,0:T(8,128)}, f32[1376,512]{1,0:T(8,128)}) custom-call(s32[3]{0:T(128)S(1)} %pad_add_fusion.scalars_ref, bf16[8448,128]{1,0:T(8,128)(2,1)S(1)} %constant_dynamic-update-slice_fusion.6.mine_ref, bf16[8448,128]{1,0:T(8,128)(2,1)S(1)} %collective-permute-done.47.other_ref), custom_call_target="tpu_custom_call" | custom-call | bytes 1 | tf_op jit(solution)/shard_map/unpack/pallas_call | solution.py:534
  279.5 4.4 %unpack.5 = (f32[1376,512]{1,0:T(8,128)}, f32[1376,512]{1,0:T(8,128)}, f32[1376,512]{1,0:T(8,128)}, f32[4,128]{1,0:T(4,128)}, f32[4,128]{1,0:T(4,128)}, /*index=5*/f32[4,128]{1,0:T(4,128)}, f32[4,128]{1,0:T(4,128)}) custom-call(s32[3]{0:T(128)S(1)} %pad_add_fusion.scalars_ref, bf16[8448,128]{1,0:T(8,128)(2,1)S(1)} %constant_dynamic-update-slice_fusion.20.mine_ref, ...), custom_call_target="tpu_custom_call" | custom-call | bytes 1 | tf_op jit(solution)/shard_map/unpack/pallas_call | solution.py:534
  283.9 2.7 unpack.6
  286.7 2.7 unpack.7
  (167 shorter events, 25.1 us)
Async XLA Ops:
  0.7 10.4 %copy-start.17 = (s32[2]{0:T(128)S(1)}, s32[2]{0:T(128)}, u32[]{:S(2)}) copy-start(s32[2]{0:T(128)} %param.24) | copy-start | bytes 28
  1.7 9.1 %collective-permute-start = (bf16[256,512]{1,0:T(8,128)(2,1)S(1)}, bf16[256,512]{1,0:T(8,128)(2,1)S(1)}, u32[]{:S(2)}, u32[]{:S(2)}) collective-permute-start(bf16[256,512]{1,0:T(8,128)(2,1)S(1)} %get-tuple-element.391), channel_id=1, source_target_pairs={{0,3},{1,2},{2,1},{3,0},{4,7},{5,6},{6,5},{7,4},{8,11},{9,10},{10,... | collective-permute-start | bytes 786440 | tf_op jit(solution)/shard_map/ppermute | solution.py:559
  10.9 2.0 collective-permute-start.1
  12.9 20.1 %copy-start.16 = (bf16[2,256,512]{2,1,0:T(8,128)(2,1)S(1)}, bf16[2,256,512]{2,1,0:T(8,128)(2,1)}, u32[]{:S(2)}) copy-start(bf16[2,256,512]{2,1,0:T(8,128)(2,1)} %param.43) | copy-start | bytes 1572868
  29.6 1.0 copy-start.2
  30.6 1.0 copy-start.3
  31.5 0.8 copy-start.7
  33.0 21.0 %copy-start = (f32[512,512]{1,0:T(8,128)}, f32[512,512]{1,0:T(8,128)S(1)}, u32[]{:S(2)}) copy-start(f32[512,512]{1,0:T(8,128)S(1)} %get-tuple-element.222.args_0_) | copy-start | bytes 3145732
  33.0 21.0 %copy-start.1 = (f32[512,512]{1,0:T(8,128)}, f32[512,512]{1,0:T(8,128)S(1)}, u32[]{:S(2)}) copy-start(f32[512,512]{1,0:T(8,128)S(1)} %get-tuple-element.192.args_1_) | copy-start | bytes 3145732
  33.0 21.0 %copy-start.6 = (bf16[512,512]{1,0:T(8,128)(2,1)}, bf16[512,512]{1,0:T(8,128)(2,1)S(1)}, u32[]{:S(2)}) copy-start(bf16[512,512]{1,0:T(8,128)(2,1)S(1)} %get-tuple-element.225.args_9_.args_0_) | copy-start | bytes 1572868
  33.0 8.9 %collective-permute-start.2 = (bf16[512,512]{1,0:T(8,128)(2,1)S(1)}, bf16[512,512]{1,0:T(8,128)(2,1)S(1)}, u32[]{:S(2)}, u32[]{:S(2)}) collective-permute-start(bf16[512,512]{1,0:T(8,128)(2,1)S(1)} %get-tuple-element.188.args_5_.args_1_), channel_id=1, source_target_pairs={{0,1},{1,0},{2,3},{3,2},{4,5},{5,4},{6,7},{7,6},{8,9},{9,8},{10,11... | collective-permute-start | bytes 1572872 | tf_op jit(solution)/shard_map/ppermute | solution.py:559
  33.1 8.8 %collective-permute-start.3 = (bf16[256,512]{1,0:T(8,128)(2,1)S(1)}, bf16[256,512]{1,0:T(8,128)(2,1)S(1)}, u32[]{:S(2)}, u32[]{:S(2)}) collective-permute-start(bf16[256,512]{1,0:T(8,128)(2,1)S(1)} %get-tuple-element.389), channel_id=1, source_target_pairs={{0,3},{1,2},{2,1},{3,0},{4,7},{5,6},{6,5},{7,4},{8,11},{9,10},{10,... | collective-permute-start | bytes 786440 | tf_op jit(solution)/shard_map/ppermute | solution.py:559
  41.9 24.8 %copy-start.8 = (bf16[512,512]{1,0:T(8,128)(2,1)}, bf16[512,512]{1,0:T(8,128)(2,1)S(1)}, u32[]{:S(2)}) copy-start(bf16[512,512]{1,0:T(8,128)(2,1)S(1)} %collective-permute-done.2.args_6_.args_2_) | copy-start | bytes 1572868
  54.0 1.0 copy-start.4
  55.0 1.0 copy-start.5
  56.7 10.0 %copy-start.10 = (bf16[512,512]{1,0:T(8,128)(2,1)}, bf16[512,512]{1,0:T(8,128)(2,1)S(1)}, u32[]{:S(2)}) copy-start(bf16[512,512]{1,0:T(8,128)(2,1)S(1)} %get-tuple-element.206.args_0_) | copy-start | bytes 1572868
  67.1 6.4 %collective-permute-start.5 = (bf16[8448,128]{1,0:T(8,128)(2,1)S(1)}, bf16[8448,128]{1,0:T(8,128)(2,1)S(1)}, u32[]{:S(2)}, u32[]{:S(2)}) collective-permute-start(bf16[8448,128]{1,0:T(8,128)(2,1)S(1)} %get-tuple-element.359), channel_id=1, source_target_pairs={{0,1},{1,0},{2,3},{3,2},{4,5},{5,4},{6,7},{7,6},{8,9},{9,8},{10,11... | collective-permute-start | bytes 6488072 | tf_op jit(solution)/shard_map/ppermute | solution.py:559
  73.4 0.8 copy-start.11
  75.7 21.5 %collective-permute-start.6 = (bf16[4224,128]{1,0:T(8,128)(2,1)}, bf16[4224,128]{1,0:T(8,128)(2,1)}, u32[]{:S(2)}, u32[]{:S(2)}) collective-permute-start(bf16[4224,128]{1,0:T(8,128)(2,1)} %get-tuple-element.362), channel_id=1, source_target_pairs={{0,2},{1,5},{2,0},{3,7},{4,6},{5,1},{6,4},{7,3},{8,10},{9,13},{10,... | collective-permute-start | bytes 3244040 | tf_op jit(solution)/shard_map/ppermute | solution.py:559
  78.1 20.8 %collective-permute-start.4 = (bf16[256,512]{1,0:T(8,128)(2,1)}, bf16[256,512]{1,0:T(8,128)(2,1)S(1)}, u32[]{:S(2)}, u32[]{:S(2)}) collective-permute-start(bf16[256,512]{1,0:T(8,128)(2,1)} %get-tuple-element.196), channel_id=1, source_target_pairs={{0,3},{1,2},{2,1},{3,0},{4,7},{5,6},{6,5},{7,4},{8,11},{9,10},{10,... | collective-permute-start | bytes 786440 | tf_op jit(solution)/shard_map/ppermute | solution.py:559
  78.9 1.0 copy-start.12
  88.6 8.6 %copy-start.15 = (bf16[4224,128]{1,0:T(8,128)(2,1)S(1)}, bf16[4224,128]{1,0:T(8,128)(2,1)}, u32[]{:S(2)}) copy-start(bf16[4224,128]{1,0:T(8,128)(2,1)} %get-tuple-element.217) | copy-start | bytes 3244036
  97.1 7.1 %collective-permute-start.7 = (bf16[512,512]{1,0:T(8,128)(2,1)S(1)}, bf16[512,512]{1,0:T(8,128)(2,1)S(1)}, u32[]{:S(2)}, u32[]{:S(2)}) collective-permute-start(bf16[512,512]{1,0:T(8,128)(2,1)S(1)} %get-tuple-element.216), channel_id=1, source_target_pairs={{0,1},{1,0},{2,3},{3,2},{4,5},{5,4},{6,7},{7,6},{8,9},{9,8},{10,11... | collective-permute-start | bytes 1572872 | tf_op jit(solution)/shard_map/ppermute | solution.py:559
  116.2 10.1 %collective-permute-start.8 = (bf16[8448,128]{1,0:T(8,128)(2,1)S(1)}, bf16[8448,128]{1,0:T(8,128)(2,1)S(1)}, u32[]{:S(2)}, u32[]{:S(2)}) collective-permute-start(bf16[8448,128]{1,0:T(8,128)(2,1)S(1)} %get-tuple-element.356), channel_id=1, source_target_pairs={{0,1},{1,0},{2,3},{3,2},{4,5},{5,4},{6,7},{7,6},{8,9},{9,8},{10,11... | collective-permute-start | bytes 6488072 | tf_op jit(solution)/shard_map/ppermute | solution.py:559
  116.8 9.4 %collective-permute-start.9 = (bf16[2112,128]{1,0:T(8,128)(2,1)S(1)}, bf16[2112,128]{1,0:T(8,128)(2,1)S(1)}, u32[]{:S(2)}, u32[]{:S(2)}) collective-permute-start(bf16[2112,128]{1,0:T(8,128)(2,1)S(1)} %get-tuple-element.371), channel_id=1, source_target_pairs={{0,4},{1,3},{2,6},{3,1},{4,0},{5,7},{6,2},{7,5},{8,12},{9,11},{10,... | collective-permute-start | bytes 1622024 | tf_op jit(solution)/shard_map/ppermute | solution.py:559
  126.9 1.0 copy-start.9
  130.7 11.7 %collective-permute-start.10 = (bf16[4096,128]{1,0:T(8,128)(2,1)S(1)}, bf16[4096,128]{1,0:T(8,128)(2,1)S(1)}, u32[]{:S(2)}, u32[]{:S(2)}) collective-permute-start(bf16[4096,128]{1,0:T(8,128)(2,1)S(1)} %get-tuple-element.366), channel_id=1, source_target_pairs={{0,1},{1,0},{2,3},{3,2},{4,5},{5,4},{6,7},{7,6},{8,9},{9,8},{10,11... | collective-permute-start | bytes 3145736 | tf_op jit(solution)/shard_map/ppermute | solution.py:559
  130.8 8.9 %collective-permute-start.11 = (bf16[1056,128]{1,0:T(8,128)(2,1)S(1)}, bf16[1056,128]{1,0:T(8,128)(2,1)S(1)}, u32[]{:S(2)}, u32[]{:S(2)}) collective-permute-start(bf16[1056,128]{1,0:T(8,128)(2,1)S(1)} %get-tuple-element.379), channel_id=1, source_target_pairs={{0,8},{1,9},{2,10},{3,11},{4,12},{5,13},{6,14},{7,15},{8,0},{9,1},... | collective-permute-start | bytes 811016 | tf_op jit(solution)/shard_map/ppermute | solution.py:559
  132.4 20.0 %collective-permute-start.13 = (bf16[4224,128]{1,0:T(8,128)(2,1)S(1)}, bf16[4224,128]{1,0:T(8,128)(2,1)S(1)}, u32[]{:S(2)}, u32[]{:S(2)}) collective-permute-start(bf16[4224,128]{1,0:T(8,128)(2,1)S(1)} %get-tuple-element.361), channel_id=1, source_target_pairs={{0,2},{1,5},{2,0},{3,7},{4,6},{5,1},{6,4},{7,3},{8,10},{9,13},{10,... | collective-permute-start | bytes 3244040 | tf_op jit(solution)/shard_map/ppermute | solution.py:559
  139.8 12.2 %collective-permute-start.14 = (bf16[528,128]{1,0:T(8,128)(2,1)S(1)}, bf16[528,128]{1,0:T(8,128)(2,1)S(1)}, u32[]{:S(2)}, u32[]{:S(2)}) collective-permute-start(bf16[528,128]{1,0:T(8,128)(2,1)S(1)} %get-tuple-element.395), channel_id=1, source_target_pairs={{0,16},{1,17},{2,18},{3,19},{4,20},{5,21},{6,22},{7,23},{8,24},{9,... | collective-permute-start | bytes 405512 | tf_op jit(solution)/shard_map/ppermute | solution.py:559
  142.8 11.6 %collective-permute-start.12 = (bf16[2048,128]{1,0:T(8,128)(2,1)S(1)}, bf16[2048,128]{1,0:T(8,128)(2,1)S(1)}, u32[]{:S(2)}, u32[]{:S(2)}) collective-permute-start(bf16[2048,128]{1,0:T(8,128)(2,1)S(1)} %get-tuple-element.374), channel_id=1, source_target_pairs={{0,2},{1,5},{2,0},{3,7},{4,6},{5,1},{6,4},{7,3},{8,10},{9,13},{10,... | collective-permute-start | bytes 1572872 | tf_op jit(solution)/shard_map/ppermute | solution.py:559
  152.0 11.6 %collective-permute-start.18 = (bf16[528,128]{1,0:T(8,128)(2,1)S(1)}, bf16[528,128]{1,0:T(8,128)(2,1)S(1)}, u32[]{:S(2)}, u32[]{:S(2)}) collective-permute-start(bf16[528,128]{1,0:T(8,128)(2,1)S(1)} %add_convert_fusion.16), channel_id=1, source_target_pairs={{0,16},{1,17},{2,18},{3,19},{4,20},{5,21},{6,22},{7,23},{8,24},{9,... | collective-permute-start | bytes 405512 | tf_op jit(solution)/shard_map/ppermute | solution.py:559
  152.8 12.6 %collective-permute-start.17 = (bf16[2112,128]{1,0:T(8,128)(2,1)S(1)}, bf16[2112,128]{1,0:T(8,128)(2,1)S(1)}, u32[]{:S(2)}, u32[]{:S(2)}) collective-permute-start(bf16[2112,128]{1,0:T(8,128)(2,1)S(1)} %get-tuple-element.369), channel_id=1, source_target_pairs={{0,4},{1,3},{2,6},{3,1},{4,0},{5,7},{6,2},{7,5},{8,12},{9,11},{10,... | collective-permute-start | bytes 1622024 | tf_op jit(solution)/shard_map/ppermute | solution.py:559
  154.6 11.5 %collective-permute-start.16 = (bf16[1024,128]{1,0:T(8,128)(2,1)S(1)}, bf16[1024,128]{1,0:T(8,128)(2,1)S(1)}, u32[]{:S(2)}, u32[]{:S(2)}) collective-permute-start(bf16[1024,128]{1,0:T(8,128)(2,1)S(1)} %get-tuple-element.383), channel_id=1, source_target_pairs={{0,4},{1,3},{2,6},{3,1},{4,0},{5,7},{6,2},{7,5},{8,12},{9,11},{10,... | collective-permute-start | bytes 786440 | tf_op jit(solution)/shard_map/ppermute | solution.py:559
  163.6 8.1 %collective-permute-start.15 = (bf16[512,512]{1,0:T(8,128)(2,1)S(1)}, bf16[512,512]{1,0:T(8,128)(2,1)S(1)}, u32[]{:S(2)}, u32[]{:S(2)}) collective-permute-start(bf16[512,512]{1,0:T(8,128)(2,1)S(1)} %get-tuple-element.266), channel_id=1, source_target_pairs={{0,1},{1,0},{2,3},{3,2},{4,5},{5,4},{6,7},{7,6},{8,9},{9,8},{10,11... | collective-permute-start | bytes 1572872 | tf_op jit(solution)/shard_map/ppermute | solution.py:559
  163.7 9.3 %collective-permute-start.23 = (bf16[1056,128]{1,0:T(8,128)(2,1)S(1)}, bf16[1056,128]{1,0:T(8,128)(2,1)S(1)}, u32[]{:S(2)}, u32[]{:S(2)}) collective-permute-start(bf16[1056,128]{1,0:T(8,128)(2,1)S(1)} %constant_dynamic-update-slice_fusion), channel_id=1, source_target_pairs={{0,8},{1,9},{2,10},{3,11},{4,12},{5,13},{6,14},{7,15},{8,0},{9,1},... | collective-permute-start | bytes 811016 | tf_op jit(solution)/shard_map/ppermute | solution.py:559
  165.6 13.3 %collective-permute-start.22 = (bf16[1056,128]{1,0:T(8,128)(2,1)S(1)}, bf16[1056,128]{1,0:T(8,128)(2,1)S(1)}, u32[]{:S(2)}, u32[]{:S(2)}) collective-permute-start(bf16[1056,128]{1,0:T(8,128)(2,1)S(1)} %get-tuple-element.377), channel_id=1, source_target_pairs={{0,8},{1,9},{2,10},{3,11},{4,12},{5,13},{6,14},{7,15},{8,0},{9,1},... | collective-permute-start | bytes 811016 | tf_op jit(solution)/shard_map/ppermute | solution.py:559
  166.2 15.4 %collective-permute-start.21 = (bf16[512,128]{1,0:T(8,128)(2,1)S(1)}, bf16[512,128]{1,0:T(8,128)(2,1)S(1)}, u32[]{:S(2)}, u32[]{:S(2)}) collective-permute-start(bf16[512,128]{1,0:T(8,128)(2,1)S(1)} %get-tuple-element.399), channel_id=1, source_target_pairs={{0,8},{1,9},{2,10},{3,11},{4,12},{5,13},{6,14},{7,15},{8,0},{9,1},... | collective-permute-start | bytes 393224 | tf_op jit(solution)/shard_map/ppermute | solution.py:559
  171.6 12.8 %collective-permute-start.20 = (bf16[4096,128]{1,0:T(8,128)(2,1)S(1)}, bf16[4096,128]{1,0:T(8,128)(2,1)S(1)}, u32[]{:S(2)}, u32[]{:S(2)}) collective-permute-start(bf16[4096,128]{1,0:T(8,128)(2,1)S(1)} %get-tuple-element.365), channel_id=1, source_target_pairs={{0,1},{1,0},{2,3},{3,2},{4,5},{5,4},{6,7},{7,6},{8,9},{9,8},{10,11... | collective-permute-start | bytes 3145736 | tf_op jit(solution)/shard_map/ppermute | solution.py:559
  172.0 13.7 %collective-permute-start.19 = (bf16[256,512]{1,0:T(8,128)(2,1)S(1)}, bf16[256,512]{1,0:T(8,128)(2,1)S(1)}, u32[]{:S(2)}, u32[]{:S(2)}) collective-permute-start(bf16[256,512]{1,0:T(8,128)(2,1)S(1)} %get-tuple-element.279), channel_id=1, source_target_pairs={{0,3},{1,2},{2,1},{3,0},{4,7},{5,6},{6,5},{7,4},{8,11},{9,10},{10,... | collective-permute-start | bytes 786440 | tf_op jit(solution)/shard_map/ppermute | solution.py:559
  173.1 13.4 %collective-permute-start.27 = (bf16[2112,128]{1,0:T(8,128)(2,1)S(1)}, bf16[2112,128]{1,0:T(8,128)(2,1)S(1)}, u32[]{:S(2)}, u32[]{:S(2)}) collective-permute-start(bf16[2112,128]{1,0:T(8,128)(2,1)S(1)} %constant_dynamic-update-slice_fusion.2), channel_id=1, source_target_pairs={{0,4},{1,3},{2,6},{3,1},{4,0},{5,7},{6,2},{7,5},{8,12},{9,11},{10,... | collective-permute-start | bytes 1622024 | tf_op jit(solution)/shard_map/ppermute | solution.py:559
  179.0 10.8 %collective-permute-start.26 = (bf16[528,128]{1,0:T(8,128)(2,1)S(1)}, bf16[528,128]{1,0:T(8,128)(2,1)S(1)}, u32[]{:S(2)}, u32[]{:S(2)}) collective-permute-start(bf16[528,128]{1,0:T(8,128)(2,1)S(1)} %get-tuple-element.393), channel_id=1, source_target_pairs={{0,16},{1,17},{2,18},{3,19},{4,20},{5,21},{6,22},{7,23},{8,24},{9,... | collective-permute-start | bytes 405512 | tf_op jit(solution)/shard_map/ppermute | solution.py:559
  181.7 8.7 %collective-permute-start.25 = (bf16[256,128]{1,0:T(8,128)(2,1)S(1)}, bf16[256,128]{1,0:T(8,128)(2,1)S(1)}, u32[]{:S(2)}, u32[]{:S(2)}) collective-permute-start(bf16[256,128]{1,0:T(8,128)(2,1)S(1)} %get-tuple-element.403), channel_id=1, source_target_pairs={{0,16},{1,17},{2,18},{3,19},{4,20},{5,21},{6,22},{7,23},{8,24},{9,... | collective-permute-start | bytes 196616 | tf_op jit(solution)/shard_map/ppermute | solution.py:559
  184.7 9.2 %collective-permute-start.24 = (bf16[2048,128]{1,0:T(8,128)(2,1)S(1)}, bf16[2048,128]{1,0:T(8,128)(2,1)S(1)}, u32[]{:S(2)}, u32[]{:S(2)}) collective-permute-start(bf16[2048,128]{1,0:T(8,128)(2,1)S(1)} %get-tuple-element.373), channel_id=1, source_target_pairs={{0,2},{1,5},{2,0},{3,7},{4,6},{5,1},{6,4},{7,3},{8,10},{9,13},{10,... | collective-permute-start | bytes 1572872 | tf_op jit(solution)/shard_map/ppermute | solution.py:559
  186.7 21.7 %collective-permute-start.31 = (bf16[4224,128]{1,0:T(8,128)(2,1)S(1)}, bf16[4224,128]{1,0:T(8,128)(2,1)S(1)}, u32[]{:S(2)}, u32[]{:S(2)}) collective-permute-start(bf16[4224,128]{1,0:T(8,128)(2,1)S(1)} %constant_dynamic-update-slice_fusion.4), channel_id=1, source_target_pairs={{0,2},{1,5},{2,0},{3,7},{4,6},{5,1},{6,4},{7,3},{8,10},{9,13},{10,... | collective-permute-start | bytes 3244040 | tf_op jit(solution)/shard_map/ppermute | solution.py:559
  189.8 18.8 %collective-permute-start.30 = (bf16[528,128]{1,0:T(8,128)(2,1)S(1)}, bf16[528,128]{1,0:T(8,128)(2,1)S(1)}, u32[]{:S(2)}, u32[]{:S(2)}) collective-permute-start(bf16[528,128]{1,0:T(8,128)(2,1)S(1)} %add_convert_fusion.15), channel_id=1, source_target_pairs={{0,16},{1,17},{2,18},{3,19},{4,20},{5,21},{6,22},{7,23},{8,24},{9,... | collective-permute-start | bytes 405512 | tf_op jit(solution)/shard_map/ppermute | solution.py:559
  190.4 19.5 %collective-permute-start.29 = (bf16[256,128]{1,0:T(8,128)(2,1)S(1)}, bf16[256,128]{1,0:T(8,128)(2,1)S(1)}, u32[]{:S(2)}, u32[]{:S(2)}) collective-permute-start(bf16[256,128]{1,0:T(8,128)(2,1)S(1)} %add_convert_fusion.20), channel_id=1, source_target_pairs={{0,16},{1,17},{2,18},{3,19},{4,20},{5,21},{6,22},{7,23},{8,24},{9,... | collective-permute-start | bytes 196616 | tf_op jit(solution)/shard_map/ppermute | solution.py:559
  194.2 16.7 %collective-permute-start.28 = (bf16[1024,128]{1,0:T(8,128)(2,1)S(1)}, bf16[1024,128]{1,0:T(8,128)(2,1)S(1)}, u32[]{:S(2)}, u32[]{:S(2)}) collective-permute-start(bf16[1024,128]{1,0:T(8,128)(2,1)S(1)} %get-tuple-element.380), channel_id=1, source_target_pairs={{0,4},{1,3},{2,6},{3,1},{4,0},{5,7},{6,2},{7,5},{8,12},{9,11},{10,... | collective-permute-start | bytes 786440 | tf_op jit(solution)/shard_map/ppermute | solution.py:559
  208.7 9.4 %collective-permute-start.34 = (bf16[1056,128]{1,0:T(8,128)(2,1)S(1)}, bf16[1056,128]{1,0:T(8,128)(2,1)S(1)}, u32[]{:S(2)}, u32[]{:S(2)}) collective-permute-start(bf16[1056,128]{1,0:T(8,128)(2,1)S(1)} %constant_dynamic-update-slice_fusion.8), channel_id=1, source_target_pairs={{0,8},{1,9},{2,10},{3,11},{4,12},{5,13},{6,14},{7,15},{8,0},{9,1},... | collective-permute-start | bytes 811016 | tf_op jit(solution)/shard_map/ppermute | solution.py:559
  209.9 9.8 %collective-permute-start.33 = (bf16[512,128]{1,0:T(8,128)(2,1)S(1)}, bf16[512,128]{1,0:T(8,128)(2,1)S(1)}, u32[]{:S(2)}, u32[]{:S(2)}) collective-permute-start(bf16[512,128]{1,0:T(8,128)(2,1)S(1)} %constant_dynamic-update-slice_fusion.10), channel_id=1, source_target_pairs={{0,8},{1,9},{2,10},{3,11},{4,12},{5,13},{6,14},{7,15},{8,0},{9,1},... | collective-permute-start | bytes 393224 | tf_op jit(solution)/shard_map/ppermute | solution.py:559
  211.0 9.9 %collective-permute-start.32 = (bf16[512,128]{1,0:T(8,128)(2,1)S(1)}, bf16[512,128]{1,0:T(8,128)(2,1)S(1)}, u32[]{:S(2)}, u32[]{:S(2)}) collective-permute-start(bf16[512,128]{1,0:T(8,128)(2,1)S(1)} %get-tuple-element.396), channel_id=1, source_target_pairs={{0,8},{1,9},{2,10},{3,11},{4,12},{5,13},{6,14},{7,15},{8,0},{9,1},... | collective-permute-start | bytes 393224 | tf_op jit(solution)/shard_map/ppermute | solution.py:559
  218.2 13.1 %collective-permute-start.37 = (bf16[2112,128]{1,0:T(8,128)(2,1)S(1)}, bf16[2112,128]{1,0:T(8,128)(2,1)S(1)}, u32[]{:S(2)}, u32[]{:S(2)}) collective-permute-start(bf16[2112,128]{1,0:T(8,128)(2,1)S(1)} %constant_dynamic-update-slice_fusion.12), channel_id=1, source_target_pairs={{0,4},{1,3},{2,6},{3,1},{4,0},{5,7},{6,2},{7,5},{8,12},{9,11},{10,... | collective-permute-start | bytes 1622024 | tf_op jit(solution)/shard_map/ppermute | solution.py:559
  231.4 15.2 %collective-permute-start.40 = (bf16[4224,128]{1,0:T(8,128)(2,1)S(1)}, bf16[4224,128]{1,0:T(8,128)(2,1)S(1)}, u32[]{:S(2)}, u32[]{:S(2)}) collective-permute-start(bf16[4224,128]{1,0:T(8,128)(2,1)S(1)} %constant_dynamic-update-slice_fusion.16), channel_id=1, source_target_pairs={{0,2},{1,5},{2,0},{3,7},{4,6},{5,1},{6,4},{7,3},{8,10},{9,13},{10,... | collective-permute-start | bytes 3244040 | tf_op jit(solution)/shard_map/ppermute | solution.py:559
  232.4 9.2 %collective-permute-start.36 = (bf16[1024,128]{1,0:T(8,128)(2,1)S(1)}, bf16[1024,128]{1,0:T(8,128)(2,1)S(1)}, u32[]{:S(2)}, u32[]{:S(2)}) collective-permute-start(bf16[1024,128]{1,0:T(8,128)(2,1)S(1)} %constant_dynamic-update-slice_fusion.14), channel_id=1, source_target_pairs={{0,4},{1,3},{2,6},{3,1},{4,0},{5,7},{6,2},{7,5},{8,12},{9,11},{10,... | collective-permute-start | bytes 786440 | tf_op jit(solution)/shard_map/ppermute | solution.py:559
  233.1 9.8 %collective-permute-start.35 = (bf16[256,128]{1,0:T(8,128)(2,1)S(1)}, bf16[256,128]{1,0:T(8,128)(2,1)S(1)}, u32[]{:S(2)}, u32[]{:S(2)}) collective-permute-start(bf16[256,128]{1,0:T(8,128)(2,1)S(1)} %get-tuple-element.400), channel_id=1, source_target_pairs={{0,16},{1,17},{2,18},{3,19},{4,20},{5,21},{6,22},{7,23},{8,24},{9,... | collective-permute-start | bytes 196616 | tf_op jit(solution)/shard_map/ppermute | solution.py:559
  241.7 10.6 %collective-permute-start.39 = (bf16[2048,128]{1,0:T(8,128)(2,1)S(1)}, bf16[2048,128]{1,0:T(8,128)(2,1)S(1)}, u32[]{:S(2)}, u32[]{:S(2)}) collective-permute-start(bf16[2048,128]{1,0:T(8,128)(2,1)S(1)} %constant_dynamic-update-slice_fusion.18), channel_id=1, source_target_pairs={{0,2},{1,5},{2,0},{3,7},{4,6},{5,1},{6,4},{7,3},{8,10},{9,13},{10,... | collective-permute-start | bytes 1572872 | tf_op jit(solution)/shard_map/ppermute | solution.py:559
  242.9 9.5 %collective-permute-start.38 = (bf16[256,128]{1,0:T(8,128)(2,1)S(1)}, bf16[256,128]{1,0:T(8,128)(2,1)S(1)}, u32[]{:S(2)}, u32[]{:S(2)}) collective-permute-start(bf16[256,128]{1,0:T(8,128)(2,1)S(1)} %add_convert_fusion.19), channel_id=1, source_target_pairs={{0,16},{1,17},{2,18},{3,19},{4,20},{5,21},{6,22},{7,23},{8,24},{9,... | collective-permute-start | bytes 196616 | tf_op jit(solution)/shard_map/ppermute | solution.py:559
  252.4 5.0 %collective-permute-start.41 = (bf16[512,128]{1,0:T(8,128)(2,1)S(1)}, bf16[512,128]{1,0:T(8,128)(2,1)S(1)}, u32[]{:S(2)}, u32[]{:S(2)}) collective-permute-start(bf16[512,128]{1,0:T(8,128)(2,1)S(1)} %constant_dynamic-update-slice_fusion.24), channel_id=1, source_target_pairs={{0,8},{1,9},{2,10},{3,11},{4,12},{5,13},{6,14},{7,15},{8,0},{9,1},... | collective-permute-start | bytes 393224 | tf_op jit(solution)/shard_map/ppermute | solution.py:559
  257.5 8.1 %collective-permute-start.42 = (bf16[1024,128]{1,0:T(8,128)(2,1)S(1)}, bf16[1024,128]{1,0:T(8,128)(2,1)S(1)}, u32[]{:S(2)}, u32[]{:S(2)}) collective-permute-start(bf16[1024,128]{1,0:T(8,128)(2,1)S(1)} %constant_dynamic-update-slice_fusion.26), channel_id=1, source_target_pairs={{0,4},{1,3},{2,6},{3,1},{4,0},{5,7},{6,2},{7,5},{8,12},{9,11},{10,... | collective-permute-start | bytes 786440 | tf_op jit(solution)/shard_map/ppermute | solution.py:559
  259.1 16.0 %collective-permute-start.47 = (bf16[8448,128]{1,0:T(8,128)(2,1)S(1)}, bf16[8448,128]{1,0:T(8,128)(2,1)S(1)}, u32[]{:S(2)}, u32[]{:S(2)}) collective-permute-start(bf16[8448,128]{1,0:T(8,128)(2,1)S(1)} %constant_dynamic-update-slice_fusion.6.mine_ref), channel_id=1, source_target_pairs={{0,1},{1,0},{2,3},{3,2},{4,5},{5,4},{6,7},{7,6},{8,9},{9,8},{10,11... | collective-permute-start | bytes 6488072 | tf_op jit(solution)/shard_map/ppermute | solution.py:559
  259.1 20.4 %collective-permute-start.46 = (bf16[8448,128]{1,0:T(8,128)(2,1)S(1)}, bf16[8448,128]{1,0:T(8,128)(2,1)S(1)}, u32[]{:S(2)}, u32[]{:S(2)}) collective-permute-start(bf16[8448,128]{1,0:T(8,128)(2,1)S(1)} %constant_dynamic-update-slice_fusion.20.mine_ref), channel_id=1, source_target_pairs={{0,1},{1,0},{2,3},{3,2},{4,5},{5,4},{6,7},{7,6},{8,9},{9,8},{10,11... | collective-permute-start | bytes 6488072 | tf_op jit(solution)/shard_map/ppermute | solution.py:559
  265.6 9.2 %collective-permute-start.43 = (bf16[2048,128]{1,0:T(8,128)(2,1)S(1)}, bf16[2048,128]{1,0:T(8,128)(2,1)S(1)}, u32[]{:S(2)}, u32[]{:S(2)}) collective-permute-start(bf16[2048,128]{1,0:T(8,128)(2,1)S(1)} %constant_dynamic-update-slice_fusion.28), channel_id=1, source_target_pairs={{0,2},{1,5},{2,0},{3,7},{4,6},{5,1},{6,4},{7,3},{8,10},{9,13},{10,... | collective-permute-start | bytes 1572872 | tf_op jit(solution)/shard_map/ppermute | solution.py:559
  267.4 16.5 %collective-permute-start.45 = (bf16[4096,128]{1,0:T(8,128)(2,1)S(1)}, bf16[4096,128]{1,0:T(8,128)(2,1)S(1)}, u32[]{:S(2)}, u32[]{:S(2)}) collective-permute-start(bf16[4096,128]{1,0:T(8,128)(2,1)S(1)} %constant_dynamic-update-slice_fusion.22.mine_ref), channel_id=1, source_target_pairs={{0,1},{1,0},{2,3},{3,2},{4,5},{5,4},{6,7},{7,6},{8,9},{9,8},{10,11... | collective-permute-start | bytes 3145736 | tf_op jit(solution)/shard_map/ppermute | solution.py:559
  275.0 11.6 %collective-permute-start.44 = (bf16[4096,128]{1,0:T(8,128)(2,1)S(1)}, bf16[4096,128]{1,0:T(8,128)(2,1)S(1)}, u32[]{:S(2)}, u32[]{:S(2)}) collective-permute-start(bf16[4096,128]{1,0:T(8,128)(2,1)S(1)} %constant_dynamic-update-slice_fusion.30.mine_ref), channel_id=1, source_target_pairs={{0,1},{1,0},{2,3},{3,2},{4,5},{5,4},{6,7},{7,6},{8,9},{9,8},{10,11... | collective-permute-start | bytes 3145736 | tf_op jit(solution)/shard_map/ppermute | solution.py:559
  (2 other events, 1.4 us)
